TPU v7x, 512 devices: a whole 4x8x8 slice. The times are simulated.
512 devices in a mesh: ka: 128 (over x_lo, z, y), ga: 4 (over x_hi, core).
Axes of the slice: x: 4 (x_hi: 2, x_lo: 2; x = x_hi * 2 + x_lo), y: 8, z: 8, core: 2. Of those that a mesh axis runs over, the one named last changes fastest.
Arguments:
- cond_pairs: bfloat16 [4, 768, 2, 16, 1024], P(None, 'ka', None, None, 'ga'), may hold values from -1 to 1
- val_pairs: bfloat16 [4, 768, 2, 16, 1024], P(None, 'ka', None, None, 'ga'), may hold values from -1 to 1
- screened: bfloat16 [4, 2, 1024, 1024], P(None, None, 'ka', 'ga'), may hold values from -1 to 4, as said below
- k_plus: int32 [4, 768], replicated, may hold values from 0 to 767, as said below
Outputs:
- kernel_forward: float32 [4, 768, 2, 256], P(None, 'ka', None, 'ga')
- kernel_back: float32 [4, 768, 2, 256], P(None, 'ka', None, 'ga')
Inputs may be any that keep to these rules, and one draw needn't show every extreme that they name: screened[q, 0] is symmetric and screened[q, 1] antisymmetric in the last two dimensions, so W(q) is Hermitian. For each q there is one translation (dx, dy) of the periodic 64 x 12 grid, with k = x * 12 + y, such that k_plus[q, k] = ((x + dx) mod 64) * 12 + (y + dy) mod 12.
All inputs are finite; a program needn't handle non-finite values.
Results may differ from a plain program's by a relative error of at most 0.0029.
Values may be sent and summed in bfloat16 or wider, within the bound.
No kernel may reach another device: no remote copies, remote signals or barrier semaphores. Data moves between devices by JAX's collectives and lax.ppermute only.
A program may use at most 64 MiB of HBM per device.

v0:
```python
import jax
import jax.numpy as jnp
from jax import lax
from jax.sharding import PartitionSpec as P

NG = 1024
Q = 4
CPAIR = 16
VPAIR = 16


def passed_along(block, axis, distance):
    devices = range(lax.axis_size(axis))
    route = [((i - distance) % len(devices), i) for i in devices]
    return lax.ppermute(block, axis, route)


def swapped(shard, axis, bit):
    return lax.ppermute(shard, axis, [(i, i ^ 1 << bit) for i in range(lax.axis_size(axis))])


def screen_fold(left_real, left_imag, piece):
    real_next = jnp.dot(left_real, piece[0], preferred_element_type=jnp.float32) + jnp.dot(
        left_imag, piece[1], preferred_element_type=jnp.float32
    )
    imag_next = jnp.dot(left_real, piece[1], preferred_element_type=jnp.float32) - jnp.dot(
        left_imag, piece[0], preferred_element_type=jnp.float32
    )
    return (real_next, imag_next)


def pair_contract(left, right):
    return jnp.einsum("kag,kbg->kab", left, right, preferred_element_type=jnp.float32)


def local(cond_pairs, val_pairs, screened, k_plus):
    local_k = cond_pairs.shape[1]
    columns = screened.shape[3]
    grid_y = 2 * local_k
    forward = []
    for q_index in range(Q):
        cond_full = lax.all_gather(cond_pairs[q_index], "ga", axis=3, tiled=True)
        left_real = cond_full[:, 0].reshape(local_k * CPAIR, NG)
        left_imag = cond_full[:, 1].reshape(local_k * CPAIR, NG)
        real_x, imag_x = screen_fold(
            left_real, left_imag, lax.all_gather(screened[q_index], "ka", axis=1, tiled=True)
        )
        real_b = real_x.astype(jnp.bfloat16).reshape(local_k, CPAIR, columns)
        imag_b = imag_x.astype(jnp.bfloat16).reshape(local_k, CPAIR, columns)
        val_real = val_pairs[q_index][:, 0]
        val_imag = val_pairs[q_index][:, 1]
        kernel_real = pair_contract(real_b, val_real) - pair_contract(imag_b, val_imag)
        kernel_imag = pair_contract(real_b, val_imag) + pair_contract(imag_b, val_real)
        forward.append(jnp.stack([kernel_real, kernel_imag], 1).reshape(local_k, 2, CPAIR * VPAIR))
    partial_value = jnp.stack(forward, 0)
    total = lax.psum(partial_value, "ga")
    width = total.shape[3] // lax.axis_size("ga")
    kernel_share = lax.dynamic_slice_in_dim(total, lax.axis_index("ga") * width, width, 3)
    count = lax.axis_size("ka")
    corner = k_plus[:, 0]
    row_step = corner // grid_y
    col_step = corner % grid_y
    hop_length = 2 * row_step % count
    moved = kernel_share
    nbits = count.bit_length() - 1
    for bit_number in range(1, nbits):
        arrived = passed_along(moved, "ka", 1 << bit_number)
        taken = hop_length // (1 << bit_number) % 2 == 1
        moved = jnp.where(taken[:, None, None, None], arrived, moved)
    partner = swapped(moved, "ka", 0)
    half_index = lax.axis_index("ka") % 2
    whole_row = jnp.where(
        half_index == 0, jnp.concatenate([moved, partner], 1), jnp.concatenate([partner, moved], 1)
    )
    doubled = jnp.concatenate([whole_row, whole_row], 1)
    backs = []
    for q_index in range(Q):
        begin = (half_index * local_k - col_step[q_index] + grid_y) % grid_y
        backs.append(lax.dynamic_slice_in_dim(doubled[q_index], begin, local_k, 0))
    kernel_back = jnp.stack(backs, 0)
    return (kernel_share, kernel_back)


def solution(mesh):
    in_specs = (
        P(None, "ka", None, None, "ga"),
        P(None, "ka", None, None, "ga"),
        P(None, None, "ka", "ga"),
        P(),
    )
    out_specs = (P(None, "ka", None, "ga"), P(None, "ka", None, "ga"))
    return jax.shard_map(local, mesh=mesh, in_specs=in_specs, out_specs=out_specs, check_vma=False)
```

profile of v0, /device:TPU:8, one launch (start us, length us, event | category | flops | bytes accessed | tf_op | source)
XLA Modules:
  0.0 1886.7 jit_solution(3142191809410031896)
XLA Ops:
  7.2 1.4 fusion.45
  13.4 8.0 all-gather.6
  22.4 8.1 all-gather.4
  30.5 8.1 all-gather.2
  38.7 8.1 all-gather
  46.8 412.7 %all-gather.19.cloned.1.call-done = bf16[1,2,1024,256]{3,2,1,0:T(8,128)(2,1)} async-done(((bf16[1,2,8,256]{3,2,1,0:T(8,128)(2,1)}), bf16[1,2,1024,256]{3,2,1,0:T(8,128)(2,1)}) %all-gather.19.cloned.1.call-update) | async-done | bytes 1048592 | tf_op jit(solution)/shard_map/all_gather | solution.py:46
  463.6 438.4 %all-gather.17.cloned.1.call-done = bf16[1,2,1024,256]{3,2,1,0:T(8,128)(2,1)} async-done(((bf16[1,2,8,256]{3,2,1,0:T(8,128)(2,1)}), bf16[1,2,1024,256]{3,2,1,0:T(8,128)(2,1)}) %all-gather.17.cloned.1.call-update) | async-done | bytes 1048592 | tf_op jit(solution)/shard_map/all_gather | solution.py:46
  906.0 438.8 %all-gather.15.cloned.1.call-done = bf16[1,2,1024,256]{3,2,1,0:T(8,128)(2,1)} async-done(((bf16[1,2,8,256]{3,2,1,0:T(8,128)(2,1)}), bf16[1,2,1024,256]{3,2,1,0:T(8,128)(2,1)}) %all-gather.15.cloned.1.call-update) | async-done | bytes 1048592 | tf_op jit(solution)/shard_map/all_gather | solution.py:46
  1346.0 1.3 fusion.2
  1348.8 438.5 %all-gather.13.cloned.1.call-done = bf16[1,2,1024,256]{3,2,1,0:T(8,128)(2,1)} async-done(((bf16[1,2,8,256]{3,2,1,0:T(8,128)(2,1)}), bf16[1,2,1024,256]{3,2,1,0:T(8,128)(2,1)}) %all-gather.13.cloned.1.call-update) | async-done | bytes 1048592 | tf_op jit(solution)/shard_map/all_gather | solution.py:46
  1800.8 13.7 psum.7
  1814.6 2.7 collective-permute-start
  1817.3 8.2 collective-permute-done
  1825.6 1.9 collective-permute-start.1
  1827.6 10.8 collective-permute-done.1
  1838.4 1.9 collective-permute-start.2
  1840.4 6.0 collective-permute-done.2
  1846.4 1.9 collective-permute-start.3
  1848.3 6.9 collective-permute-done.3
  1855.3 1.9 collective-permute-start.4
  1857.2 8.7 collective-permute-done.4
  1866.0 2.4 collective-permute-start.5
  1868.4 3.4 collective-permute-done.5
  1871.9 3.6 collective-permute-start.6
  (127 shorter events, 32.5 us)
Async XLA Ops:
  7.2 452.4 %all-gather.19.cloned.1.call-start = ((), (), s32[]{:S(2)}) async-start(), calls=%async_computation.3 | async-start | bytes 1056768 | tf_op jit(solution)/shard_map/all_gather | solution.py:46
  8.6 893.4 %all-gather.17.cloned.1.call-start = ((), (), s32[]{:S(2)}) async-start(), calls=%async_computation.2 | async-start | bytes 1056768 | tf_op jit(solution)/shard_map/all_gather | solution.py:46
  9.3 1335.4 %all-gather.15.cloned.1.call-start = ((), (), s32[]{:S(2)}) async-start(), calls=%async_computation.1 | async-start | bytes 1056768 | tf_op jit(solution)/shard_map/all_gather | solution.py:46
  10.1 1777.2 %all-gather.13.cloned.1.call-start = ((), (), s32[]{:S(2)}) async-start(), calls=%async_computation | async-start | bytes 1056768 | tf_op jit(solution)/shard_map/all_gather | solution.py:46
  21.4 1.0 copy-start.15
  22.4 437.2 %copy-start.4 = (bf16[6,1,16,1024]{3,2,1,0:T(8,128)(2,1)}, bf16[6,1,16,1024]{3,2,1,0:T(8,128)(2,1)S(1)}, u32[]{:S(2)}) copy-start(bf16[6,1,16,1024]{3,2,1,0:T(8,128)(2,1)S(1)} %get-tuple-element.23) | copy-start | bytes 589828
  22.4 440.4 %copy-start.12 = (bf16[1,6,2,16,256]{4,3,1,2,0:T(8,128)(2,1)}, bf16[1,6,2,16,256]{4,3,1,2,0:T(8,128)(2,1)S(1)}, u32[]{:S(2)}) copy-start(bf16[1,6,2,16,256]{4,3,1,2,0:T(8,128)(2,1)S(1)} %copy.32) | copy-start | bytes 294916
  30.5 874.7 %copy-start.10 = (bf16[1,6,2,16,256]{4,3,1,2,0:T(8,128)(2,1)}, bf16[1,6,2,16,256]{4,3,1,2,0:T(8,128)(2,1)S(1)}, u32[]{:S(2)}) copy-start(bf16[1,6,2,16,256]{4,3,1,2,0:T(8,128)(2,1)S(1)} %copy.33) | copy-start | bytes 294916
  38.7 1309.4 %copy-start.8 = (bf16[1,6,2,16,256]{4,3,1,2,0:T(8,128)(2,1)}, bf16[1,6,2,16,256]{4,3,1,2,0:T(8,128)(2,1)S(1)}, u32[]{:S(2)}) copy-start(bf16[1,6,2,16,256]{4,3,1,2,0:T(8,128)(2,1)S(1)} %copy.34) | copy-start | bytes 294916
  46.8 1743.8 %copy-start.6 = (bf16[1,6,2,16,256]{4,3,1,2,0:T(8,128)(2,1)}, bf16[1,6,2,16,256]{4,3,1,2,0:T(8,128)(2,1)S(1)}, u32[]{:S(2)}) copy-start(bf16[1,6,2,16,256]{4,3,1,2,0:T(8,128)(2,1)S(1)} %copy.35) | copy-start | bytes 294916
  1348.0 443.3 %copy-start.3 = (bf16[1,2,1024,256]{3,2,1,0:T(8,128)(2,1)S(1)}, bf16[1,2,1024,256]{3,2,1,0:T(8,128)(2,1)}, u32[]{:S(2)}) copy-start(bf16[1,2,1024,256]{3,2,1,0:T(8,128)(2,1)} %all-gather.19.cloned.1.call-done) | copy-start | bytes 3145732
  1789.9 1.5 copy-start.5
  1791.4 2.4 copy-start.2
  1791.6 1.0 copy-start.13
  1793.7 2.4 copy-start.1
  1796.1 2.4 copy-start
  1796.4 1.0 copy-start.9
  1814.6 11.0 collective-permute-start
  1825.6 12.7 collective-permute-start.1
  1838.4 7.9 collective-permute-start.2
  1846.4 8.8 collective-permute-start.3
  1855.3 10.6 collective-permute-start.4
  1866.0 5.8 collective-permute-start.5
  1871.9 7.5 collective-permute-start.6
  (11 other events, 9.8 us)
Sparse Core Ops, SparseCore 0:
  10.0 449.5 all-gather.18
  461.6 440.3 all-gather.16
  904.5 440.1 all-gather.14
  1347.2 440.0 all-gather.12
where the time goes:
time: 1890 us
  waiting for transfers between devices  1770 us (94%)
  blocking collectives  45.9 us (2%)
    all_gather x4, waiting for transfers between devices, local(): lax.all_gather(screened[q_index], 'ka', axis=1, tiled=True)  1730 us
    ppermute x6, waiting for transfers between devices, passed_along(): return lax.ppermute(block, axis, route)  43.9 us
  transfers between devices with their start and end apart: 11, of which 10 were waited for; matrix products, arithmetic and copies ran while one was open for 1% of the time, Pallas kernels for 0%

commit v1 on v0

v1 whole, which is shorter than its diff:
```python
import functools

import jax
import jax.numpy as jnp
from jax import lax
from jax.experimental import pallas as pl
from jax.experimental.pallas import tpu as pltpu
from jax.sharding import Mesh
from jax.sharding import PartitionSpec as P

NG = 1024
Q = 4
PAIR = 16
BLK = 128
NB = NG // BLK
SENT = 5
KQ = 6
BF = jnp.bfloat16
F32 = jnp.float32


def nt(left, right, precision=None):
    return lax.dot_general(
        left, right, (((1,), (1,)), ((), ())), preferred_element_type=F32, precision=precision
    )


def nn(left, right, precision=None):
    return jnp.dot(left, right, preferred_element_type=F32, precision=precision)


def contract(sign_ref, left_ref, val_ref, own_ref, oth_ref, out_ref, p_ref, q_ref):
    sign = sign_ref[0].astype(BF)
    left = left_ref[...]
    flipped = left * sign
    rows = left.shape[0]
    wrapped = jnp.concatenate([left, left[:, : 3 * BLK]], 1)
    wrapped_flip = jnp.concatenate([flipped, flipped[:, : 3 * BLK]], 1)
    for b in range(NB):
        lo, hi = b * BLK, (b + 1) * BLK
        far = wrapped[:, hi : hi + 3 * BLK]
        far_flip = wrapped_flip[:, hi : hi + 3 * BLK]
        own = own_ref[lo:hi, :]
        oth = oth_ref[lo:hi, :]
        p_back = nt(far_flip, own[:, BLK : 4 * BLK])
        q_back = -nt(far, oth[:, BLK : 4 * BLK])
        if b == 0:
            p_ref[...] = jnp.zeros_like(p_ref)
            q_ref[...] = jnp.zeros_like(q_ref)
        p_ref[:, lo:hi] += p_back
        q_ref[:, lo:hi] += q_back
        p_fore = nn(left[:, lo:hi], own)
        q_fore = nn(flipped[:, lo:hi], oth)
        first = min(SENT, NB - b)
        p_ref[:, lo : lo + first * BLK] += p_fore[:, : first * BLK]
        q_ref[:, lo : lo + first * BLK] += q_fore[:, : first * BLK]
        if first < SENT:
            p_ref[:, : (SENT - first) * BLK] += p_fore[:, first * BLK :]
            q_ref[:, : (SENT - first) * BLK] += q_fore[:, first * BLK :]
    p = p_ref[...].reshape(KQ, 2, PAIR, NG)
    q = q_ref[...].reshape(KQ, 2, PAIR, NG)
    half = rows // 2
    x_real = (p[:, 0] + q[:, 1]).reshape(half, NG).astype(BF)
    x_imag = (q[:, 0] - p[:, 1]).reshape(half, NG).astype(BF)
    val = val_ref[...]
    g1 = nt(x_real, val)
    g2 = nt(x_imag, val)
    r = lax.broadcasted_iota(jnp.int32, (half, rows), 0)
    c = lax.broadcasted_iota(jnp.int32, (half, rows), 1)
    same = r // PAIR == c // (2 * PAIR)
    g1 = jnp.where(same, g1, 0.0)
    g2 = jnp.where(same, g2, 0.0)
    c = lax.broadcasted_iota(jnp.int32, (rows, 128), 0)
    l = lax.broadcasted_iota(jnp.int32, (rows, 128), 1)
    hit = c % PAIR == l % PAIR
    part = (c // PAIR) % 2
    want = l // 64
    e1 = jnp.where(hit & (part == want), 1.0, 0.0)
    e2 = jnp.where(hit & (part != want), jnp.where(want == 0, -1.0, 1.0), 0.0)
    t = nn(g1, e1, lax.Precision.HIGHEST) + nn(g2, e2, lax.Precision.HIGHEST)
    r = lax.broadcasted_iota(jnp.int32, (half, 128), 0)
    l = lax.broadcasted_iota(jnp.int32, (half, 128), 1)
    t = jnp.where(r % 4 == (l // PAIR) % 4, t, 0.0)
    o = lax.broadcasted_iota(jnp.int32, (4 * KQ, half), 0)
    r = lax.broadcasted_iota(jnp.int32, (4 * KQ, half), 1)
    e3 = jnp.where((r // PAIR == o % KQ) & ((r % PAIR) // 4 == o // KQ), 1.0, 0.0)
    out_ref[...] = nn(e3, t, lax.Precision.HIGHEST)


def contracted(sign, left, val, own, oth):
    vm = pl.BlockSpec(memory_space=pltpu.VMEM)
    return pl.pallas_call(
        contract,
        out_shape=jax.ShapeDtypeStruct((4 * KQ, 128), F32),
        in_specs=[pl.BlockSpec(memory_space=pltpu.SMEM), vm, vm, vm, vm],
        out_specs=vm,
        scratch_shapes=[
            pltpu.VMEM((2 * KQ * PAIR, NG), F32),
            pltpu.VMEM((2 * KQ * PAIR, NG), F32),
        ],
        cost_estimate=pl.CostEstimate(
            flops=1_600_000_000, bytes_accessed=4_000_000, transcendentals=0
        ),
    )(sign, left, val, own, oth)


def pick_rows(at_ref, got_ref, fwd_ref, pay_ref):
    xl = at_ref[0]
    yl = at_ref[1]
    for q in range(Q):
        base = (q // 2) * 8 + (q % 2) * 2
        other = at_ref[2 + q]
        begin = at_ref[6 + q]
        for t in range(KQ):
            fwd_ref[q, pl.ds(t, 1), :] = got_ref[base + yl * 4 + t // 3, pl.ds(xl * 3 + t % 3, 1), :]
            col = lax.rem(begin + t, 12)
            slot = base + (col // 6) * 4 + (col % 6) // 3
            pay_ref[pl.ds(q * KQ + t, 1), :] = got_ref[slot, pl.ds(other * 3 + col % 3, 1), :]


def pick_back(at_ref, got_ref, out_ref):
    for q in range(Q):
        out_ref[q, :, :] = got_ref[at_ref[q], q * KQ : (q + 1) * KQ, :]


def local(cond, val, screened, k_plus):
    xl, yl, core = lax.axis_index("xl"), lax.axis_index("yl"), lax.axis_index("c")
    z, yh = lax.axis_index("z"), lax.axis_index("yh")
    row8 = ("xl", "xh", "c")
    w = lax.all_to_all(screened.reshape(8, 8, 256), row8, 0, 0)
    w = jnp.transpose(w.reshape(2, 4, 8, 256), (0, 2, 1, 3)).reshape(2, 8, NG)
    w = jnp.concatenate([w, w[:, :, : 4 * BLK]], 2)
    cut = [
        lax.dynamic_slice_in_dim(w[i], (4 * i + z // 2) * BLK, SENT * BLK, 1) for i in range(2)
    ]
    w = jnp.stack(cut, 0)
    w = lax.all_to_all(jnp.broadcast_to(w, (64,) + w.shape), ("z", "yh", "yl"), 0, 0)
    own = jnp.transpose(w, (1, 0, 2, 3)).reshape(NG, SENT * BLK)
    oth = lax.ppermute(own, "c", [(0, 1), (1, 0)])

    def spread(pairs):
        got = lax.all_to_all(pairs.reshape(8, 3, 2, PAIR, 256), row8, 0, 0)
        return jnp.transpose(got.reshape(2, 4, 3, 2, PAIR, 256), (0, 2, 3, 4, 1, 5)).reshape(
            KQ, 2, PAIR, NG
        )

    left = spread(cond)
    left = jnp.where(core == 0, left, jnp.stack([left[:, 1], -left[:, 0]], 1))
    right = spread(val)
    sign = jnp.where(core == 0, 1.0, -1.0).astype(F32).reshape(1)
    block = contracted(
        sign, left.reshape(2 * KQ * PAIR, NG), right.reshape(2 * KQ * PAIR, NG), own, oth
    )
    slots = jnp.broadcast_to(block.reshape(1, 1, 4, KQ, 128), (2, 2, 4, KQ, 128))
    got = lax.all_to_all(slots.reshape(16, KQ, 128), ("xl", "yl", "xh", "c"), 0, 0)
    corner = k_plus[:, 0]
    row_step, col_step = corner // 12, corner % 12
    here = z * 4 + yh
    other = xl ^ ((here + row_step) // 32 % 2)
    begin = (6 * yl - col_step + 12) % 12
    at = jnp.concatenate([jnp.stack([xl, yl]), other, begin]).astype(jnp.int32)
    vm = pl.BlockSpec(memory_space=pltpu.VMEM)
    sm = pl.BlockSpec(memory_space=pltpu.SMEM)
    forward, pay = pl.pallas_call(
        pick_rows,
        out_shape=(
            jax.ShapeDtypeStruct((Q, KQ, 128), F32),
            jax.ShapeDtypeStruct((Q * KQ, 128), F32),
        ),
        in_specs=[sm, vm],
        out_specs=(vm, vm),
    )(at, got)
    came = lax.all_to_all(jnp.broadcast_to(pay, (32,) + pay.shape), ("z", "yh"), 0, 0)
    source = ((here - row_step) % 32).astype(jnp.int32)
    back = pl.pallas_call(
        pick_back,
        out_shape=jax.ShapeDtypeStruct((Q, KQ, 128), F32),
        in_specs=[sm, vm],
        out_specs=vm,
    )(source, came)
    return forward.reshape(Q, KQ, 2, 64), back.reshape(Q, KQ, 2, 64)


def solution(mesh):
    fine = Mesh(mesh.devices.reshape(2, 8, 4, 2, 2, 2), ("xl", "z", "yh", "yl", "xh", "c"))
    ka, ga = ("xl", "z", "yh", "yl"), ("xh", "c")
    in_specs = (
        P(None, ka, None, None, ga),
        P(None, ka, None, None, ga),
        P(None, None, ka, ga),
        P(),
    )
    out_specs = (P(None, ka, None, ga), P(None, ka, None, ga))
    return jax.shard_map(local, mesh=fine, in_specs=in_specs, out_specs=out_specs, check_vma=False)
```

time: 1890 us -> 137 us (0.07)
  the two profiles are of different devices: /device:TPU:8 before, /device:TPU:16 now
where the time goes in v1:
time: 137 us; the launch traced here: 136 us
  blocking collectives  50.8 us (37%)
  waiting for transfers between devices  38.6 us (28%)
  starting transfers between devices  24.4 us (18%)
  local copies, waits for them, and re-layouts  8.98 us (7%)
  Pallas kernels  8.91 us (7%)
  other arithmetic  3.77 us (3%)
    all_to_all x1, blocking collectives, local(): lax.all_to_all(jnp.broadcast_to(w, (64,) + w.shape), ('z', 'yh', 'yl'), 0...  50.8 us
    all_to_all x1, waiting for transfers between devices, local(): lax.all_to_all(jnp.broadcast_to(pay, (32,) + pay.shape), ('z', 'yh'), 0, 0)  15.5 us
    all_to_all x2, waiting for transfers between devices, spread(): got = lax.all_to_all(pairs.reshape(8, 3, 2, PAIR, 256), row8, 0, 0)  12.2 us
    all_to_all x1, starting transfers between devices, local(): lax.all_to_all(jnp.broadcast_to(pay, (32,) + pay.shape), ('z', 'yh'), 0, 0)  6.95 us
    all_to_all x2, starting transfers between devices, spread(): got = lax.all_to_all(pairs.reshape(8, 3, 2, PAIR, 256), row8, 0, 0)  6.91 us
    all_to_all x1, waiting for transfers between devices, local(): lax.all_to_all(slots.reshape(16, KQ, 128), ('xl', 'yl', 'xh', 'c'), 0, 0)  5.55 us
    all_to_all x1, waiting for transfers between devices, local(): w = lax.all_to_all(screened.reshape(8, 8, 256), row8, 0, 0)  5.36 us
    pallas_call x1, Pallas kernels, contracted(): pl.pallas_call(contract, out_shape=jax.ShapeDtypeStruct((4 * KQ, 128), F3...  5.35 us
  transfers between devices with their start and end apart: 6, of which 5 were waited for; matrix products, arithmetic and copies ran while one was open for 5% of the time, Pallas kernels for 0%

profile of v1, /device:TPU:16, one launch (start us, length us, event | category | flops | bytes accessed | tf_op | source)
XLA Modules:
  0.0 136.2 jit_solution(2360263712936196567)
XLA Ops:
  0.6 4.3 %all-to-all-start.2 = ((bf16[8,8,256]{2,1,0:T(8,128)(2,1)}), bf16[8,8,256]{2,1,0:T(8,128)(2,1)S(1)}, u32[]{:S(2)}, u32[]{:S(2)}) async-start(bf16[8,8,256]{2,1,0:T(8,128)(2,1)} %bitcast.40), calls=%async_computation.2 | async-start | bytes 65536 | tf_op jit(solution)/shard_map/all_to_all | solution.py:130
  4.9 5.4 %all-to-all-done.2 = bf16[8,8,256]{2,1,0:T(8,128)(2,1)S(1)} async-done(((bf16[8,8,256]{2,1,0:T(8,128)(2,1)}), bf16[8,8,256]{2,1,0:T(8,128)(2,1)S(1)}, u32[]{:S(2)}, u32[]{:S(2)}) %all-to-all-start.2) | async-done | bytes 32800 | tf_op jit(solution)/shard_map/all_to_all | solution.py:130
  10.5 50.8 %all_to_all.30 = bf16[64,2,8,640]{3,2,1,0:T(8,128)(2,1)S(1)} all-to-all(bf16[64,2,8,640]{3,2,1,0:T(8,128)(2,1)S(1)} %broadcast_in_dim.13), channel_id=1, replica_groups=mesh['xl'=2,'z'=8,'yh'=4,'yl'=2,'xh'=2,'c'=2] {'z','yh','yl'}, dimensions={0} | all-to-all | bytes 2621440 | tf_op jit(solution)/shard_map/all_to_all | solution.py:137
  61.3 3.5 %all-to-all-start = ((bf16[8,3,2,16,256]{4,3,2,1,0:T(8,128)(2,1)}), bf16[8,3,2,16,256]{4,3,2,1,0:T(8,128)(2,1)S(1)}, u32[]{:S(2)}, u32[]{:S(2)}) async-start(bf16[8,3,2,16,256]{4,3,2,1,0:T(8,128)(2,1)} %bitcast.3), calls=%async_computation | async-start | bytes 786432 | tf_op jit(solution)/shard_map/all_to_all | solution.py:142
  64.9 2.3 %collective-permute-start = (bf16[1024,640]{1,0:T(8,128)(2,1)S(1)}, bf16[1024,640]{1,0:T(8,128)(2,1)}, u32[]{:S(2)}, u32[]{:S(2)}) collective-permute-start(bf16[1024,640]{1,0:T(8,128)(2,1)S(1)} %bitcast.34), channel_id=1, source_target_pairs={{0,1},{1,0},{2,3},{3,2},{4,5},{5,4},{6,7},{7,6},{8,9},{9,8},{10,11... | collective-permute-start | bytes 3932168 | tf_op jit(solution)/shard_map/ppermute | solution.py:139
  67.2 6.1 %all-to-all-done = bf16[8,3,2,16,256]{4,3,2,1,0:T(8,128)(2,1)S(1)} async-done(((bf16[8,3,2,16,256]{4,3,2,1,0:T(8,128)(2,1)}), bf16[8,3,2,16,256]{4,3,2,1,0:T(8,128)(2,1)S(1)}, u32[]{:S(2)}, u32[]{:S(2)}) %all-to-all-start) | async-done | bytes 393248 | tf_op jit(solution)/shard_map/all_to_all | solution.py:142
  73.3 3.5 %all-to-all-start.1 = ((bf16[8,3,2,16,256]{4,3,2,1,0:T(8,128)(2,1)}), bf16[8,3,2,16,256]{4,3,2,1,0:T(8,128)(2,1)S(1)}, u32[]{:S(2)}, u32[]{:S(2)}) async-start(bf16[8,3,2,16,256]{4,3,2,1,0:T(8,128)(2,1)} %bitcast.7), calls=%async_computation.1 | async-start | bytes 786432 | tf_op jit(solution)/shard_map/all_to_all | solution.py:142
  76.8 0.8 fusion.1
  77.6 0.8 divide_reduce_fusion
  79.3 6.1 %all-to-all-done.1 = bf16[8,3,2,16,256]{4,3,2,1,0:T(8,128)(2,1)S(1)} async-done(((bf16[8,3,2,16,256]{4,3,2,1,0:T(8,128)(2,1)}), bf16[8,3,2,16,256]{4,3,2,1,0:T(8,128)(2,1)S(1)}, u32[]{:S(2)}, u32[]{:S(2)}) %all-to-all-start.1) | async-done | bytes 393248 | tf_op jit(solution)/shard_map/all_to_all | solution.py:142
  85.7 0.8 copy.30
  86.9 0.8 bitcast_select_fusion.left_ref
  87.7 5.4 %shard_map.59 = f32[24,128]{1,0:T(8,128)} custom-call(f32[1]{0:T(128)} %bitcast.2.sign_ref, bf16[192,1024]{1,0:T(8,128)(2,1)} %bitcast_select_fusion.left_ref, bf16[192,1024]{1,0:T(8,128)(2,1)} %bitcast.39, bf16[1024,640]{1,0:T(8,128)(2,1)} %bitcast.35, bf16[1024,640]{1,0:T(8,128)(2,1)} %collective-permute-done.oth_ref), custom_call_target="tpu_custom_call" | custom-call | flops 1600000000 | bytes 4000000 | tf_op jit(solution)/shard_map/pallas_call | solution.py:92
  93.1 0.7 broadcast_in_dim.14
  94.4 3.9 %all-to-all-start.4 = ((f32[16,6,128]{2,1,0:T(8,128)}), f32[16,6,128]{2,1,0:T(8,128)S(1)}, u32[]{:S(2)}, u32[]{:S(2)}) async-start(f32[16,6,128]{2,1,0:T(8,128)} %bitcast.18), calls=%async_computation.4 | async-start | bytes 131072 | tf_op jit(solution)/shard_map/all_to_all | solution.py:155
  99.0 5.6 %all-to-all-done.4.got_ref = f32[16,6,128]{2,1,0:T(8,128)S(1)} async-done(((f32[16,6,128]{2,1,0:T(8,128)}), f32[16,6,128]{2,1,0:T(8,128)S(1)}, u32[]{:S(2)}, u32[]{:S(2)}) %all-to-all-start.4) | async-done | bytes 49184 | tf_op jit(solution)/shard_map/all_to_all | solution.py:155
  105.2 1.9 %shard_map.60 = (f32[4,6,128]{2,1,0:T(8,128)}, f32[24,128]{1,0:T(8,128)}) custom-call(s32[10]{0:T(128)} %pad_add_fusion.at_ref, f32[16,6,128]{2,1,0:T(8,128)} %copy-done.2), custom_call_target="tpu_custom_call" | custom-call | tf_op jit(solution)/shard_map/pallas_call | solution.py:164
  107.1 1.5 %broadcast_in_dim.16 = f32[32,24,128]{2,1,0:T(8,128)} broadcast(f32[24,128]{1,0:T(8,128)} %get-tuple-element.5), dimensions={1,2} | broadcast | bytes 405504 | tf_op jit(solution)/shard_map/broadcast_in_dim | solution.py:173
  108.6 6.9 %all-to-all-start.5 = ((f32[32,24,128]{2,1,0:T(8,128)}), f32[32,24,128]{2,1,0:T(8,128)S(1)}, u32[]{:S(2)}, u32[]{:S(2)}) async-start(f32[32,24,128]{2,1,0:T(8,128)} %broadcast_in_dim.16), calls=%async_computation.5 | async-start | bytes 786432 | tf_op jit(solution)/shard_map/all_to_all | solution.py:173
  115.5 1.4 %reshape.75 = f32[4,6,2,64]{3,2,1,0:T(2,128)} reshape(f32[4,6,128]{2,1,0:T(8,128)} %get-tuple-element.4) | data formatting | bytes 24576 | tf_op jit(solution)/shard_map/reshape | solution.py:181
  117.0 15.5 %all-to-all-done.5.got_ref = f32[32,24,128]{2,1,0:T(8,128)S(1)} async-done(((f32[32,24,128]{2,1,0:T(8,128)}), f32[32,24,128]{2,1,0:T(8,128)S(1)}, u32[]{:S(2)}, u32[]{:S(2)}) %all-to-all-start.5) | async-done | bytes 393248 | tf_op jit(solution)/shard_map/all_to_all | solution.py:173
  132.4 0.7 copy-done
  133.2 1.6 %shard_map.61 = f32[4,6,128]{2,1,0:T(8,128)} custom-call(s32[4]{0:T(128)} %get-tuple-element.16.at_ref, f32[32,24,128]{2,1,0:T(8,128)} %copy-done), custom_call_target="tpu_custom_call" | custom-call | tf_op jit(solution)/shard_map/pallas_call | solution.py:175
  134.8 1.4 %reshape.76 = f32[4,6,2,64]{3,2,1,0:T(2,128)} reshape(f32[4,6,128]{2,1,0:T(8,128)} %shard_map.61) | data formatting | bytes 24576 | tf_op jit(solution)/shard_map/reshape | solution.py:181
  (22 shorter events, 3.7 us)
Async XLA Ops:
  0.6 9.7 %all-to-all-start.2 = ((bf16[8,8,256]{2,1,0:T(8,128)(2,1)}), bf16[8,8,256]{2,1,0:T(8,128)(2,1)S(1)}, u32[]{:S(2)}, u32[]{:S(2)}) async-start(bf16[8,8,256]{2,1,0:T(8,128)(2,1)} %bitcast.40), calls=%async_computation.2 | async-start | bytes 65536 | tf_op jit(solution)/shard_map/all_to_all | solution.py:130
  61.3 12.0 %all-to-all-start = ((bf16[8,3,2,16,256]{4,3,2,1,0:T(8,128)(2,1)}), bf16[8,3,2,16,256]{4,3,2,1,0:T(8,128)(2,1)S(1)}, u32[]{:S(2)}, u32[]{:S(2)}) async-start(bf16[8,3,2,16,256]{4,3,2,1,0:T(8,128)(2,1)} %bitcast.3), calls=%async_computation | async-start | bytes 786432 | tf_op jit(solution)/shard_map/all_to_all | solution.py:142
  64.9 21.6 %copy-start.1 = (bf16[2,64,8,640]{3,2,1,0:T(8,128)(2,1)}, bf16[2,64,8,640]{3,2,1,0:T(8,128)(2,1)S(1)}, u32[]{:S(2)}) copy-start(bf16[2,64,8,640]{3,2,1,0:T(8,128)(2,1)S(1)} %copy.22) | copy-start | bytes 3932164
  64.9 22.8 %collective-permute-start = (bf16[1024,640]{1,0:T(8,128)(2,1)S(1)}, bf16[1024,640]{1,0:T(8,128)(2,1)}, u32[]{:S(2)}, u32[]{:S(2)}) collective-permute-start(bf16[1024,640]{1,0:T(8,128)(2,1)S(1)} %bitcast.34), channel_id=1, source_target_pairs={{0,1},{1,0},{2,3},{3,2},{4,5},{5,4},{6,7},{7,6},{8,9},{9,8},{10,11... | collective-permute-start | bytes 3932168 | tf_op jit(solution)/shard_map/ppermute | solution.py:139
  73.3 12.0 %all-to-all-start.1 = ((bf16[8,3,2,16,256]{4,3,2,1,0:T(8,128)(2,1)}), bf16[8,3,2,16,256]{4,3,2,1,0:T(8,128)(2,1)S(1)}, u32[]{:S(2)}, u32[]{:S(2)}) async-start(bf16[8,3,2,16,256]{4,3,2,1,0:T(8,128)(2,1)} %bitcast.7), calls=%async_computation.1 | async-start | bytes 786432 | tf_op jit(solution)/shard_map/all_to_all | solution.py:142
  94.4 10.1 %all-to-all-start.4 = ((f32[16,6,128]{2,1,0:T(8,128)}), f32[16,6,128]{2,1,0:T(8,128)S(1)}, u32[]{:S(2)}, u32[]{:S(2)}) async-start(f32[16,6,128]{2,1,0:T(8,128)} %bitcast.18), calls=%async_computation.4 | async-start | bytes 131072 | tf_op jit(solution)/shard_map/all_to_all | solution.py:155
  104.5 0.6 copy-start.2
  108.6 23.9 %all-to-all-start.5 = ((f32[32,24,128]{2,1,0:T(8,128)}), f32[32,24,128]{2,1,0:T(8,128)S(1)}, u32[]{:S(2)}, u32[]{:S(2)}) async-start(f32[32,24,128]{2,1,0:T(8,128)} %broadcast_in_dim.16), calls=%async_computation.5 | async-start | bytes 786432 | tf_op jit(solution)/shard_map/all_to_all | solution.py:173
  132.4 0.7 copy-start

commit v2 on v1

--- a/solution.py
+++ b/solution.py
@@ -1,5 +1,3 @@
-import functools
-
 import jax
 import jax.numpy as jnp
 from jax import lax
@@ -29,10 +27,43 @@
     return jnp.dot(left, right, preferred_element_type=F32, precision=precision)
 
 
-def contract(sign_ref, left_ref, val_ref, own_ref, oth_ref, out_ref, p_ref, q_ref):
-    sign = sign_ref[0].astype(BF)
+def assemble(at_ref, *refs):
+    pieces, (left_ref, flip_ref, val_ref) = refs[:8], refs[8:]
+    x, core = at_ref[0], at_ref[1]
+    minus = jnp.where(core == 0, 1.0, -1.0).astype(BF)
+    for s in range(4):
+        xl = (x ^ s) // 2
+        for t in range(2):
+            g = ((x ^ s) % 2) * 2 + (core ^ t)
+            lanes = pl.ds(pl.multiple_of(g * 256, 256), 256)
+            for j in range(3):
+                row = xl * 96 + j * 32
+                whole = pl.ds(pl.multiple_of(row, 32), 32)
+                val_ref[whole, lanes] = pieces[4 + s][t, j].reshape(32, 256)
+                for r in range(2):
+                    part = pl.ds(pl.multiple_of(row + (r ^ core) * PAIR, PAIR), PAIR)
+                    piece = pieces[s][t, j, r]
+                    if r == 0:
+                        piece = piece * minus
+                    left_ref[part, lanes] = piece
+                    flip_ref[part, lanes] = piece * minus
+
+
+def assembled(at, pieces):
+    vm = pl.BlockSpec(memory_space=pltpu.VMEM)
+    flat = jax.ShapeDtypeStruct((2 * KQ * PAIR, NG), BF)
+    return pl.pallas_call(
+        assemble,
+        out_shape=(flat, flat, flat),
+        in_specs=[pl.BlockSpec(memory_space=pltpu.SMEM)] + [vm] * 8,
+        out_specs=(vm, vm, vm),
+        cost_estimate=pl.CostEstimate(flops=0, bytes_accessed=2_000_000, transcendentals=0),
+    )(at, *pieces)
+
+
+def contract(left_ref, flip_ref, val_ref, own_ref, oth_ref, out_ref, p_ref, q_ref):
     left = left_ref[...]
-    flipped = left * sign
+    flipped = flip_ref[...]
     rows = left.shape[0]
     wrapped = jnp.concatenate([left, left[:, : 3 * BLK]], 1)
     wrapped_flip = jnp.concatenate([flipped, flipped[:, : 3 * BLK]], 1)
@@ -81,18 +112,21 @@
     r = lax.broadcasted_iota(jnp.int32, (half, 128), 0)
     l = lax.broadcasted_iota(jnp.int32, (half, 128), 1)
     t = jnp.where(r % 4 == (l // PAIR) % 4, t, 0.0)
-    o = lax.broadcasted_iota(jnp.int32, (4 * KQ, half), 0)
-    r = lax.broadcasted_iota(jnp.int32, (4 * KQ, half), 1)
-    e3 = jnp.where((r // PAIR == o % KQ) & ((r % PAIR) // 4 == o // KQ), 1.0, 0.0)
-    out_ref[...] = nn(e3, t, lax.Precision.HIGHEST)
-
-
-def contracted(sign, left, val, own, oth):
+    o = lax.broadcasted_iota(jnp.int32, (4 * 8, half), 0)
+    r = lax.broadcasted_iota(jnp.int32, (4 * 8, half), 1)
+    e3 = jnp.where((r // PAIR == o % 8) & ((r % PAIR) // 4 == o // 8), 1.0, 0.0)
+    block = nn(e3, t, lax.Precision.HIGHEST)
+    for slot in range(16):
+        g = slot % 4
+        out_ref[slot, :, :] = block[g * 8 : g * 8 + KQ, :]
+
+
+def contracted(left, flipped, val, own, oth):
     vm = pl.BlockSpec(memory_space=pltpu.VMEM)
     return pl.pallas_call(
         contract,
-        out_shape=jax.ShapeDtypeStruct((4 * KQ, 128), F32),
-        in_specs=[pl.BlockSpec(memory_space=pltpu.SMEM), vm, vm, vm, vm],
+        out_shape=jax.ShapeDtypeStruct((16, KQ, 128), F32),
+        in_specs=[vm] * 5,
         out_specs=vm,
         scratch_shapes=[
             pltpu.VMEM((2 * KQ * PAIR, NG), F32),
@@ -101,10 +135,13 @@
         cost_estimate=pl.CostEstimate(
             flops=1_600_000_000, bytes_accessed=4_000_000, transcendentals=0
         ),
-    )(sign, left, val, own, oth)
-
-
-def pick_rows(at_ref, got_ref, fwd_ref, pay_ref):
+    )(left, flipped, val, own, oth)
+
+
+def pick_rows(at_ref, came_ref, fwd_ref, pay_ref, got_ref, sem):
+    copy = pltpu.make_async_copy(came_ref, got_ref, sem)
+    copy.start()
+    copy.wait()
     xl = at_ref[0]
     yl = at_ref[1]
     for q in range(Q):
@@ -112,15 +149,28 @@
         other = at_ref[2 + q]
         begin = at_ref[6 + q]
         for t in range(KQ):
-            fwd_ref[q, pl.ds(t, 1), :] = got_ref[base + yl * 4 + t // 3, pl.ds(xl * 3 + t % 3, 1), :]
+            row = got_ref[base + yl * 4 + t // 3, pl.ds(xl * 3 + t % 3, 1), :]
+            fwd_ref[q, pl.ds(t, 1), 0, :] = row[:, :64]
+            fwd_ref[q, pl.ds(t, 1), 1, :] = row[:, 64:]
             col = lax.rem(begin + t, 12)
             slot = base + (col // 6) * 4 + (col % 6) // 3
-            pay_ref[pl.ds(q * KQ + t, 1), :] = got_ref[slot, pl.ds(other * 3 + col % 3, 1), :]
-
-
-def pick_back(at_ref, got_ref, out_ref):
+            pay_ref[0, pl.ds(q * KQ + t, 1), :] = got_ref[slot, pl.ds(other * 3 + col % 3, 1), :]
+    pay = pay_ref[0]
+    for slot in range(1, 32):
+        pay_ref[slot, :, :] = pay
+
+
+def pick_back(at_ref, came_ref, out_ref, got_ref, sem):
+    copies = [
+        pltpu.make_async_copy(came_ref.at[at_ref[q]], got_ref.at[q], sem.at[q]) for q in range(Q)
+    ]
+    for copy in copies:
+        copy.start()
     for q in range(Q):
-        out_ref[q, :, :] = got_ref[at_ref[q], q * KQ : (q + 1) * KQ, :]
+        copies[q].wait()
+        rows = got_ref[q, q * KQ : (q + 1) * KQ, :]
+        out_ref[q, :, 0, :] = rows[:, :64]
+        out_ref[q, :, 1, :] = rows[:, 64:]
 
 
 def local(cond, val, screened, k_plus):
@@ -134,25 +184,32 @@
         lax.dynamic_slice_in_dim(w[i], (4 * i + z // 2) * BLK, SENT * BLK, 1) for i in range(2)
     ]
     w = jnp.stack(cut, 0)
-    w = lax.all_to_all(jnp.broadcast_to(w, (64,) + w.shape), ("z", "yh", "yl"), 0, 0)
+    w = jnp.broadcast_to(w, (64,) + w.shape)
+    w = lax.all_to_all(w, ("z", "yh", "yl"), 0, 0)
     own = jnp.transpose(w, (1, 0, 2, 3)).reshape(NG, SENT * BLK)
     oth = lax.ppermute(own, "c", [(0, 1), (1, 0)])
 
+    x = xl * 2 + lax.axis_index("xh")
+
     def spread(pairs):
-        got = lax.all_to_all(pairs.reshape(8, 3, 2, PAIR, 256), row8, 0, 0)
-        return jnp.transpose(got.reshape(2, 4, 3, 2, PAIR, 256), (0, 2, 3, 4, 1, 5)).reshape(
-            KQ, 2, PAIR, NG
-        )
-
-    left = spread(cond)
-    left = jnp.where(core == 0, left, jnp.stack([left[:, 1], -left[:, 0]], 1))
-    right = spread(val)
-    sign = jnp.where(core == 0, 1.0, -1.0).astype(F32).reshape(1)
-    block = contracted(
-        sign, left.reshape(2 * KQ * PAIR, NG), right.reshape(2 * KQ * PAIR, NG), own, oth
-    )
-    slots = jnp.broadcast_to(block.reshape(1, 1, 4, KQ, 128), (2, 2, 4, KQ, 128))
-    got = lax.all_to_all(slots.reshape(16, KQ, 128), ("xl", "yl", "xh", "c"), 0, 0)
+        slots = pairs.reshape(4, 2, 3, 2, PAIR, 256)
+        keep = lax.dynamic_index_in_dim(slots, core, 1, False)
+        given = lax.dynamic_index_in_dim(slots, 1 - core, 1, False)
+        given = lax.ppermute(given, "c", [(0, 1), (1, 0)])
+        pieces = []
+        for s in range(4):
+            both = [lax.dynamic_index_in_dim(part, x ^ s, 0, True) for part in (keep, given)]
+            piece = jnp.concatenate(both, 0)
+            if s:
+                piece = lax.ppermute(piece, ("xl", "xh"), [(i, i ^ s) for i in range(4)])
+            pieces.append(piece)
+        return pieces
+
+    pieces = spread(cond) + spread(val)
+    here_x = jnp.stack([x, core]).astype(jnp.int32)
+    left, flipped, right = assembled(here_x, pieces)
+    slots = contracted(left, flipped, right, own, oth)
+    got = lax.all_to_all(slots, ("xl", "yl", "xh", "c"), 0, 0)
     corner = k_plus[:, 0]
     row_step, col_step = corner // 12, corner % 12
     here = z * 4 + yh
@@ -161,24 +218,27 @@
     at = jnp.concatenate([jnp.stack([xl, yl]), other, begin]).astype(jnp.int32)
     vm = pl.BlockSpec(memory_space=pltpu.VMEM)
     sm = pl.BlockSpec(memory_space=pltpu.SMEM)
+    anywhere = pl.BlockSpec(memory_space=pl.ANY)
+    out = jax.ShapeDtypeStruct((Q, KQ, 2, 64), F32)
     forward, pay = pl.pallas_call(
         pick_rows,
-        out_shape=(
-            jax.ShapeDtypeStruct((Q, KQ, 128), F32),
-            jax.ShapeDtypeStruct((Q * KQ, 128), F32),
-        ),
-        in_specs=[sm, vm],
+        out_shape=(out, jax.ShapeDtypeStruct((32, Q * KQ, 128), F32)),
+        in_specs=[sm, anywhere],
         out_specs=(vm, vm),
+        scratch_shapes=[pltpu.VMEM((16, KQ, 128), F32), pltpu.SemaphoreType.DMA],
+        compiler_params=pltpu.CompilerParams(vmem_limit_bytes=8 << 20),
     )(at, got)
-    came = lax.all_to_all(jnp.broadcast_to(pay, (32,) + pay.shape), ("z", "yh"), 0, 0)
+    came = lax.all_to_all(pay, ("z", "yh"), 0, 0)
     source = ((here - row_step) % 32).astype(jnp.int32)
     back = pl.pallas_call(
         pick_back,
-        out_shape=jax.ShapeDtypeStruct((Q, KQ, 128), F32),
-        in_specs=[sm, vm],
+        out_shape=out,
+        in_specs=[sm, anywhere],
         out_specs=vm,
+        scratch_shapes=[pltpu.VMEM((Q, Q * KQ, 128), F32), pltpu.SemaphoreType.DMA((Q,))],
+        compiler_params=pltpu.CompilerParams(vmem_limit_bytes=8 << 20),
     )(source, came)
-    return forward.reshape(Q, KQ, 2, 64), back.reshape(Q, KQ, 2, 64)
+    return forward, back
 
 
 def solution(mesh):

time: 137 us -> 140 us (1.022)
  starting transfers between devices: 24.4 us -> 52 us
  blocking collectives: 50.8 us -> 23.2 us
  local copies, waits for them, and re-layouts: 8.98 us -> 2.77 us
  other arithmetic: 3.77 us -> 7.86 us
  waiting for transfers between devices: 38.6 us -> 41.2 us
  Pallas kernels: 8.91 us -> 11.2 us
    all_to_all x1, blocking collectives: 50.8 us -> 23.2 us  [local(): came = lax.all_to_all(pay, ('z', 'yh'), 0, 0)]
    ppermute x0 -> x8, starting transfers between devices: none -> 24.6 us  [the longest x6 20.2 us: spread(): piece = lax.ppermute(piece, ('xl', 'xh'), [(i, i ^ s) for i in range(4)])]
    concatenate x0 -> x8, other arithmetic: none -> 3.78 us  [spread(): piece = jnp.concatenate(both, 0)]
    all_to_all x4 -> x2, starting transfers between devices: 17.8 us -> 21.1 us  [the longest x1 16.6 us: local(): w = lax.all_to_all(w, ('z', 'yh', 'yl'), 0, 0)]
    reshape x3 -> x0, local copies, waits for them, and re-layouts: 3.08 us -> none  [the longest x2 2.82 us: local(): return (forward.reshape(Q, KQ, 2, 64), back.reshape(Q, KQ, 2, 64))]
    ppermute x0 -> x8, waiting for transfers between devices: none -> 3.06 us  [the longest x6 3.05 us: spread(): piece = lax.ppermute(piece, ('xl', 'xh'), [(i, i ^ s) for i in range(4)])]
    pallas_call x3 -> x4, Pallas kernels: 8.91 us -> 11.2 us  [the longest x1 5.51 us: contracted(): pl.pallas_call(contract, out_shape=jax.ShapeDtypeStruct((16, KQ, 128), F3...]
    broadcast_in_dim x4 -> x1, local copies, waits for them, and re-layouts: 2.92 us -> 1.17 us  [local(): w = jnp.broadcast_to(w, (64,) + w.shape)]
  transfers between devices with their start and end apart: 6 -> 12, of which waited for: 5 -> 4; matrix products, arithmetic and copies ran while one was open for 5% -> 6% of each run, Pallas kernels for 0% -> 2%
where the time goes in v2:
time: 140 us; the launch traced here: 139 us
  starting transfers between devices  52 us (37%)
  waiting for transfers between devices  41.2 us (29%)
  blocking collectives  23.2 us (17%)
  Pallas kernels  11.2 us (8%)
  other arithmetic  7.86 us (6%)
  local copies, waits for them, and re-layouts  2.77 us (2%)
    all_to_all x1, waiting for transfers between devices, local(): w = lax.all_to_all(w, ('z', 'yh', 'yl'), 0, 0)  26.7 us
    all_to_all x1, blocking collectives, local(): came = lax.all_to_all(pay, ('z', 'yh'), 0, 0)  23.2 us
    ppermute x6, starting transfers between devices, spread(): piece = lax.ppermute(piece, ('xl', 'xh'), [(i, i ^ s) for i in range(4)])  20.2 us
    all_to_all x1, starting transfers between devices, local(): w = lax.all_to_all(w, ('z', 'yh', 'yl'), 0, 0)  16.6 us
    all_to_all x1, waiting for transfers between devices, local(): got = lax.all_to_all(slots, ('xl', 'yl', 'xh', 'c'), 0, 0)  6.1 us
    pallas_call x1, Pallas kernels, contracted(): pl.pallas_call(contract, out_shape=jax.ShapeDtypeStruct((16, KQ, 128), F3...  5.51 us
    all_to_all x1, waiting for transfers between devices, local(): w = lax.all_to_all(screened.reshape(8, 8, 256), row8, 0, 0)  5.36 us
    all_to_all x1, starting transfers between devices, local(): got = lax.all_to_all(slots, ('xl', 'yl', 'xh', 'c'), 0, 0)  4.5 us
  transfers between devices with their start and end apart: 12, of which 4 were waited for; matrix products, arithmetic and copies ran while one was open for 6% of the time, Pallas kernels for 2%

profile of v2, /device:TPU:16, one launch (start us, length us, event | category | flops | bytes accessed | tf_op | source)
XLA Modules:
  0.0 139.2 jit_solution(8583485922385314584)
XLA Ops:
  0.6 4.3 %all-to-all-start = ((bf16[8,8,256]{2,1,0:T(8,128)(2,1)}), bf16[8,8,256]{2,1,0:T(8,128)(2,1)S(1)}, u32[]{:S(2)}, u32[]{:S(2)}) async-start(bf16[8,8,256]{2,1,0:T(8,128)(2,1)} %bitcast.44), calls=%async_computation | async-start | bytes 65536 | tf_op jit(solution)/shard_map/all_to_all | solution.py:180
  4.9 5.4 %all-to-all-done = bf16[8,8,256]{2,1,0:T(8,128)(2,1)S(1)} async-done(((bf16[8,8,256]{2,1,0:T(8,128)(2,1)}), bf16[8,8,256]{2,1,0:T(8,128)(2,1)S(1)}, u32[]{:S(2)}, u32[]{:S(2)}) %all-to-all-start) | async-done | bytes 32800 | tf_op jit(solution)/shard_map/all_to_all | solution.py:180
  10.4 1.2 broadcast_in_dim.3
  11.6 16.6 %all-to-all-start.1 = ((bf16[64,2,8,640]{3,2,1,0:T(8,128)(2,1)}), bf16[64,2,8,640]{3,2,1,0:T(8,128)(2,1)S(1)}, u32[]{:S(2)}, u32[]{:S(2)}) async-start(bf16[64,2,8,640]{3,2,1,0:T(8,128)(2,1)} %broadcast_in_dim.3), calls=%async_computation.1 | async-start | bytes 2621440 | tf_op jit(solution)/shard_map/all_to_all | solution.py:188
  28.2 1.9 %collective-permute-start.4 = (bf16[4,3,2,16,256]{4,3,2,1,0:T(8,128)(2,1)S(1)}, bf16[4,3,2,16,256]{4,3,2,1,0:T(8,128)(2,1)S(1)}, u32[]{:S(2)}, u32[]{:S(2)}) collective-permute-start(bf16[4,3,2,16,256]{4,3,2,1,0:T(8,128)(2,1)S(1)} %dynamic-slice_bitcast_fusion), channel_id=1, source_target_pairs={{0,1},{1,0},{2,3},{3,2},{4,5},{5,4},{6,7},{7,6},{8,9},{9,8},{10,11... | collective-permute-start | bytes 589832 | tf_op jit(solution)/shard_map/ppermute | solution.py:198
  30.2 2.4 %collective-permute-start = (bf16[4,3,2,16,256]{4,3,2,1,0:T(8,128)(2,1)S(1)}, bf16[4,3,2,16,256]{4,3,2,1,0:T(8,128)(2,1)S(1)}, u32[]{:S(2)}, u32[]{:S(2)}) collective-permute-start(bf16[4,3,2,16,256]{4,3,2,1,0:T(8,128)(2,1)S(1)} %dynamic-slice_bitcast_fusion.1), channel_id=1, source_target_pairs={{0,1},{1,0},{2,3},{3,2},{4,5},{5,4},{6,7},{7,6},{8,9},{9,8},{10,11... | collective-permute-start | bytes 589832 | tf_op jit(solution)/shard_map/ppermute | solution.py:198
  32.6 1.3 fusion.1
  34.0 1.3 divide_reduce_fusion
  36.0 26.7 %all-to-all-done.1 = bf16[64,2,8,640]{3,2,1,0:T(8,128)(2,1)S(1)} async-done(((bf16[64,2,8,640]{3,2,1,0:T(8,128)(2,1)}), bf16[64,2,8,640]{3,2,1,0:T(8,128)(2,1)S(1)}, u32[]{:S(2)}, u32[]{:S(2)}) %all-to-all-start.1) | async-done | bytes 1310752 | tf_op jit(solution)/shard_map/all_to_all | solution.py:188
  62.9 2.1 %collective-permute-start.8 = (bf16[1024,640]{1,0:T(8,128)(2,1)S(1)}, bf16[1024,640]{1,0:T(8,128)(2,1)}, u32[]{:S(2)}, u32[]{:S(2)}) collective-permute-start(bf16[1024,640]{1,0:T(8,128)(2,1)S(1)} %bitcast.35), channel_id=1, source_target_pairs={{0,1},{1,0},{2,3},{3,2},{4,5},{5,4},{6,7},{7,6},{8,9},{9,8},{10,11... | collective-permute-start | bytes 3932168 | tf_op jit(solution)/shard_map/ppermute | solution.py:190
  67.1 3.1 %collective-permute-start.3 = (bf16[2,3,2,16,256]{4,3,2,1,0:T(8,128)(2,1)S(1)}, bf16[2,3,2,16,256]{4,3,2,1,0:T(8,128)(2,1)S(1)}, u32[]{:S(2)}, u32[]{:S(2)}) collective-permute-start(bf16[2,3,2,16,256]{4,3,2,1,0:T(8,128)(2,1)S(1)} %pad_maximum_fusion.3), channel_id=1, source_target_pairs={{0,258},{2,256},{256,2},{258,0},{1,259},{3,257},{257,3},{259,1},{4... | collective-permute-start | bytes 294920 | tf_op jit(solution)/shard_map/ppermute | solution.py:204
  71.0 2.0 %collective-permute-start.2 = (bf16[2,3,2,16,256]{4,3,2,1,0:T(8,128)(2,1)S(1)}, bf16[2,3,2,16,256]{4,3,2,1,0:T(8,128)(2,1)S(1)}, u32[]{:S(2)}, u32[]{:S(2)}) collective-permute-start(bf16[2,3,2,16,256]{4,3,2,1,0:T(8,128)(2,1)S(1)} %pad_maximum_fusion.2), channel_id=1, source_target_pairs={{0,256},{2,258},{256,0},{258,2},{1,257},{3,259},{257,1},{259,3},{4... | collective-permute-start | bytes 294920 | tf_op jit(solution)/shard_map/ppermute | solution.py:204
  73.7 5.4 %collective-permute-start.1 = (bf16[2,3,2,16,256]{4,3,2,1,0:T(8,128)(2,1)S(1)}, bf16[2,3,2,16,256]{4,3,2,1,0:T(8,128)(2,1)S(1)}, u32[]{:S(2)}, u32[]{:S(2)}) collective-permute-start(bf16[2,3,2,16,256]{4,3,2,1,0:T(8,128)(2,1)S(1)} %pad_maximum_fusion.1), channel_id=1, source_target_pairs={{0,2},{2,0},{256,258},{258,256},{1,3},{3,1},{257,259},{259,257},{4... | collective-permute-start | bytes 294920 | tf_op jit(solution)/shard_map/ppermute | solution.py:204
  79.2 2.0 %collective-permute-start.5 = (bf16[2,3,2,16,256]{4,3,2,1,0:T(8,128)(2,1)S(1)}, bf16[2,3,2,16,256]{4,3,2,1,0:T(8,128)(2,1)S(1)}, u32[]{:S(2)}, u32[]{:S(2)}) collective-permute-start(bf16[2,3,2,16,256]{4,3,2,1,0:T(8,128)(2,1)S(1)} %pad_maximum_fusion.5), channel_id=1, source_target_pairs={{0,2},{2,0},{256,258},{258,256},{1,3},{3,1},{257,259},{259,257},{4... | collective-permute-start | bytes 294920 | tf_op jit(solution)/shard_map/ppermute | solution.py:204
  81.9 3.9 %collective-permute-start.6 = (bf16[2,3,2,16,256]{4,3,2,1,0:T(8,128)(2,1)S(1)}, bf16[2,3,2,16,256]{4,3,2,1,0:T(8,128)(2,1)S(1)}, u32[]{:S(2)}, u32[]{:S(2)}) collective-permute-start(bf16[2,3,2,16,256]{4,3,2,1,0:T(8,128)(2,1)S(1)} %pad_maximum_fusion.6), channel_id=1, source_target_pairs={{0,256},{2,258},{256,0},{258,2},{1,257},{3,259},{257,1},{259,3},{4... | collective-permute-start | bytes 294920 | tf_op jit(solution)/shard_map/ppermute | solution.py:204
  85.8 4.0 %collective-permute-start.7 = (bf16[2,3,2,16,256]{4,3,2,1,0:T(8,128)(2,1)S(1)}, bf16[2,3,2,16,256]{4,3,2,1,0:T(8,128)(2,1)S(1)}, u32[]{:S(2)}, u32[]{:S(2)}) collective-permute-start(bf16[2,3,2,16,256]{4,3,2,1,0:T(8,128)(2,1)S(1)} %pad_maximum_fusion.7), channel_id=1, source_target_pairs={{0,258},{2,256},{256,2},{258,0},{1,259},{3,257},{257,3},{259,1},{4... | collective-permute-start | bytes 294920 | tf_op jit(solution)/shard_map/ppermute | solution.py:204
  90.4 3.0 %collective-permute-done.7.refs_7_ = bf16[2,3,2,16,256]{4,3,2,1,0:T(8,128)(2,1)S(1)} collective-permute-done((bf16[2,3,2,16,256]{4,3,2,1,0:T(8,128)(2,1)S(1)}, bf16[2,3,2,16,256]{4,3,2,1,0:T(8,128)(2,1)S(1)}, u32[]{:S(2)}, u32[]{:S(2)}) %collective-permute-start.7) | collective-permute-done | bytes 98336 | tf_op jit(solution)/shard_map/ppermute | solution.py:204
  94.1 2.5 %shard_map.59 = (bf16[192,1024]{1,0:T(8,128)(2,1)}, bf16[192,1024]{1,0:T(8,128)(2,1)}, bf16[192,1024]{1,0:T(8,128)(2,1)}) custom-call(s32[2]{0:T(128)} %pad_add_fusion.1.at_ref, bf16[2,3,2,16,256]{4,3,2,1,0:T(8,128)(2,1)} %pad_maximum_fusion.refs_0_, bf16[2,3,2,16,256]{4,3,2,1,0:T(8,128)(2,1)} %copy-done.7, bf16[2,3,2,16,256]{4,3,2,1,0:T(8,128)(2,1)} %copy-done.6, ...), custom_call_target="tpu_custom_call" | custom-call | bytes 2000000 | tf_op jit(solution)/shard_map/pallas_call | solution.py:55
  96.6 5.5 %shard_map.60 = f32[16,6,128]{2,1,0:T(8,128)} custom-call(bf16[192,1024]{1,0:T(8,128)(2,1)} %get-tuple-element.7.left_ref, bf16[192,1024]{1,0:T(8,128)(2,1)} %get-tuple-element.8.flip_ref, bf16[192,1024]{1,0:T(8,128)(2,1)} %get-tuple-element.9.val_ref, bf16[1024,640]{1,0:T(8,128)(2,1)} %bitcast.36, bf16[1024,640]{1,0:T(8,128)(2,1)} %collective-permute-done.8.oth_ref), custom_call_target="tpu_custom_call" | custom-call | flops 1600000000 | bytes 4000000 | tf_op jit(solution)/shard_map/pallas_call | solution.py:126
  102.1 4.5 %all-to-all-start.2 = ((f32[16,6,128]{2,1,0:T(8,128)}), f32[16,6,128]{2,1,0:T(8,128)S(1)}, u32[]{:S(2)}, u32[]{:S(2)}) async-start(f32[16,6,128]{2,1,0:T(8,128)} %shard_map.60), calls=%async_computation.2 | async-start | bytes 131072 | tf_op jit(solution)/shard_map/all_to_all | solution.py:212
  106.7 6.1 %all-to-all-done.2.came_ref = f32[16,6,128]{2,1,0:T(8,128)S(1)} async-done(((f32[16,6,128]{2,1,0:T(8,128)}), f32[16,6,128]{2,1,0:T(8,128)S(1)}, u32[]{:S(2)}, u32[]{:S(2)}) %all-to-all-start.2) | async-done | bytes 49184 | tf_op jit(solution)/shard_map/all_to_all | solution.py:212
  112.8 1.6 %shard_map.61 = (f32[4,6,2,64]{3,2,1,0:T(2,128)}, f32[32,24,128]{2,1,0:T(8,128)S(1)}) custom-call(s32[10]{0:T(128)S(1)} %pad_add_fusion.at_ref, f32[16,6,128]{2,1,0:T(8,128)S(1)} %all-to-all-done.2.came_ref), custom_call_target="tpu_custom_call" | custom-call | tf_op jit(solution)/shard_map/pallas_call | solution.py:223
  114.5 23.2 %all_to_all.20.came_ref = f32[32,24,128]{2,1,0:T(8,128)S(1)} all-to-all(f32[32,24,128]{2,1,0:T(8,128)S(1)} %get-tuple-element.11), channel_id=1, replica_groups=mesh['xl'=2,'z'=8,'yh'=4,'yl'=2,'xh'=2,'c'=2] {'z','yh'}, dimensions={0} | all-to-all | bytes 786432 | tf_op jit(solution)/shard_map/all_to_all | solution.py:231
  137.7 1.6 %shard_map.62 = f32[4,6,2,64]{3,2,1,0:T(2,128)} custom-call(s32[4]{0:T(128)S(1)} %get-tuple-element.30.at_ref, f32[32,24,128]{2,1,0:T(8,128)S(1)} %all_to_all.20.came_ref), custom_call_target="tpu_custom_call" | custom-call | tf_op jit(solution)/shard_map/pallas_call | solution.py:233
  (51 shorter events, 6.8 us)
Async XLA Ops:
  0.6 9.7 %all-to-all-start = ((bf16[8,8,256]{2,1,0:T(8,128)(2,1)}), bf16[8,8,256]{2,1,0:T(8,128)(2,1)S(1)}, u32[]{:S(2)}, u32[]{:S(2)}) async-start(bf16[8,8,256]{2,1,0:T(8,128)(2,1)} %bitcast.44), calls=%async_computation | async-start | bytes 65536 | tf_op jit(solution)/shard_map/all_to_all | solution.py:180
  11.6 16.6 %copy-start.1 = (bf16[4,6,2,16,256]{4,3,2,1,0:T(8,128)(2,1)S(1)}, bf16[4,6,2,16,256]{4,3,2,1,0:T(8,128)(2,1)}, u32[]{:S(2)}) copy-start(bf16[4,6,2,16,256]{4,3,2,1,0:T(8,128)(2,1)} %param.5) | copy-start | bytes 1179652
  11.6 18.6 %copy-start.2 = (bf16[4,6,2,16,256]{4,3,2,1,0:T(8,128)(2,1)S(1)}, bf16[4,6,2,16,256]{4,3,2,1,0:T(8,128)(2,1)}, u32[]{:S(2)}) copy-start(bf16[4,6,2,16,256]{4,3,2,1,0:T(8,128)(2,1)} %param.4) | copy-start | bytes 1179652
  11.6 51.1 %all-to-all-start.1 = ((bf16[64,2,8,640]{3,2,1,0:T(8,128)(2,1)}), bf16[64,2,8,640]{3,2,1,0:T(8,128)(2,1)S(1)}, u32[]{:S(2)}, u32[]{:S(2)}) async-start(bf16[64,2,8,640]{3,2,1,0:T(8,128)(2,1)} %broadcast_in_dim.3), calls=%async_computation.1 | async-start | bytes 2621440 | tf_op jit(solution)/shard_map/all_to_all | solution.py:188
  28.2 38.0 %collective-permute-start.4 = (bf16[4,3,2,16,256]{4,3,2,1,0:T(8,128)(2,1)S(1)}, bf16[4,3,2,16,256]{4,3,2,1,0:T(8,128)(2,1)S(1)}, u32[]{:S(2)}, u32[]{:S(2)}) collective-permute-start(bf16[4,3,2,16,256]{4,3,2,1,0:T(8,128)(2,1)S(1)} %dynamic-slice_bitcast_fusion), channel_id=1, source_target_pairs={{0,1},{1,0},{2,3},{3,2},{4,5},{5,4},{6,7},{7,6},{8,9},{9,8},{10,11... | collective-permute-start | bytes 589832 | tf_op jit(solution)/shard_map/ppermute | solution.py:198
  30.2 36.0 %collective-permute-start = (bf16[4,3,2,16,256]{4,3,2,1,0:T(8,128)(2,1)S(1)}, bf16[4,3,2,16,256]{4,3,2,1,0:T(8,128)(2,1)S(1)}, u32[]{:S(2)}, u32[]{:S(2)}) collective-permute-start(bf16[4,3,2,16,256]{4,3,2,1,0:T(8,128)(2,1)S(1)} %dynamic-slice_bitcast_fusion.1), channel_id=1, source_target_pairs={{0,1},{1,0},{2,3},{3,2},{4,5},{5,4},{6,7},{7,6},{8,9},{9,8},{10,11... | collective-permute-start | bytes 589832 | tf_op jit(solution)/shard_map/ppermute | solution.py:198
  62.8 33.8 %copy-start = (bf16[2,64,8,640]{3,2,1,0:T(8,128)(2,1)}, bf16[2,64,8,640]{3,2,1,0:T(8,128)(2,1)S(1)}, u32[]{:S(2)}) copy-start(bf16[2,64,8,640]{3,2,1,0:T(8,128)(2,1)S(1)} %copy.6) | copy-start | bytes 3932164
  62.8 16.3 %copy-start.4 = (bf16[1,3,2,16,256]{4,3,2,1,0:T(8,128)(2,1)S(1)}, bf16[1,3,2,16,256]{4,3,2,1,0:T(8,128)(2,1)}, u32[]{:S(2)}) copy-start(bf16[1,3,2,16,256]{4,3,2,1,0:T(8,128)(2,1)} %get-tuple-element.16) | copy-start | bytes 147460
  62.8 18.3 %copy-start.3 = (bf16[1,3,2,16,256]{4,3,2,1,0:T(8,128)(2,1)S(1)}, bf16[1,3,2,16,256]{4,3,2,1,0:T(8,128)(2,1)}, u32[]{:S(2)}) copy-start(bf16[1,3,2,16,256]{4,3,2,1,0:T(8,128)(2,1)} %get-tuple-element.14) | copy-start | bytes 147460
  62.9 33.8 %collective-permute-start.8 = (bf16[1024,640]{1,0:T(8,128)(2,1)S(1)}, bf16[1024,640]{1,0:T(8,128)(2,1)}, u32[]{:S(2)}, u32[]{:S(2)}) collective-permute-start(bf16[1024,640]{1,0:T(8,128)(2,1)S(1)} %bitcast.35), channel_id=1, source_target_pairs={{0,1},{1,0},{2,3},{3,2},{4,5},{5,4},{6,7},{7,6},{8,9},{9,8},{10,11... | collective-permute-start | bytes 3932168 | tf_op jit(solution)/shard_map/ppermute | solution.py:190
  67.1 14.8 %collective-permute-start.3 = (bf16[2,3,2,16,256]{4,3,2,1,0:T(8,128)(2,1)S(1)}, bf16[2,3,2,16,256]{4,3,2,1,0:T(8,128)(2,1)S(1)}, u32[]{:S(2)}, u32[]{:S(2)}) collective-permute-start(bf16[2,3,2,16,256]{4,3,2,1,0:T(8,128)(2,1)S(1)} %pad_maximum_fusion.3), channel_id=1, source_target_pairs={{0,258},{2,256},{256,2},{258,0},{1,259},{3,257},{257,3},{259,1},{4... | collective-permute-start | bytes 294920 | tf_op jit(solution)/shard_map/ppermute | solution.py:204
  71.0 14.8 %collective-permute-start.2 = (bf16[2,3,2,16,256]{4,3,2,1,0:T(8,128)(2,1)S(1)}, bf16[2,3,2,16,256]{4,3,2,1,0:T(8,128)(2,1)S(1)}, u32[]{:S(2)}, u32[]{:S(2)}) collective-permute-start(bf16[2,3,2,16,256]{4,3,2,1,0:T(8,128)(2,1)S(1)} %pad_maximum_fusion.2), channel_id=1, source_target_pairs={{0,256},{2,258},{256,0},{258,2},{1,257},{3,259},{257,1},{259,3},{4... | collective-permute-start | bytes 294920 | tf_op jit(solution)/shard_map/ppermute | solution.py:204
  73.7 16.7 %collective-permute-start.1 = (bf16[2,3,2,16,256]{4,3,2,1,0:T(8,128)(2,1)S(1)}, bf16[2,3,2,16,256]{4,3,2,1,0:T(8,128)(2,1)S(1)}, u32[]{:S(2)}, u32[]{:S(2)}) collective-permute-start(bf16[2,3,2,16,256]{4,3,2,1,0:T(8,128)(2,1)S(1)} %pad_maximum_fusion.1), channel_id=1, source_target_pairs={{0,2},{2,0},{256,258},{258,256},{1,3},{3,1},{257,259},{259,257},{4... | collective-permute-start | bytes 294920 | tf_op jit(solution)/shard_map/ppermute | solution.py:204
  79.2 11.2 %collective-permute-start.5 = (bf16[2,3,2,16,256]{4,3,2,1,0:T(8,128)(2,1)S(1)}, bf16[2,3,2,16,256]{4,3,2,1,0:T(8,128)(2,1)S(1)}, u32[]{:S(2)}, u32[]{:S(2)}) collective-permute-start(bf16[2,3,2,16,256]{4,3,2,1,0:T(8,128)(2,1)S(1)} %pad_maximum_fusion.5), channel_id=1, source_target_pairs={{0,2},{2,0},{256,258},{258,256},{1,3},{3,1},{257,259},{259,257},{4... | collective-permute-start | bytes 294920 | tf_op jit(solution)/shard_map/ppermute | solution.py:204
  81.8 11.6 %copy-start.5 = (bf16[2,3,2,16,256]{4,3,2,1,0:T(8,128)(2,1)}, bf16[2,3,2,16,256]{4,3,2,1,0:T(8,128)(2,1)S(1)}, u32[]{:S(2)}) copy-start(bf16[2,3,2,16,256]{4,3,2,1,0:T(8,128)(2,1)S(1)} %collective-permute-done.3.refs_3_) | copy-start | bytes 294916
  81.9 8.6 %collective-permute-start.6 = (bf16[2,3,2,16,256]{4,3,2,1,0:T(8,128)(2,1)S(1)}, bf16[2,3,2,16,256]{4,3,2,1,0:T(8,128)(2,1)S(1)}, u32[]{:S(2)}, u32[]{:S(2)}) collective-permute-start(bf16[2,3,2,16,256]{4,3,2,1,0:T(8,128)(2,1)S(1)} %pad_maximum_fusion.6), channel_id=1, source_target_pairs={{0,256},{2,258},{256,0},{258,2},{1,257},{3,259},{257,1},{259,3},{4... | collective-permute-start | bytes 294920 | tf_op jit(solution)/shard_map/ppermute | solution.py:204
  85.7 7.7 %copy-start.6 = (bf16[2,3,2,16,256]{4,3,2,1,0:T(8,128)(2,1)}, bf16[2,3,2,16,256]{4,3,2,1,0:T(8,128)(2,1)S(1)}, u32[]{:S(2)}) copy-start(bf16[2,3,2,16,256]{4,3,2,1,0:T(8,128)(2,1)S(1)} %collective-permute-done.2.refs_2_) | copy-start | bytes 294916
  85.8 7.7 %collective-permute-start.7 = (bf16[2,3,2,16,256]{4,3,2,1,0:T(8,128)(2,1)S(1)}, bf16[2,3,2,16,256]{4,3,2,1,0:T(8,128)(2,1)S(1)}, u32[]{:S(2)}, u32[]{:S(2)}) collective-permute-start(bf16[2,3,2,16,256]{4,3,2,1,0:T(8,128)(2,1)S(1)} %pad_maximum_fusion.7), channel_id=1, source_target_pairs={{0,258},{2,256},{256,2},{258,0},{1,259},{3,257},{257,3},{259,1},{4... | collective-permute-start | bytes 294920 | tf_op jit(solution)/shard_map/ppermute | solution.py:204
  90.4 3.1 %copy-start.7 = (bf16[2,3,2,16,256]{4,3,2,1,0:T(8,128)(2,1)}, bf16[2,3,2,16,256]{4,3,2,1,0:T(8,128)(2,1)S(1)}, u32[]{:S(2)}) copy-start(bf16[2,3,2,16,256]{4,3,2,1,0:T(8,128)(2,1)S(1)} %collective-permute-done.1.refs_1_) | copy-start | bytes 294916
  90.4 3.1 %copy-start.8 = (bf16[2,3,2,16,256]{4,3,2,1,0:T(8,128)(2,1)}, bf16[2,3,2,16,256]{4,3,2,1,0:T(8,128)(2,1)S(1)}, u32[]{:S(2)}) copy-start(bf16[2,3,2,16,256]{4,3,2,1,0:T(8,128)(2,1)S(1)} %collective-permute-done.5.refs_5_) | copy-start | bytes 294916
  90.4 3.1 %copy-start.9 = (bf16[2,3,2,16,256]{4,3,2,1,0:T(8,128)(2,1)}, bf16[2,3,2,16,256]{4,3,2,1,0:T(8,128)(2,1)S(1)}, u32[]{:S(2)}) copy-start(bf16[2,3,2,16,256]{4,3,2,1,0:T(8,128)(2,1)S(1)} %collective-permute-done.6.refs_6_) | copy-start | bytes 294916
  93.5 0.6 copy-start.10
  102.1 10.7 %all-to-all-start.2 = ((f32[16,6,128]{2,1,0:T(8,128)}), f32[16,6,128]{2,1,0:T(8,128)S(1)}, u32[]{:S(2)}, u32[]{:S(2)}) async-start(f32[16,6,128]{2,1,0:T(8,128)} %shard_map.60), calls=%async_computation.2 | async-start | bytes 131072 | tf_op jit(solution)/shard_map/all_to_all | solution.py:212

commit v3 on v2

--- a/solution.py
+++ b/solution.py
@@ -28,7 +28,7 @@
 
 
 def assemble(at_ref, *refs):
-    pieces, (left_ref, flip_ref, val_ref) = refs[:8], refs[8:]
+    pieces, (left_ref, flip_ref, val_ref) = refs[:4], refs[4:]
     x, core = at_ref[0], at_ref[1]
     minus = jnp.where(core == 0, 1.0, -1.0).astype(BF)
     for s in range(4):
@@ -39,10 +39,10 @@
             for j in range(3):
                 row = xl * 96 + j * 32
                 whole = pl.ds(pl.multiple_of(row, 32), 32)
-                val_ref[whole, lanes] = pieces[4 + s][t, j].reshape(32, 256)
+                val_ref[whole, lanes] = pieces[s][1, t, j].reshape(32, 256)
                 for r in range(2):
                     part = pl.ds(pl.multiple_of(row + (r ^ core) * PAIR, PAIR), PAIR)
-                    piece = pieces[s][t, j, r]
+                    piece = pieces[s][0, t, j, r]
                     if r == 0:
                         piece = piece * minus
                     left_ref[part, lanes] = piece
@@ -55,39 +55,36 @@
     return pl.pallas_call(
         assemble,
         out_shape=(flat, flat, flat),
-        in_specs=[pl.BlockSpec(memory_space=pltpu.SMEM)] + [vm] * 8,
+        in_specs=[pl.BlockSpec(memory_space=pltpu.SMEM)] + [vm] * 4,
         out_specs=(vm, vm, vm),
         cost_estimate=pl.CostEstimate(flops=0, bytes_accessed=2_000_000, transcendentals=0),
     )(at, *pieces)
 
 
-def contract(left_ref, flip_ref, val_ref, own_ref, oth_ref, out_ref, p_ref, q_ref):
-    left = left_ref[...]
-    flipped = flip_ref[...]
-    rows = left.shape[0]
-    wrapped = jnp.concatenate([left, left[:, : 3 * BLK]], 1)
-    wrapped_flip = jnp.concatenate([flipped, flipped[:, : 3 * BLK]], 1)
+def screen(ahead_ref, behind_ref, w_ref, sum_ref, negate):
+    ahead = ahead_ref[...]
+    behind = behind_ref[...]
+    wrapped = jnp.concatenate([behind, behind[:, : 3 * BLK]], 1)
+    sum_ref[...] = jnp.zeros_like(sum_ref)
     for b in range(NB):
         lo, hi = b * BLK, (b + 1) * BLK
-        far = wrapped[:, hi : hi + 3 * BLK]
-        far_flip = wrapped_flip[:, hi : hi + 3 * BLK]
-        own = own_ref[lo:hi, :]
-        oth = oth_ref[lo:hi, :]
-        p_back = nt(far_flip, own[:, BLK : 4 * BLK])
-        q_back = -nt(far, oth[:, BLK : 4 * BLK])
-        if b == 0:
-            p_ref[...] = jnp.zeros_like(p_ref)
-            q_ref[...] = jnp.zeros_like(q_ref)
-        p_ref[:, lo:hi] += p_back
-        q_ref[:, lo:hi] += q_back
-        p_fore = nn(left[:, lo:hi], own)
-        q_fore = nn(flipped[:, lo:hi], oth)
+        w = w_ref[lo:hi, :]
+        back = nt(wrapped[:, hi : hi + 3 * BLK], w[:, BLK : 4 * BLK])
+        sum_ref[:, lo:hi] += -back if negate else back
+        fore = nn(ahead[:, lo:hi], w)
         first = min(SENT, NB - b)
-        p_ref[:, lo : lo + first * BLK] += p_fore[:, : first * BLK]
-        q_ref[:, lo : lo + first * BLK] += q_fore[:, : first * BLK]
+        sum_ref[:, lo : lo + first * BLK] += fore[:, : first * BLK]
         if first < SENT:
-            p_ref[:, : (SENT - first) * BLK] += p_fore[:, first * BLK :]
-            q_ref[:, : (SENT - first) * BLK] += q_fore[:, first * BLK :]
+            sum_ref[:, : (SENT - first) * BLK] += fore[:, first * BLK :]
+
+
+def contract_own(left_ref, flip_ref, own_ref, p_ref):
+    screen(left_ref, flip_ref, own_ref, p_ref, False)
+
+
+def contract(left_ref, flip_ref, val_ref, oth_ref, p_ref, out_ref, q_ref):
+    screen(flip_ref, left_ref, oth_ref, q_ref, True)
+    rows = left_ref.shape[0]
     p = p_ref[...].reshape(KQ, 2, PAIR, NG)
     q = q_ref[...].reshape(KQ, 2, PAIR, NG)
     half = rows // 2
@@ -123,19 +120,23 @@
 
 def contracted(left, flipped, val, own, oth):
     vm = pl.BlockSpec(memory_space=pltpu.VMEM)
+    cost = pl.CostEstimate(flops=800_000_000, bytes_accessed=3_000_000, transcendentals=0)
+    sums = (2 * KQ * PAIR, NG)
+    p = pl.pallas_call(
+        contract_own,
+        out_shape=jax.ShapeDtypeStruct(sums, F32),
+        in_specs=[vm] * 3,
+        out_specs=vm,
+        cost_estimate=cost,
+    )(left, flipped, own)
     return pl.pallas_call(
         contract,
         out_shape=jax.ShapeDtypeStruct((16, KQ, 128), F32),
         in_specs=[vm] * 5,
         out_specs=vm,
-        scratch_shapes=[
-            pltpu.VMEM((2 * KQ * PAIR, NG), F32),
-            pltpu.VMEM((2 * KQ * PAIR, NG), F32),
-        ],
-        cost_estimate=pl.CostEstimate(
-            flops=1_600_000_000, bytes_accessed=4_000_000, transcendentals=0
-        ),
-    )(left, flipped, val, own, oth)
+        scratch_shapes=[pltpu.VMEM(sums, F32)],
+        cost_estimate=cost,
+    )(left, flipped, val, oth, p)
 
 
 def pick_rows(at_ref, came_ref, fwd_ref, pay_ref, got_ref, sem):
@@ -176,36 +177,37 @@
 def local(cond, val, screened, k_plus):
     xl, yl, core = lax.axis_index("xl"), lax.axis_index("yl"), lax.axis_index("c")
     z, yh = lax.axis_index("z"), lax.axis_index("yh")
-    row8 = ("xl", "xh", "c")
-    w = lax.all_to_all(screened.reshape(8, 8, 256), row8, 0, 0)
-    w = jnp.transpose(w.reshape(2, 4, 8, 256), (0, 2, 1, 3)).reshape(2, 8, NG)
-    w = jnp.concatenate([w, w[:, :, : 4 * BLK]], 2)
+    w = screened.reshape(2, 1, 4, 8, 256)
+    w = jnp.broadcast_to(w, (2, 2, 4, 8, 256)).reshape(16, 8, 256)
+    w = lax.all_to_all(w, ("xl", "yl", "xh", "c"), 0, 0)
+    w = jnp.transpose(w.reshape(2, 2, 4, 8, 256), (0, 1, 3, 2, 4)).reshape(2, 2, 8, NG)
+    w = jnp.concatenate([w, w[..., : 4 * BLK]], 3)
     cut = [
-        lax.dynamic_slice_in_dim(w[i], (4 * i + z // 2) * BLK, SENT * BLK, 1) for i in range(2)
+        lax.dynamic_slice_in_dim(w[i], (4 * i + z // 2) * BLK, SENT * BLK, 2) for i in range(2)
     ]
     w = jnp.stack(cut, 0)
-    w = jnp.broadcast_to(w, (64,) + w.shape)
-    w = lax.all_to_all(w, ("z", "yh", "yl"), 0, 0)
-    own = jnp.transpose(w, (1, 0, 2, 3)).reshape(NG, SENT * BLK)
+    w = jnp.broadcast_to(w, (32,) + w.shape)
+    w = lax.all_to_all(w, ("z", "yh"), 0, 0)
+    own = jnp.transpose(w, (1, 0, 2, 3, 4)).reshape(NG, SENT * BLK)
     oth = lax.ppermute(own, "c", [(0, 1), (1, 0)])
 
     x = xl * 2 + lax.axis_index("xh")
 
-    def spread(pairs):
-        slots = pairs.reshape(4, 2, 3, 2, PAIR, 256)
-        keep = lax.dynamic_index_in_dim(slots, core, 1, False)
-        given = lax.dynamic_index_in_dim(slots, 1 - core, 1, False)
-        given = lax.ppermute(given, "c", [(0, 1), (1, 0)])
-        pieces = []
-        for s in range(4):
-            both = [lax.dynamic_index_in_dim(part, x ^ s, 0, True) for part in (keep, given)]
-            piece = jnp.concatenate(both, 0)
-            if s:
-                piece = lax.ppermute(piece, ("xl", "xh"), [(i, i ^ s) for i in range(4)])
-            pieces.append(piece)
-        return pieces
-
-    pieces = spread(cond) + spread(val)
+    slots = [pairs.reshape(4, 2, 3, 2, PAIR, 256) for pairs in (cond, val)]
+    keep = [lax.dynamic_index_in_dim(part, core, 1, False) for part in slots]
+    given = [lax.dynamic_index_in_dim(part, 1 - core, 1, False) for part in slots]
+    given = jnp.stack(given, 0)
+    given = lax.ppermute(given, "c", [(0, 1), (1, 0)])
+    pieces = []
+    for s in range(4):
+        both = [
+            lax.dynamic_index_in_dim(part, x ^ s, 0, False)
+            for part in (keep[0], given[0], keep[1], given[1])
+        ]
+        piece = jnp.stack(both, 0).reshape(2, 2, 3, 2, PAIR, 256)
+        if s:
+            piece = lax.ppermute(piece, ("xl", "xh"), [(i, i ^ s) for i in range(4)])
+        pieces.append(piece)
     here_x = jnp.stack([x, core]).astype(jnp.int32)
     left, flipped, right = assembled(here_x, pieces)
     slots = contracted(left, flipped, right, own, oth)

time: 140 us -> 142 us (1.014)
  starting transfers between devices: 52 us -> 38 us
  waiting for transfers between devices: 41.2 us -> 51.1 us
  blocking collectives: 23.2 us -> 29.1 us
  other arithmetic: 7.86 us -> 3.23 us
  local copies, waits for them, and re-layouts: 2.77 us -> 5.37 us
  Pallas kernels: 11.2 us -> 13.5 us
    ppermute x8 -> x4, starting transfers between devices: 24.6 us -> 11.7 us  [the longest x3 9.82 us: local(): piece = lax.ppermute(piece, ('xl', 'xh'), [(i, i ^ s) for i in range(4)])]
    all_to_all x2, waiting for transfers between devices: 32 us -> 38.7 us  [the longest x1 32.6 us: local(): w = lax.all_to_all(w, ('z', 'yh'), 0, 0)]
    all_to_all x1, blocking collectives: 23.2 us -> 29.1 us  [local(): came = lax.all_to_all(pay, ('z', 'yh'), 0, 0)]
    concatenate x10 -> x2, other arithmetic: 3.84 us -> 0.07 us  [local(): w = jnp.concatenate([w, w[..., :4 * BLK]], 3)]
    pallas_call x0 -> x1, Pallas kernels: none -> 3.46 us  [contracted(): pl.pallas_call(contract_own, out_shape=jax.ShapeDtypeStruct(sums, F32), i...]
    ppermute x8 -> x4, waiting for transfers between devices: 3.06 us -> 6.33 us  [the longest x3 6.33 us: local(): piece = lax.ppermute(piece, ('xl', 'xh'), [(i, i ^ s) for i in range(4)])]
  transfers between devices with their start and end apart: 12 -> 8, of which waited for: 4 -> 5; matrix products, arithmetic and copies ran while one was open for 6% -> 3% of each run, Pallas kernels for 2% -> 4%
where the time goes in v3:
time: 142 us; the launch traced here: 141 us
  waiting for transfers between devices  51.1 us (36%)
  starting transfers between devices  38 us (27%)
  blocking collectives  29.1 us (20%)
  Pallas kernels  13.5 us (10%)
  local copies, waits for them, and re-layouts  5.37 us (4%)
  other arithmetic  3.23 us (2%)
    all_to_all x1, waiting for transfers between devices, local(): w = lax.all_to_all(w, ('z', 'yh'), 0, 0)  32.6 us
    all_to_all x1, blocking collectives, local(): came = lax.all_to_all(pay, ('z', 'yh'), 0, 0)  29.1 us
    all_to_all x1, starting transfers between devices, local(): w = lax.all_to_all(w, ('z', 'yh'), 0, 0)  15.3 us
    ppermute x3, starting transfers between devices, local(): piece = lax.ppermute(piece, ('xl', 'xh'), [(i, i ^ s) for i in range(4)])  9.82 us
    ppermute x3, waiting for transfers between devices, local(): piece = lax.ppermute(piece, ('xl', 'xh'), [(i, i ^ s) for i in range(4)])  6.33 us
    all_to_all x1, waiting for transfers between devices, local(): w = lax.all_to_all(w, ('xl', 'yl', 'xh', 'c'), 0, 0)  6.15 us
    all_to_all x1, waiting for transfers between devices, local(): got = lax.all_to_all(slots, ('xl', 'yl', 'xh', 'c'), 0, 0)  6.04 us
    all_to_all x1, starting transfers between devices, local(): w = lax.all_to_all(w, ('xl', 'yl', 'xh', 'c'), 0, 0)  5.42 us
  transfers between devices with their start and end apart: 8, of which 5 were waited for; matrix products, arithmetic and copies ran while one was open for 3% of the time, Pallas kernels for 4%

profile of v3, /device:TPU:16, one launch (start us, length us, event | category | flops | bytes accessed | tf_op | source)
XLA Modules:
  0.0 141.4 jit_solution(14663005520899891298)
XLA Ops:
  0.6 1.4 broadcast_in_dim.11
  2.0 5.4 %all-to-all-start = ((bf16[16,8,256]{2,1,0:T(8,128)(2,1)}), bf16[16,8,256]{2,1,0:T(8,128)(2,1)S(1)}, u32[]{:S(2)}, u32[]{:S(2)}) async-start(bf16[16,8,256]{2,1,0:T(8,128)(2,1)} %bitcast.29), calls=%async_computation | async-start | bytes 131072 | tf_op jit(solution)/shard_map/all_to_all | solution.py:182
  7.5 6.2 %all-to-all-done = bf16[16,8,256]{2,1,0:T(8,128)(2,1)S(1)} async-done(((bf16[16,8,256]{2,1,0:T(8,128)(2,1)}), bf16[16,8,256]{2,1,0:T(8,128)(2,1)S(1)}, u32[]{:S(2)}, u32[]{:S(2)}) %all-to-all-start) | async-done | bytes 65568 | tf_op jit(solution)/shard_map/all_to_all | solution.py:182
  13.7 1.2 broadcast_in_dim.12
  14.9 15.3 %all-to-all-start.1 = ((bf16[32,2,2,8,640]{4,3,2,1,0:T(8,128)(2,1)}), bf16[32,2,2,8,640]{4,3,2,1,0:T(8,128)(2,1)S(1)}, u32[]{:S(2)}, u32[]{:S(2)}) async-start(bf16[32,2,2,8,640]{4,3,2,1,0:T(8,128)(2,1)} %broadcast_in_dim.12), calls=%async_computation.1 | async-start | bytes 2621440 | tf_op jit(solution)/shard_map/all_to_all | solution.py:190
  30.3 1.9 %collective-permute-start = (bf16[2,4,3,2,16,256]{5,4,3,2,1,0:T(8,128)(2,1)S(1)}, bf16[2,4,3,2,16,256]{5,4,3,2,1,0:T(8,128)(2,1)S(1)}, u32[]{:S(2)}, u32[]{:S(2)}) collective-permute-start(bf16[2,4,3,2,16,256]{5,4,3,2,1,0:T(8,128)(2,1)S(1)} %pad_maximum_fusion), channel_id=1, source_target_pairs={{0,1},{1,0},{2,3},{3,2},{4,5},{5,4},{6,7},{7,6},{8,9},{9,8},{10,11... | collective-permute-start | bytes 1179656 | tf_op jit(solution)/shard_map/ppermute | solution.py:200
  32.3 0.8 divide_reduce_fusion
  33.1 0.8 fusion.1
  34.7 32.6 %all-to-all-done.1 = bf16[32,2,2,8,640]{4,3,2,1,0:T(8,128)(2,1)S(1)} async-done(((bf16[32,2,2,8,640]{4,3,2,1,0:T(8,128)(2,1)}), bf16[32,2,2,8,640]{4,3,2,1,0:T(8,128)(2,1)S(1)}, u32[]{:S(2)}, u32[]{:S(2)}) %all-to-all-start.1) | async-done | bytes 1310752 | tf_op jit(solution)/shard_map/all_to_all | solution.py:190
  67.5 2.1 %collective-permute-start.4 = (bf16[1024,640]{1,0:T(8,128)(2,1)S(1)}, bf16[1024,640]{1,0:T(8,128)(2,1)S(1)}, u32[]{:S(2)}, u32[]{:S(2)}) collective-permute-start(bf16[1024,640]{1,0:T(8,128)(2,1)S(1)} %bitcast.56), channel_id=1, source_target_pairs={{0,1},{1,0},{2,3},{3,2},{4,5},{5,4},{6,7},{7,6},{8,9},{9,8},{10,11... | collective-permute-start | bytes 3932168 | tf_op jit(solution)/shard_map/ppermute | solution.py:192
  69.8 5.4 %collective-permute-start.1 = (bf16[2,2,3,2,16,256]{5,4,3,2,1,0:T(8,128)(2,1)S(1)}, bf16[2,2,3,2,16,256]{5,4,3,2,1,0:T(8,128)(2,1)S(1)}, u32[]{:S(2)}, u32[]{:S(2)}) collective-permute-start(bf16[2,2,3,2,16,256]{5,4,3,2,1,0:T(8,128)(2,1)S(1)} %bitcast.66), channel_id=1, source_target_pairs={{0,2},{2,0},{256,258},{258,256},{1,3},{3,1},{257,259},{259,257},{4... | collective-permute-start | bytes 589832 | tf_op jit(solution)/shard_map/ppermute | solution.py:209
  75.2 1.9 %collective-permute-start.2 = (bf16[2,2,3,2,16,256]{5,4,3,2,1,0:T(8,128)(2,1)S(1)}, bf16[2,2,3,2,16,256]{5,4,3,2,1,0:T(8,128)(2,1)S(1)}, u32[]{:S(2)}, u32[]{:S(2)}) collective-permute-start(bf16[2,2,3,2,16,256]{5,4,3,2,1,0:T(8,128)(2,1)S(1)} %bitcast.67), channel_id=1, source_target_pairs={{0,256},{2,258},{256,0},{258,2},{1,257},{3,259},{257,1},{259,3},{4... | collective-permute-start | bytes 589832 | tf_op jit(solution)/shard_map/ppermute | solution.py:209
  77.2 2.5 %collective-permute-start.3 = (bf16[2,2,3,2,16,256]{5,4,3,2,1,0:T(8,128)(2,1)S(1)}, bf16[2,2,3,2,16,256]{5,4,3,2,1,0:T(8,128)(2,1)S(1)}, u32[]{:S(2)}, u32[]{:S(2)}) collective-permute-start(bf16[2,2,3,2,16,256]{5,4,3,2,1,0:T(8,128)(2,1)S(1)} %bitcast.68), channel_id=1, source_target_pairs={{0,258},{2,256},{256,2},{258,0},{1,259},{3,257},{257,3},{259,1},{4... | collective-permute-start | bytes 589832 | tf_op jit(solution)/shard_map/ppermute | solution.py:209
  81.0 3.2 %collective-permute-done.2.refs_2_ = bf16[2,2,3,2,16,256]{5,4,3,2,1,0:T(8,128)(2,1)S(1)} collective-permute-done((bf16[2,2,3,2,16,256]{5,4,3,2,1,0:T(8,128)(2,1)S(1)}, bf16[2,2,3,2,16,256]{5,4,3,2,1,0:T(8,128)(2,1)S(1)}, u32[]{:S(2)}, u32[]{:S(2)}) %collective-permute-start.2) | collective-permute-done | bytes 196640 | tf_op jit(solution)/shard_map/ppermute | solution.py:209
  84.2 3.2 %collective-permute-done.3.refs_3_ = bf16[2,2,3,2,16,256]{5,4,3,2,1,0:T(8,128)(2,1)S(1)} collective-permute-done((bf16[2,2,3,2,16,256]{5,4,3,2,1,0:T(8,128)(2,1)S(1)}, bf16[2,2,3,2,16,256]{5,4,3,2,1,0:T(8,128)(2,1)S(1)}, u32[]{:S(2)}, u32[]{:S(2)}) %collective-permute-start.3) | collective-permute-done | bytes 196640 | tf_op jit(solution)/shard_map/ppermute | solution.py:209
  88.0 2.4 %shard_map.59 = (bf16[192,1024]{1,0:T(8,128)(2,1)}, bf16[192,1024]{1,0:T(8,128)(2,1)}, bf16[192,1024]{1,0:T(8,128)(2,1)}) custom-call(s32[2]{0:T(128)} %pad_add_fusion.1.at_ref, bf16[2,2,3,2,16,256]{5,4,3,2,1,0:T(8,128)(2,1)} %bitcast.61, bf16[2,2,3,2,16,256]{5,4,3,2,1,0:T(8,128)(2,1)} %copy-done.4, bf16[2,2,3,2,16,256]{5,4,3,2,1,0:T(8,128)(2,1)} %copy-done.5, ...), custom_call_target="tpu_custom_call" | custom-call | bytes 2000000 | tf_op jit(solution)/shard_map/pallas_call | solution.py:55
  90.5 3.5 %shard_map.60.p_ref = f32[192,1024]{1,0:T(8,128)} custom-call(bf16[192,1024]{1,0:T(8,128)(2,1)} %get-tuple-element.7.left_ref, bf16[192,1024]{1,0:T(8,128)(2,1)} %get-tuple-element.8.flip_ref, bf16[1024,640]{1,0:T(8,128)(2,1)} %bitcast.57), custom_call_target="tpu_custom_call" | custom-call | flops 800000000 | bytes 3000000 | tf_op jit(solution)/shard_map/pallas_call | solution.py:125
  94.0 1.1 copy-done
  95.0 4.4 %shard_map.61 = f32[16,6,128]{2,1,0:T(8,128)} custom-call(bf16[192,1024]{1,0:T(8,128)(2,1)} %get-tuple-element.7.left_ref, bf16[192,1024]{1,0:T(8,128)(2,1)} %get-tuple-element.8.flip_ref, bf16[192,1024]{1,0:T(8,128)(2,1)} %get-tuple-element.9.val_ref, bf16[1024,640]{1,0:T(8,128)(2,1)} %copy-done, f32[192,1024]{1,0:T(8,128)} %shard_map.60.p_ref), custom_call_target="tpu_custom_call" | custom-call | flops 800000000 | bytes 3000000 | tf_op jit(solution)/shard_map/pallas_call | solution.py:132
  99.5 3.5 %all-to-all-start.2 = ((f32[16,6,128]{2,1,0:T(8,128)}), f32[16,6,128]{2,1,0:T(8,128)S(1)}, u32[]{:S(2)}, u32[]{:S(2)}) async-start(f32[16,6,128]{2,1,0:T(8,128)} %shard_map.61), calls=%async_computation.2 | async-start | bytes 131072 | tf_op jit(solution)/shard_map/all_to_all | solution.py:214
  103.0 6.0 %all-to-all-done.2.came_ref = f32[16,6,128]{2,1,0:T(8,128)S(1)} async-done(((f32[16,6,128]{2,1,0:T(8,128)}), f32[16,6,128]{2,1,0:T(8,128)S(1)}, u32[]{:S(2)}, u32[]{:S(2)}) %all-to-all-start.2) | async-done | bytes 49184 | tf_op jit(solution)/shard_map/all_to_all | solution.py:214
  109.1 1.6 %shard_map.62 = (f32[4,6,2,64]{3,2,1,0:T(2,128)}, f32[32,24,128]{2,1,0:T(8,128)S(1)}) custom-call(s32[10]{0:T(128)S(1)} %pad_add_fusion.at_ref, f32[16,6,128]{2,1,0:T(8,128)S(1)} %all-to-all-done.2.came_ref), custom_call_target="tpu_custom_call" | custom-call | tf_op jit(solution)/shard_map/pallas_call | solution.py:225
  110.7 29.1 %all_to_all.20.came_ref = f32[32,24,128]{2,1,0:T(8,128)S(1)} all-to-all(f32[32,24,128]{2,1,0:T(8,128)S(1)} %get-tuple-element.11), channel_id=1, replica_groups=mesh['xl'=2,'z'=8,'yh'=4,'yl'=2,'xh'=2,'c'=2] {'z','yh'}, dimensions={0} | all-to-all | bytes 786432 | tf_op jit(solution)/shard_map/all_to_all | solution.py:233
  139.9 1.6 %shard_map.63 = f32[4,6,2,64]{3,2,1,0:T(2,128)} custom-call(s32[4]{0:T(128)S(1)} %get-tuple-element.32.at_ref, f32[32,24,128]{2,1,0:T(8,128)S(1)} %all_to_all.20.came_ref), custom_call_target="tpu_custom_call" | custom-call | tf_op jit(solution)/shard_map/pallas_call | solution.py:235
  (49 shorter events, 3.3 us)
Async XLA Ops:
  2.0 11.6 %all-to-all-start = ((bf16[16,8,256]{2,1,0:T(8,128)(2,1)}), bf16[16,8,256]{2,1,0:T(8,128)(2,1)S(1)}, u32[]{:S(2)}, u32[]{:S(2)}) async-start(bf16[16,8,256]{2,1,0:T(8,128)(2,1)} %bitcast.29), calls=%async_computation | async-start | bytes 131072 | tf_op jit(solution)/shard_map/all_to_all | solution.py:182
  14.9 15.3 %copy-start.2 = (bf16[4,6,2,16,256]{4,3,2,1,0:T(8,128)(2,1)S(1)}, bf16[4,6,2,16,256]{4,3,2,1,0:T(8,128)(2,1)}, u32[]{:S(2)}) copy-start(bf16[4,6,2,16,256]{4,3,2,1,0:T(8,128)(2,1)} %param.5) | copy-start | bytes 1179652
  14.9 15.3 %copy-start.3 = (bf16[4,6,2,16,256]{4,3,2,1,0:T(8,128)(2,1)S(1)}, bf16[4,6,2,16,256]{4,3,2,1,0:T(8,128)(2,1)}, u32[]{:S(2)}) copy-start(bf16[4,6,2,16,256]{4,3,2,1,0:T(8,128)(2,1)} %param.4) | copy-start | bytes 1179652
  14.9 52.4 %all-to-all-start.1 = ((bf16[32,2,2,8,640]{4,3,2,1,0:T(8,128)(2,1)}), bf16[32,2,2,8,640]{4,3,2,1,0:T(8,128)(2,1)S(1)}, u32[]{:S(2)}, u32[]{:S(2)}) async-start(bf16[32,2,2,8,640]{4,3,2,1,0:T(8,128)(2,1)} %broadcast_in_dim.12), calls=%async_computation.1 | async-start | bytes 2621440 | tf_op jit(solution)/shard_map/all_to_all | solution.py:190
  30.3 39.3 %collective-permute-start = (bf16[2,4,3,2,16,256]{5,4,3,2,1,0:T(8,128)(2,1)S(1)}, bf16[2,4,3,2,16,256]{5,4,3,2,1,0:T(8,128)(2,1)S(1)}, u32[]{:S(2)}, u32[]{:S(2)}) collective-permute-start(bf16[2,4,3,2,16,256]{5,4,3,2,1,0:T(8,128)(2,1)S(1)} %pad_maximum_fusion), channel_id=1, source_target_pairs={{0,1},{1,0},{2,3},{3,2},{4,5},{5,4},{6,7},{7,6},{8,9},{9,8},{10,11... | collective-permute-start | bytes 1179656 | tf_op jit(solution)/shard_map/ppermute | solution.py:200
  67.4 9.8 %copy-start.1 = (bf16[2,32,2,8,640]{4,3,2,1,0:T(8,128)(2,1)}, bf16[2,32,2,8,640]{4,3,2,1,0:T(8,128)(2,1)S(1)}, u32[]{:S(2)}) copy-start(bf16[2,32,2,8,640]{4,3,2,1,0:T(8,128)(2,1)S(1)} %copy.6) | copy-start | bytes 3932164
  67.4 2.3 %copy-start.12 = (bf16[1,3,2,16,256]{4,3,2,1,0:T(8,128)(2,1)S(1)}, bf16[1,3,2,16,256]{4,3,2,1,0:T(8,128)(2,1)}, u32[]{:S(2)}) copy-start(bf16[1,3,2,16,256]{4,3,2,1,0:T(8,128)(2,1)} %get-tuple-element.20) | copy-start | bytes 147460
  67.5 2.3 %copy-start.13 = (bf16[1,3,2,16,256]{4,3,2,1,0:T(8,128)(2,1)S(1)}, bf16[1,3,2,16,256]{4,3,2,1,0:T(8,128)(2,1)}, u32[]{:S(2)}) copy-start(bf16[1,3,2,16,256]{4,3,2,1,0:T(8,128)(2,1)} %get-tuple-element.38) | copy-start | bytes 147460
  67.5 7.7 %copy-start.10 = (bf16[1,3,2,16,256]{4,3,2,1,0:T(8,128)(2,1)S(1)}, bf16[1,3,2,16,256]{4,3,2,1,0:T(8,128)(2,1)}, u32[]{:S(2)}) copy-start(bf16[1,3,2,16,256]{4,3,2,1,0:T(8,128)(2,1)} %get-tuple-element.19) | copy-start | bytes 147460
  67.5 7.7 %copy-start.11 = (bf16[1,3,2,16,256]{4,3,2,1,0:T(8,128)(2,1)S(1)}, bf16[1,3,2,16,256]{4,3,2,1,0:T(8,128)(2,1)}, u32[]{:S(2)}) copy-start(bf16[1,3,2,16,256]{4,3,2,1,0:T(8,128)(2,1)} %get-tuple-element.39) | copy-start | bytes 147460
  67.5 9.7 %copy-start.8 = (bf16[1,3,2,16,256]{4,3,2,1,0:T(8,128)(2,1)S(1)}, bf16[1,3,2,16,256]{4,3,2,1,0:T(8,128)(2,1)}, u32[]{:S(2)}) copy-start(bf16[1,3,2,16,256]{4,3,2,1,0:T(8,128)(2,1)} %get-tuple-element.18) | copy-start | bytes 147460
  67.5 9.7 %copy-start.9 = (bf16[1,3,2,16,256]{4,3,2,1,0:T(8,128)(2,1)S(1)}, bf16[1,3,2,16,256]{4,3,2,1,0:T(8,128)(2,1)}, u32[]{:S(2)}) copy-start(bf16[1,3,2,16,256]{4,3,2,1,0:T(8,128)(2,1)} %get-tuple-element.40) | copy-start | bytes 147460
  67.5 26.4 %collective-permute-start.4 = (bf16[1024,640]{1,0:T(8,128)(2,1)S(1)}, bf16[1024,640]{1,0:T(8,128)(2,1)S(1)}, u32[]{:S(2)}, u32[]{:S(2)}) collective-permute-start(bf16[1024,640]{1,0:T(8,128)(2,1)S(1)} %bitcast.56), channel_id=1, source_target_pairs={{0,1},{1,0},{2,3},{3,2},{4,5},{5,4},{6,7},{7,6},{8,9},{9,8},{10,11... | collective-permute-start | bytes 3932168 | tf_op jit(solution)/shard_map/ppermute | solution.py:192
  69.6 10.7 %copy-start.7 = (bf16[1,3,2,16,256]{4,3,2,1,0:T(8,128)(2,1)S(1)}, bf16[1,3,2,16,256]{4,3,2,1,0:T(8,128)(2,1)}, u32[]{:S(2)}) copy-start(bf16[1,3,2,16,256]{4,3,2,1,0:T(8,128)(2,1)} %get-tuple-element.37) | copy-start | bytes 147460
  69.8 11.3 %collective-permute-start.1 = (bf16[2,2,3,2,16,256]{5,4,3,2,1,0:T(8,128)(2,1)S(1)}, bf16[2,2,3,2,16,256]{5,4,3,2,1,0:T(8,128)(2,1)S(1)}, u32[]{:S(2)}, u32[]{:S(2)}) collective-permute-start(bf16[2,2,3,2,16,256]{5,4,3,2,1,0:T(8,128)(2,1)S(1)} %bitcast.66), channel_id=1, source_target_pairs={{0,2},{2,0},{256,258},{258,256},{1,3},{3,1},{257,259},{259,257},{4... | collective-permute-start | bytes 589832 | tf_op jit(solution)/shard_map/ppermute | solution.py:209
  75.2 9.0 %collective-permute-start.2 = (bf16[2,2,3,2,16,256]{5,4,3,2,1,0:T(8,128)(2,1)S(1)}, bf16[2,2,3,2,16,256]{5,4,3,2,1,0:T(8,128)(2,1)S(1)}, u32[]{:S(2)}, u32[]{:S(2)}) collective-permute-start(bf16[2,2,3,2,16,256]{5,4,3,2,1,0:T(8,128)(2,1)S(1)} %bitcast.67), channel_id=1, source_target_pairs={{0,256},{2,258},{256,0},{258,2},{1,257},{3,259},{257,1},{259,3},{4... | collective-permute-start | bytes 589832 | tf_op jit(solution)/shard_map/ppermute | solution.py:209
  77.2 10.1 %collective-permute-start.3 = (bf16[2,2,3,2,16,256]{5,4,3,2,1,0:T(8,128)(2,1)S(1)}, bf16[2,2,3,2,16,256]{5,4,3,2,1,0:T(8,128)(2,1)S(1)}, u32[]{:S(2)}, u32[]{:S(2)}) collective-permute-start(bf16[2,2,3,2,16,256]{5,4,3,2,1,0:T(8,128)(2,1)S(1)} %bitcast.68), channel_id=1, source_target_pairs={{0,258},{2,256},{256,2},{258,0},{1,259},{3,257},{257,3},{259,1},{4... | collective-permute-start | bytes 589832 | tf_op jit(solution)/shard_map/ppermute | solution.py:209
  81.0 6.3 %copy-start.4 = (bf16[2,2,3,2,16,256]{5,4,3,2,1,0:T(8,128)(2,1)}, bf16[2,2,3,2,16,256]{5,4,3,2,1,0:T(8,128)(2,1)S(1)}, u32[]{:S(2)}) copy-start(bf16[2,2,3,2,16,256]{5,4,3,2,1,0:T(8,128)(2,1)S(1)} %collective-permute-done.1.refs_1_) | copy-start | bytes 589828
  84.2 3.2 %copy-start.5 = (bf16[2,2,3,2,16,256]{5,4,3,2,1,0:T(8,128)(2,1)}, bf16[2,2,3,2,16,256]{5,4,3,2,1,0:T(8,128)(2,1)S(1)}, u32[]{:S(2)}) copy-start(bf16[2,2,3,2,16,256]{5,4,3,2,1,0:T(8,128)(2,1)S(1)} %collective-permute-done.2.refs_2_) | copy-start | bytes 589828
  87.4 0.7 copy-start.6
  94.0 1.1 copy-start
  99.5 9.6 %all-to-all-start.2 = ((f32[16,6,128]{2,1,0:T(8,128)}), f32[16,6,128]{2,1,0:T(8,128)S(1)}, u32[]{:S(2)}, u32[]{:S(2)}) async-start(f32[16,6,128]{2,1,0:T(8,128)} %shard_map.61), calls=%async_computation.2 | async-start | bytes 131072 | tf_op jit(solution)/shard_map/all_to_all | solution.py:214

commit v4 on v2

--- a/solution.py
+++ b/solution.py
@@ -28,7 +28,7 @@
 
 
 def assemble(at_ref, *refs):
-    pieces, (left_ref, flip_ref, val_ref) = refs[:8], refs[8:]
+    pieces, (left_ref, flip_ref, val_ref) = refs[:4], refs[4:]
     x, core = at_ref[0], at_ref[1]
     minus = jnp.where(core == 0, 1.0, -1.0).astype(BF)
     for s in range(4):
@@ -39,10 +39,10 @@
             for j in range(3):
                 row = xl * 96 + j * 32
                 whole = pl.ds(pl.multiple_of(row, 32), 32)
-                val_ref[whole, lanes] = pieces[4 + s][t, j].reshape(32, 256)
+                val_ref[whole, lanes] = pieces[s][1, t, j].reshape(32, 256)
                 for r in range(2):
                     part = pl.ds(pl.multiple_of(row + (r ^ core) * PAIR, PAIR), PAIR)
-                    piece = pieces[s][t, j, r]
+                    piece = pieces[s][0, t, j, r]
                     if r == 0:
                         piece = piece * minus
                     left_ref[part, lanes] = piece
@@ -55,7 +55,7 @@
     return pl.pallas_call(
         assemble,
         out_shape=(flat, flat, flat),
-        in_specs=[pl.BlockSpec(memory_space=pltpu.SMEM)] + [vm] * 8,
+        in_specs=[pl.BlockSpec(memory_space=pltpu.SMEM)] + [vm] * 4,
         out_specs=(vm, vm, vm),
         cost_estimate=pl.CostEstimate(flops=0, bytes_accessed=2_000_000, transcendentals=0),
     )(at, *pieces)
@@ -176,8 +176,7 @@
 def local(cond, val, screened, k_plus):
     xl, yl, core = lax.axis_index("xl"), lax.axis_index("yl"), lax.axis_index("c")
     z, yh = lax.axis_index("z"), lax.axis_index("yh")
-    row8 = ("xl", "xh", "c")
-    w = lax.all_to_all(screened.reshape(8, 8, 256), row8, 0, 0)
+    w = lax.all_to_all(screened.reshape(8, 8, 256), ("xl", "xh", "c"), 0, 0)
     w = jnp.transpose(w.reshape(2, 4, 8, 256), (0, 2, 1, 3)).reshape(2, 8, NG)
     w = jnp.concatenate([w, w[:, :, : 4 * BLK]], 2)
     cut = [
@@ -191,21 +190,21 @@
 
     x = xl * 2 + lax.axis_index("xh")
 
-    def spread(pairs):
-        slots = pairs.reshape(4, 2, 3, 2, PAIR, 256)
-        keep = lax.dynamic_index_in_dim(slots, core, 1, False)
-        given = lax.dynamic_index_in_dim(slots, 1 - core, 1, False)
-        given = lax.ppermute(given, "c", [(0, 1), (1, 0)])
-        pieces = []
-        for s in range(4):
-            both = [lax.dynamic_index_in_dim(part, x ^ s, 0, True) for part in (keep, given)]
-            piece = jnp.concatenate(both, 0)
-            if s:
-                piece = lax.ppermute(piece, ("xl", "xh"), [(i, i ^ s) for i in range(4)])
-            pieces.append(piece)
-        return pieces
-
-    pieces = spread(cond) + spread(val)
+    slots = [pairs.reshape(4, 2, 3, 2, PAIR, 256) for pairs in (cond, val)]
+    keep = [lax.dynamic_index_in_dim(part, core, 1, False) for part in slots]
+    given = [lax.dynamic_index_in_dim(part, 1 - core, 1, False) for part in slots]
+    given = jnp.stack(given, 0)
+    given = lax.ppermute(given, "c", [(0, 1), (1, 0)])
+    pieces = []
+    for s in range(4):
+        both = [
+            lax.dynamic_index_in_dim(part, x ^ s, 0, False)
+            for part in (keep[0], given[0], keep[1], given[1])
+        ]
+        piece = jnp.stack(both, 0).reshape(2, 2, 3, 2, PAIR, 256)
+        if s:
+            piece = lax.ppermute(piece, ("xl", "xh"), [(i, i ^ s) for i in range(4)])
+        pieces.append(piece)
     here_x = jnp.stack([x, core]).astype(jnp.int32)
     left, flipped, right = assembled(here_x, pieces)
     slots = contracted(left, flipped, right, own, oth)

time: 140 us -> 129 us (0.921)
  starting transfers between devices: 52 us -> 39.2 us
  waiting for transfers between devices: 41.2 us -> 46.4 us
  other arithmetic: 7.86 us -> 4.4 us
    ppermute x8 -> x4, starting transfers between devices: 24.6 us -> 11.7 us  [the longest x3 9.82 us: local(): piece = lax.ppermute(piece, ('xl', 'xh'), [(i, i ^ s) for i in range(4)])]
    concatenate x8 -> x0, other arithmetic: 3.78 us -> none  [spread(): piece = jnp.concatenate(both, 0)]
    all_to_all x1, waiting for transfers between devices: 26.7 us -> 30.4 us  [local(): w = lax.all_to_all(w, ('z', 'yh', 'yl'), 0, 0)]
    ppermute x8 -> x4, waiting for transfers between devices: 3.06 us -> 4.58 us  [the longest x3 4.57 us: local(): piece = lax.ppermute(piece, ('xl', 'xh'), [(i, i ^ s) for i in range(4)])]
  transfers between devices with their start and end apart: 12 -> 8, of which waited for: 4 -> 5; matrix products, arithmetic and copies ran while one was open for 6% -> 4% of each run, Pallas kernels for 2% -> 2%
where the time goes in v4:
time: 129 us; the launch traced here: 128 us
  waiting for transfers between devices  46.4 us (36%)
  starting transfers between devices  39.2 us (30%)
  blocking collectives  23.2 us (18%)
  Pallas kernels  11.2 us (9%)
  other arithmetic  4.4 us (3%)
  local copies, waits for them, and re-layouts  2.85 us (2%)
    all_to_all x1, waiting for transfers between devices, local(): w = lax.all_to_all(w, ('z', 'yh', 'yl'), 0, 0)  30.4 us
    all_to_all x1, blocking collectives, local(): came = lax.all_to_all(pay, ('z', 'yh'), 0, 0)  23.2 us
    all_to_all x1, starting transfers between devices, local(): w = lax.all_to_all(w, ('z', 'yh', 'yl'), 0, 0)  16.6 us
    ppermute x3, starting transfers between devices, local(): piece = lax.ppermute(piece, ('xl', 'xh'), [(i, i ^ s) for i in range(4)])  9.82 us
    all_to_all x1, waiting for transfers between devices, local(): got = lax.all_to_all(slots, ('xl', 'yl', 'xh', 'c'), 0, 0)  6.1 us
    pallas_call x1, Pallas kernels, contracted(): pl.pallas_call(contract, out_shape=jax.ShapeDtypeStruct((16, KQ, 128), F3...  5.51 us
    all_to_all x1, waiting for transfers between devices, local(): w = lax.all_to_all(screened.reshape(8, 8, 256), ('xl', 'xh', 'c'), 0, 0)  5.36 us
    ppermute x3, waiting for transfers between devices, local(): piece = lax.ppermute(piece, ('xl', 'xh'), [(i, i ^ s) for i in range(4)])  4.57 us
  transfers between devices with their start and end apart: 8, of which 5 were waited for; matrix products, arithmetic and copies ran while one was open for 4% of the time, Pallas kernels for 2%

profile of v4, /device:TPU:16, one launch (start us, length us, event | category | flops | bytes accessed | tf_op | source)
XLA Modules:
  0.0 128.2 jit_solution(14270566428982704360)
XLA Ops:
  0.6 4.3 %all-to-all-start = ((bf16[8,8,256]{2,1,0:T(8,128)(2,1)}), bf16[8,8,256]{2,1,0:T(8,128)(2,1)S(1)}, u32[]{:S(2)}, u32[]{:S(2)}) async-start(bf16[8,8,256]{2,1,0:T(8,128)(2,1)} %bitcast.68), calls=%async_computation | async-start | bytes 65536 | tf_op jit(solution)/shard_map/all_to_all | solution.py:179
  4.9 5.4 %all-to-all-done = bf16[8,8,256]{2,1,0:T(8,128)(2,1)S(1)} async-done(((bf16[8,8,256]{2,1,0:T(8,128)(2,1)}), bf16[8,8,256]{2,1,0:T(8,128)(2,1)S(1)}, u32[]{:S(2)}, u32[]{:S(2)}) %all-to-all-start) | async-done | bytes 32800 | tf_op jit(solution)/shard_map/all_to_all | solution.py:179
  10.4 1.2 broadcast_in_dim.3
  11.6 16.6 %all-to-all-start.1 = ((bf16[64,2,8,640]{3,2,1,0:T(8,128)(2,1)}), bf16[64,2,8,640]{3,2,1,0:T(8,128)(2,1)S(1)}, u32[]{:S(2)}, u32[]{:S(2)}) async-start(bf16[64,2,8,640]{3,2,1,0:T(8,128)(2,1)} %broadcast_in_dim.3), calls=%async_computation.1 | async-start | bytes 2621440 | tf_op jit(solution)/shard_map/all_to_all | solution.py:187
  28.3 1.9 %collective-permute-start = (bf16[2,4,3,2,16,256]{5,4,3,2,1,0:T(8,128)(2,1)S(1)}, bf16[2,4,3,2,16,256]{5,4,3,2,1,0:T(8,128)(2,1)S(1)}, u32[]{:S(2)}, u32[]{:S(2)}) collective-permute-start(bf16[2,4,3,2,16,256]{5,4,3,2,1,0:T(8,128)(2,1)S(1)} %pad_maximum_fusion), channel_id=1, source_target_pairs={{0,1},{1,0},{2,3},{3,2},{4,5},{5,4},{6,7},{7,6},{8,9},{9,8},{10,11... | collective-permute-start | bytes 1179656 | tf_op jit(solution)/shard_map/ppermute | solution.py:197
  30.3 0.7 dynamic-slice_bitcast_fusion.3
  31.0 1.3 %divide_reduce_fusion = (s32[4]{0:T(128)}, s32[4]{0:T(128)}) fusion(s32[4,768]{1,0:T(4,128)} %param.7), kind=kLoop, calls=%fused_computation.36 | loop fusion | flops 8 | bytes 48 | tf_op jit(solution)/shard_map/jit(floor_divide)/div | solution.py:213
  32.3 30.4 %all-to-all-done.1 = bf16[64,2,8,640]{3,2,1,0:T(8,128)(2,1)S(1)} async-done(((bf16[64,2,8,640]{3,2,1,0:T(8,128)(2,1)}), bf16[64,2,8,640]{3,2,1,0:T(8,128)(2,1)S(1)}, u32[]{:S(2)}, u32[]{:S(2)}) %all-to-all-start.1) | async-done | bytes 1310752 | tf_op jit(solution)/shard_map/all_to_all | solution.py:187
  62.9 2.1 %collective-permute-start.4 = (bf16[1024,640]{1,0:T(8,128)(2,1)S(1)}, bf16[1024,640]{1,0:T(8,128)(2,1)}, u32[]{:S(2)}, u32[]{:S(2)}) collective-permute-start(bf16[1024,640]{1,0:T(8,128)(2,1)S(1)} %bitcast.55), channel_id=1, source_target_pairs={{0,1},{1,0},{2,3},{3,2},{4,5},{5,4},{6,7},{7,6},{8,9},{9,8},{10,11... | collective-permute-start | bytes 3932168 | tf_op jit(solution)/shard_map/ppermute | solution.py:189
  65.0 0.8 fusion.1
  65.8 0.7 and_select_fusion
  66.6 3.2 %collective-permute-start.1 = (bf16[2,2,3,2,16,256]{5,4,3,2,1,0:T(8,128)(2,1)S(1)}, bf16[2,2,3,2,16,256]{5,4,3,2,1,0:T(8,128)(2,1)S(1)}, u32[]{:S(2)}, u32[]{:S(2)}) collective-permute-start(bf16[2,2,3,2,16,256]{5,4,3,2,1,0:T(8,128)(2,1)S(1)} %bitcast.65), channel_id=1, source_target_pairs={{0,2},{2,0},{256,258},{258,256},{1,3},{3,1},{257,259},{259,257},{4... | collective-permute-start | bytes 589832 | tf_op jit(solution)/shard_map/ppermute | solution.py:206
  69.9 2.7 %collective-permute-start.2 = (bf16[2,2,3,2,16,256]{5,4,3,2,1,0:T(8,128)(2,1)S(1)}, bf16[2,2,3,2,16,256]{5,4,3,2,1,0:T(8,128)(2,1)S(1)}, u32[]{:S(2)}, u32[]{:S(2)}) collective-permute-start(bf16[2,2,3,2,16,256]{5,4,3,2,1,0:T(8,128)(2,1)S(1)} %bitcast.66), channel_id=1, source_target_pairs={{0,256},{2,258},{256,0},{258,2},{1,257},{3,259},{257,1},{259,3},{4... | collective-permute-start | bytes 589832 | tf_op jit(solution)/shard_map/ppermute | solution.py:206
  72.6 4.0 %collective-permute-start.3 = (bf16[2,2,3,2,16,256]{5,4,3,2,1,0:T(8,128)(2,1)S(1)}, bf16[2,2,3,2,16,256]{5,4,3,2,1,0:T(8,128)(2,1)S(1)}, u32[]{:S(2)}, u32[]{:S(2)}) collective-permute-start(bf16[2,2,3,2,16,256]{5,4,3,2,1,0:T(8,128)(2,1)S(1)} %bitcast.67), channel_id=1, source_target_pairs={{0,258},{2,256},{256,2},{258,0},{1,259},{3,257},{257,3},{259,1},{4... | collective-permute-start | bytes 589832 | tf_op jit(solution)/shard_map/ppermute | solution.py:206
  77.2 0.7 pad_maximum_fusion.1
  77.9 2.2 %collective-permute-done.2.refs_2_ = bf16[2,2,3,2,16,256]{5,4,3,2,1,0:T(8,128)(2,1)S(1)} collective-permute-done((bf16[2,2,3,2,16,256]{5,4,3,2,1,0:T(8,128)(2,1)S(1)}, bf16[2,2,3,2,16,256]{5,4,3,2,1,0:T(8,128)(2,1)S(1)}, u32[]{:S(2)}, u32[]{:S(2)}) %collective-permute-start.2) | collective-permute-done | bytes 196640 | tf_op jit(solution)/shard_map/ppermute | solution.py:206
  80.0 2.4 %collective-permute-done.3.refs_3_ = bf16[2,2,3,2,16,256]{5,4,3,2,1,0:T(8,128)(2,1)S(1)} collective-permute-done((bf16[2,2,3,2,16,256]{5,4,3,2,1,0:T(8,128)(2,1)S(1)}, bf16[2,2,3,2,16,256]{5,4,3,2,1,0:T(8,128)(2,1)S(1)}, u32[]{:S(2)}, u32[]{:S(2)}) %collective-permute-start.3) | collective-permute-done | bytes 196640 | tf_op jit(solution)/shard_map/ppermute | solution.py:206
  83.1 2.5 %shard_map.59 = (bf16[192,1024]{1,0:T(8,128)(2,1)}, bf16[192,1024]{1,0:T(8,128)(2,1)}, bf16[192,1024]{1,0:T(8,128)(2,1)}) custom-call(s32[2]{0:T(128)} %pad_add_fusion.1.at_ref, bf16[2,2,3,2,16,256]{5,4,3,2,1,0:T(8,128)(2,1)} %bitcast.57, bf16[2,2,3,2,16,256]{5,4,3,2,1,0:T(8,128)(2,1)} %copy-done.3, bf16[2,2,3,2,16,256]{5,4,3,2,1,0:T(8,128)(2,1)} %copy-done.4, ...), custom_call_target="tpu_custom_call" | custom-call | bytes 2000000 | tf_op jit(solution)/shard_map/pallas_call | solution.py:55
  85.6 5.5 %shard_map.60 = f32[16,6,128]{2,1,0:T(8,128)} custom-call(bf16[192,1024]{1,0:T(8,128)(2,1)} %get-tuple-element.7.left_ref, bf16[192,1024]{1,0:T(8,128)(2,1)} %get-tuple-element.8.flip_ref, bf16[192,1024]{1,0:T(8,128)(2,1)} %get-tuple-element.9.val_ref, bf16[1024,640]{1,0:T(8,128)(2,1)} %bitcast.56, bf16[1024,640]{1,0:T(8,128)(2,1)} %collective-permute-done.4.oth_ref), custom_call_target="tpu_custom_call" | custom-call | flops 1600000000 | bytes 4000000 | tf_op jit(solution)/shard_map/pallas_call | solution.py:126
  91.1 4.5 %all-to-all-start.2 = ((f32[16,6,128]{2,1,0:T(8,128)}), f32[16,6,128]{2,1,0:T(8,128)S(1)}, u32[]{:S(2)}, u32[]{:S(2)}) async-start(f32[16,6,128]{2,1,0:T(8,128)} %shard_map.60), calls=%async_computation.2 | async-start | bytes 131072 | tf_op jit(solution)/shard_map/all_to_all | solution.py:211
  95.7 6.1 %all-to-all-done.2.came_ref = f32[16,6,128]{2,1,0:T(8,128)S(1)} async-done(((f32[16,6,128]{2,1,0:T(8,128)}), f32[16,6,128]{2,1,0:T(8,128)S(1)}, u32[]{:S(2)}, u32[]{:S(2)}) %all-to-all-start.2) | async-done | bytes 49184 | tf_op jit(solution)/shard_map/all_to_all | solution.py:211
  101.8 1.6 %shard_map.61 = (f32[4,6,2,64]{3,2,1,0:T(2,128)}, f32[32,24,128]{2,1,0:T(8,128)S(1)}) custom-call(s32[10]{0:T(128)S(1)} %pad_add_fusion.at_ref, f32[16,6,128]{2,1,0:T(8,128)S(1)} %all-to-all-done.2.came_ref), custom_call_target="tpu_custom_call" | custom-call | tf_op jit(solution)/shard_map/pallas_call | solution.py:222
  103.4 23.2 %all_to_all.20.came_ref = f32[32,24,128]{2,1,0:T(8,128)S(1)} all-to-all(f32[32,24,128]{2,1,0:T(8,128)S(1)} %get-tuple-element.11), channel_id=1, replica_groups=mesh['xl'=2,'z'=8,'yh'=4,'yl'=2,'xh'=2,'c'=2] {'z','yh'}, dimensions={0} | all-to-all | bytes 786432 | tf_op jit(solution)/shard_map/all_to_all | solution.py:230
  126.6 1.6 %shard_map.62 = f32[4,6,2,64]{3,2,1,0:T(2,128)} custom-call(s32[4]{0:T(128)S(1)} %get-tuple-element.32.at_ref, f32[32,24,128]{2,1,0:T(8,128)S(1)} %all_to_all.20.came_ref), custom_call_target="tpu_custom_call" | custom-call | tf_op jit(solution)/shard_map/pallas_call | solution.py:232
  (41 shorter events, 1.8 us)
Async XLA Ops:
  0.6 9.7 %all-to-all-start = ((bf16[8,8,256]{2,1,0:T(8,128)(2,1)}), bf16[8,8,256]{2,1,0:T(8,128)(2,1)S(1)}, u32[]{:S(2)}, u32[]{:S(2)}) async-start(bf16[8,8,256]{2,1,0:T(8,128)(2,1)} %bitcast.68), calls=%async_computation | async-start | bytes 65536 | tf_op jit(solution)/shard_map/all_to_all | solution.py:179
  11.6 16.6 %copy-start.1 = (bf16[4,6,2,16,256]{4,3,2,1,0:T(8,128)(2,1)S(1)}, bf16[4,6,2,16,256]{4,3,2,1,0:T(8,128)(2,1)}, u32[]{:S(2)}) copy-start(bf16[4,6,2,16,256]{4,3,2,1,0:T(8,128)(2,1)} %param.5) | copy-start | bytes 1179652
  11.6 16.6 %copy-start.2 = (bf16[4,6,2,16,256]{4,3,2,1,0:T(8,128)(2,1)S(1)}, bf16[4,6,2,16,256]{4,3,2,1,0:T(8,128)(2,1)}, u32[]{:S(2)}) copy-start(bf16[4,6,2,16,256]{4,3,2,1,0:T(8,128)(2,1)} %param.4) | copy-start | bytes 1179652
  11.6 51.1 %all-to-all-start.1 = ((bf16[64,2,8,640]{3,2,1,0:T(8,128)(2,1)}), bf16[64,2,8,640]{3,2,1,0:T(8,128)(2,1)S(1)}, u32[]{:S(2)}, u32[]{:S(2)}) async-start(bf16[64,2,8,640]{3,2,1,0:T(8,128)(2,1)} %broadcast_in_dim.3), calls=%async_computation.1 | async-start | bytes 2621440 | tf_op jit(solution)/shard_map/all_to_all | solution.py:187
  28.3 38.2 %collective-permute-start = (bf16[2,4,3,2,16,256]{5,4,3,2,1,0:T(8,128)(2,1)S(1)}, bf16[2,4,3,2,16,256]{5,4,3,2,1,0:T(8,128)(2,1)S(1)}, u32[]{:S(2)}, u32[]{:S(2)}) collective-permute-start(bf16[2,4,3,2,16,256]{5,4,3,2,1,0:T(8,128)(2,1)S(1)} %pad_maximum_fusion), channel_id=1, source_target_pairs={{0,1},{1,0},{2,3},{3,2},{4,5},{5,4},{6,7},{7,6},{8,9},{9,8},{10,11... | collective-permute-start | bytes 1179656 | tf_op jit(solution)/shard_map/ppermute | solution.py:197
  62.8 9.8 %copy-start = (bf16[2,64,8,640]{3,2,1,0:T(8,128)(2,1)}, bf16[2,64,8,640]{3,2,1,0:T(8,128)(2,1)S(1)}, u32[]{:S(2)}) copy-start(bf16[2,64,8,640]{3,2,1,0:T(8,128)(2,1)S(1)} %copy.6) | copy-start | bytes 3932164
  62.8 3.7 %copy-start.9 = (bf16[1,3,2,16,256]{4,3,2,1,0:T(8,128)(2,1)S(1)}, bf16[1,3,2,16,256]{4,3,2,1,0:T(8,128)(2,1)}, u32[]{:S(2)}) copy-start(bf16[1,3,2,16,256]{4,3,2,1,0:T(8,128)(2,1)} %get-tuple-element.20) | copy-start | bytes 147460
  62.9 3.7 %copy-start.10 = (bf16[1,3,2,16,256]{4,3,2,1,0:T(8,128)(2,1)S(1)}, bf16[1,3,2,16,256]{4,3,2,1,0:T(8,128)(2,1)}, u32[]{:S(2)}) copy-start(bf16[1,3,2,16,256]{4,3,2,1,0:T(8,128)(2,1)} %get-tuple-element.38) | copy-start | bytes 147460
  62.9 6.9 %copy-start.7 = (bf16[1,3,2,16,256]{4,3,2,1,0:T(8,128)(2,1)S(1)}, bf16[1,3,2,16,256]{4,3,2,1,0:T(8,128)(2,1)}, u32[]{:S(2)}) copy-start(bf16[1,3,2,16,256]{4,3,2,1,0:T(8,128)(2,1)} %get-tuple-element.19) | copy-start | bytes 147460
  62.9 6.9 %copy-start.8 = (bf16[1,3,2,16,256]{4,3,2,1,0:T(8,128)(2,1)S(1)}, bf16[1,3,2,16,256]{4,3,2,1,0:T(8,128)(2,1)}, u32[]{:S(2)}) copy-start(bf16[1,3,2,16,256]{4,3,2,1,0:T(8,128)(2,1)} %get-tuple-element.39) | copy-start | bytes 147460
  62.9 9.7 %copy-start.6 = (bf16[1,3,2,16,256]{4,3,2,1,0:T(8,128)(2,1)S(1)}, bf16[1,3,2,16,256]{4,3,2,1,0:T(8,128)(2,1)}, u32[]{:S(2)}) copy-start(bf16[1,3,2,16,256]{4,3,2,1,0:T(8,128)(2,1)} %get-tuple-element.40) | copy-start | bytes 147460
  62.9 22.7 %collective-permute-start.4 = (bf16[1024,640]{1,0:T(8,128)(2,1)S(1)}, bf16[1024,640]{1,0:T(8,128)(2,1)}, u32[]{:S(2)}, u32[]{:S(2)}) collective-permute-start(bf16[1024,640]{1,0:T(8,128)(2,1)S(1)} %bitcast.55), channel_id=1, source_target_pairs={{0,1},{1,0},{2,3},{3,2},{4,5},{5,4},{6,7},{7,6},{8,9},{9,8},{10,11... | collective-permute-start | bytes 3932168 | tf_op jit(solution)/shard_map/ppermute | solution.py:189
  66.6 11.2 %collective-permute-start.1 = (bf16[2,2,3,2,16,256]{5,4,3,2,1,0:T(8,128)(2,1)S(1)}, bf16[2,2,3,2,16,256]{5,4,3,2,1,0:T(8,128)(2,1)S(1)}, u32[]{:S(2)}, u32[]{:S(2)}) collective-permute-start(bf16[2,2,3,2,16,256]{5,4,3,2,1,0:T(8,128)(2,1)S(1)} %bitcast.65), channel_id=1, source_target_pairs={{0,2},{2,0},{256,258},{258,256},{1,3},{3,1},{257,259},{259,257},{4... | collective-permute-start | bytes 589832 | tf_op jit(solution)/shard_map/ppermute | solution.py:206
  69.9 10.2 %collective-permute-start.2 = (bf16[2,2,3,2,16,256]{5,4,3,2,1,0:T(8,128)(2,1)S(1)}, bf16[2,2,3,2,16,256]{5,4,3,2,1,0:T(8,128)(2,1)S(1)}, u32[]{:S(2)}, u32[]{:S(2)}) collective-permute-start(bf16[2,2,3,2,16,256]{5,4,3,2,1,0:T(8,128)(2,1)S(1)} %bitcast.66), channel_id=1, source_target_pairs={{0,256},{2,258},{256,0},{258,2},{1,257},{3,259},{257,1},{259,3},{4... | collective-permute-start | bytes 589832 | tf_op jit(solution)/shard_map/ppermute | solution.py:206
  72.6 9.8 %collective-permute-start.3 = (bf16[2,2,3,2,16,256]{5,4,3,2,1,0:T(8,128)(2,1)S(1)}, bf16[2,2,3,2,16,256]{5,4,3,2,1,0:T(8,128)(2,1)S(1)}, u32[]{:S(2)}, u32[]{:S(2)}) collective-permute-start(bf16[2,2,3,2,16,256]{5,4,3,2,1,0:T(8,128)(2,1)S(1)} %bitcast.67), channel_id=1, source_target_pairs={{0,258},{2,256},{256,2},{258,0},{1,259},{3,257},{257,3},{259,1},{4... | collective-permute-start | bytes 589832 | tf_op jit(solution)/shard_map/ppermute | solution.py:206
  77.9 4.6 %copy-start.3 = (bf16[2,2,3,2,16,256]{5,4,3,2,1,0:T(8,128)(2,1)}, bf16[2,2,3,2,16,256]{5,4,3,2,1,0:T(8,128)(2,1)S(1)}, u32[]{:S(2)}) copy-start(bf16[2,2,3,2,16,256]{5,4,3,2,1,0:T(8,128)(2,1)S(1)} %collective-permute-done.1.refs_1_) | copy-start | bytes 589828
  80.0 2.4 %copy-start.4 = (bf16[2,2,3,2,16,256]{5,4,3,2,1,0:T(8,128)(2,1)}, bf16[2,2,3,2,16,256]{5,4,3,2,1,0:T(8,128)(2,1)S(1)}, u32[]{:S(2)}) copy-start(bf16[2,2,3,2,16,256]{5,4,3,2,1,0:T(8,128)(2,1)S(1)} %collective-permute-done.2.refs_2_) | copy-start | bytes 589828
  82.4 0.7 copy-start.5
  91.1 10.7 %all-to-all-start.2 = ((f32[16,6,128]{2,1,0:T(8,128)}), f32[16,6,128]{2,1,0:T(8,128)S(1)}, u32[]{:S(2)}, u32[]{:S(2)}) async-start(f32[16,6,128]{2,1,0:T(8,128)} %shard_map.60), calls=%async_computation.2 | async-start | bytes 131072 | tf_op jit(solution)/shard_map/all_to_all | solution.py:211

commit v5 on v4

--- a/solution.py
+++ b/solution.py
@@ -61,33 +61,53 @@
     )(at, *pieces)
 
 
-def contract(left_ref, flip_ref, val_ref, own_ref, oth_ref, out_ref, p_ref, q_ref):
+def contract(left_in, flip_in, val_in, own_in, oth_in, out_ref, *scratch):
+    left_ref, flip_ref, val_ref, own_ref, oth_ref, p_ref, q_ref, sem, own_sem, oth_sem = scratch
+    first = [
+        pltpu.make_async_copy(left_in, left_ref, sem.at[0]),
+        pltpu.make_async_copy(flip_in, flip_ref, sem.at[1]),
+    ]
+    last = pltpu.make_async_copy(val_in, val_ref, sem.at[2])
+
+    def chunks(source, target, sems):
+        return [
+            pltpu.make_async_copy(
+                source.at[pl.ds(i * BLK, BLK), :], target.at[pl.ds(i * BLK, BLK), :], sems.at[i]
+            )
+            for i in range(4)
+        ]
+
+    own_copies = chunks(own_in, own_ref, own_sem)
+    oth_copies = chunks(oth_in, oth_ref, oth_sem)
+    for copy in first + own_copies + oth_copies + [last]:
+        copy.start()
+    for copy in first:
+        copy.wait()
     left = left_ref[...]
     flipped = flip_ref[...]
     rows = left.shape[0]
-    wrapped = jnp.concatenate([left, left[:, : 3 * BLK]], 1)
-    wrapped_flip = jnp.concatenate([flipped, flipped[:, : 3 * BLK]], 1)
-    for b in range(NB):
-        lo, hi = b * BLK, (b + 1) * BLK
-        far = wrapped[:, hi : hi + 3 * BLK]
-        far_flip = wrapped_flip[:, hi : hi + 3 * BLK]
-        own = own_ref[lo:hi, :]
-        oth = oth_ref[lo:hi, :]
-        p_back = nt(far_flip, own[:, BLK : 4 * BLK])
-        q_back = -nt(far, oth[:, BLK : 4 * BLK])
-        if b == 0:
-            p_ref[...] = jnp.zeros_like(p_ref)
-            q_ref[...] = jnp.zeros_like(q_ref)
-        p_ref[:, lo:hi] += p_back
-        q_ref[:, lo:hi] += q_back
-        p_fore = nn(left[:, lo:hi], own)
-        q_fore = nn(flipped[:, lo:hi], oth)
-        first = min(SENT, NB - b)
-        p_ref[:, lo : lo + first * BLK] += p_fore[:, : first * BLK]
-        q_ref[:, lo : lo + first * BLK] += q_fore[:, : first * BLK]
-        if first < SENT:
-            p_ref[:, : (SENT - first) * BLK] += p_fore[:, first * BLK :]
-            q_ref[:, : (SENT - first) * BLK] += q_fore[:, first * BLK :]
+
+    def screen(ahead, behind, w_ref, sum_ref, copies, negate):
+        sum_ref[...] = jnp.zeros_like(sum_ref)
+        wrapped = jnp.concatenate([behind, behind[:, : 3 * BLK]], 1)
+        for i in range(4):
+            copies[i].wait()
+            for half in range(2):
+                b = i + 4 * half
+                lo, hi = b * BLK, (b + 1) * BLK
+                sent = SENT - half
+                w = w_ref[i * BLK : (i + 1) * BLK, half * SENT * BLK : (half + 1) * SENT * BLK - half * BLK]
+                back = nt(wrapped[:, hi : hi + (sent - 1) * BLK], w[:, BLK:])
+                sum_ref[:, lo:hi] += -back if negate else back
+                fore = nn(ahead[:, lo:hi], w)
+                direct = min(sent, NB - b)
+                sum_ref[:, lo : lo + direct * BLK] += fore[:, : direct * BLK]
+                if direct < sent:
+                    sum_ref[:, : (sent - direct) * BLK] += fore[:, direct * BLK :]
+
+    screen(left, flipped, own_ref, p_ref, own_copies, False)
+    screen(flipped, left, oth_ref, q_ref, oth_copies, True)
+    last.wait()
     p = p_ref[...].reshape(KQ, 2, PAIR, NG)
     q = q_ref[...].reshape(KQ, 2, PAIR, NG)
     half = rows // 2
@@ -122,16 +142,18 @@
 
 
 def contracted(left, flipped, val, own, oth):
-    vm = pl.BlockSpec(memory_space=pltpu.VMEM)
+    sums = (2 * KQ * PAIR, NG)
+    sent = (NG // 2, (2 * SENT - 1) * BLK)
     return pl.pallas_call(
         contract,
         out_shape=jax.ShapeDtypeStruct((16, KQ, 128), F32),
-        in_specs=[vm] * 5,
-        out_specs=vm,
-        scratch_shapes=[
-            pltpu.VMEM((2 * KQ * PAIR, NG), F32),
-            pltpu.VMEM((2 * KQ * PAIR, NG), F32),
-        ],
+        in_specs=[pl.BlockSpec(memory_space=pl.ANY)] * 5,
+        out_specs=pl.BlockSpec(memory_space=pltpu.VMEM),
+        scratch_shapes=[pltpu.VMEM(sums, BF)] * 3
+        + [pltpu.VMEM(sent, BF)] * 2
+        + [pltpu.VMEM(sums, F32)] * 2
+        + [pltpu.SemaphoreType.DMA((3,)), pltpu.SemaphoreType.DMA((4,)), pltpu.SemaphoreType.DMA((4,))],
+        compiler_params=pltpu.CompilerParams(vmem_limit_bytes=32 << 20),
         cost_estimate=pl.CostEstimate(
             flops=1_600_000_000, bytes_accessed=4_000_000, transcendentals=0
         ),
@@ -180,12 +202,13 @@
     w = jnp.transpose(w.reshape(2, 4, 8, 256), (0, 2, 1, 3)).reshape(2, 8, NG)
     w = jnp.concatenate([w, w[:, :, : 4 * BLK]], 2)
     cut = [
-        lax.dynamic_slice_in_dim(w[i], (4 * i + z // 2) * BLK, SENT * BLK, 1) for i in range(2)
+        lax.dynamic_slice_in_dim(w[i], (4 * i + z // 2) * BLK, (SENT - i) * BLK, 1)
+        for i in range(2)
     ]
-    w = jnp.stack(cut, 0)
+    w = jnp.concatenate(cut, 1)
     w = jnp.broadcast_to(w, (64,) + w.shape)
     w = lax.all_to_all(w, ("z", "yh", "yl"), 0, 0)
-    own = jnp.transpose(w, (1, 0, 2, 3)).reshape(NG, SENT * BLK)
+    own = w.reshape(NG // 2, (2 * SENT - 1) * BLK)
     oth = lax.ppermute(own, "c", [(0, 1), (1, 0)])
 
     x = xl * 2 + lax.axis_index("xh")

time: 129 us -> 129 us (level)
  local copies, waits for them, and re-layouts: 2.85 us -> 5.86 us
  waiting for transfers between devices: 46.4 us -> 43.6 us
    unnamed x22 -> x16, local copies, waits for them, and re-layouts: 0.71 us -> 3.7 us
    all_to_all x1, waiting for transfers between devices: 30.4 us -> 27.5 us  [local(): w = lax.all_to_all(w, ('z', 'yh', 'yl'), 0, 0)]
where the time goes in v5:
time: 129 us; the launch traced here: 128 us
  waiting for transfers between devices  43.6 us (34%)
  starting transfers between devices  39.1 us (30%)
  blocking collectives  23.1 us (18%)
  Pallas kernels  11.5 us (9%)
  local copies, waits for them, and re-layouts  5.86 us (5%)
  other arithmetic  4.39 us (3%)
    all_to_all x1, waiting for transfers between devices, local(): w = lax.all_to_all(w, ('z', 'yh', 'yl'), 0, 0)  27.5 us
    all_to_all x1, blocking collectives, local(): came = lax.all_to_all(pay, ('z', 'yh'), 0, 0)  23.1 us
    all_to_all x1, starting transfers between devices, local(): w = lax.all_to_all(w, ('z', 'yh', 'yl'), 0, 0)  16.6 us
    ppermute x3, starting transfers between devices, local(): piece = lax.ppermute(piece, ('xl', 'xh'), [(i, i ^ s) for i in range(4)])  9.82 us
    all_to_all x1, waiting for transfers between devices, local(): got = lax.all_to_all(slots, ('xl', 'yl', 'xh', 'c'), 0, 0)  6.1 us
    pallas_call x1, Pallas kernels, contracted(): pl.pallas_call(contract, out_shape=jax.ShapeDtypeStruct((16, KQ, 128), F3...  5.84 us
    all_to_all x1, waiting for transfers between devices, local(): w = lax.all_to_all(screened.reshape(8, 8, 256), ('xl', 'xh', 'c'), 0, 0)  5.36 us
    ppermute x3, waiting for transfers between devices, local(): piece = lax.ppermute(piece, ('xl', 'xh'), [(i, i ^ s) for i in range(4)])  4.58 us
  transfers between devices with their start and end apart: 8, of which 5 were waited for; matrix products, arithmetic and copies ran while one was open for 4% of the time, Pallas kernels for 2%

profile of v5, /device:TPU:16, one launch (start us, length us, event | category | flops | bytes accessed | tf_op | source)
XLA Modules:
  0.0 128.5 jit_solution(14042032105056559324)
XLA Ops:
  0.6 4.3 %all-to-all-start = ((bf16[8,8,256]{2,1,0:T(8,128)(2,1)}), bf16[8,8,256]{2,1,0:T(8,128)(2,1)S(1)}, u32[]{:S(2)}, u32[]{:S(2)}) async-start(bf16[8,8,256]{2,1,0:T(8,128)(2,1)} %bitcast.70), calls=%async_computation | async-start | bytes 65536 | tf_op jit(solution)/shard_map/all_to_all | solution.py:201
  4.9 5.4 %all-to-all-done = bf16[8,8,256]{2,1,0:T(8,128)(2,1)S(1)} async-done(((bf16[8,8,256]{2,1,0:T(8,128)(2,1)}), bf16[8,8,256]{2,1,0:T(8,128)(2,1)S(1)}, u32[]{:S(2)}, u32[]{:S(2)}) %all-to-all-start) | async-done | bytes 32800 | tf_op jit(solution)/shard_map/all_to_all | solution.py:201
  10.4 1.1 broadcast_in_dim.3
  11.5 16.6 %all-to-all-start.1 = ((bf16[64,8,1152]{2,1,0:T(8,128)(2,1)}), bf16[64,8,1152]{2,1,0:T(8,128)(2,1)S(1)}, u32[]{:S(2)}, u32[]{:S(2)}) async-start(bf16[64,8,1152]{2,1,0:T(8,128)(2,1)} %broadcast_in_dim.3), calls=%async_computation.1 | async-start | bytes 2359296 | tf_op jit(solution)/shard_map/all_to_all | solution.py:210
  28.2 1.9 %collective-permute-start = (bf16[2,4,3,2,16,256]{5,4,3,2,1,0:T(8,128)(2,1)S(1)}, bf16[2,4,3,2,16,256]{5,4,3,2,1,0:T(8,128)(2,1)S(1)}, u32[]{:S(2)}, u32[]{:S(2)}) collective-permute-start(bf16[2,4,3,2,16,256]{5,4,3,2,1,0:T(8,128)(2,1)S(1)} %pad_maximum_fusion), channel_id=1, source_target_pairs={{0,1},{1,0},{2,3},{3,2},{4,5},{5,4},{6,7},{7,6},{8,9},{9,8},{10,11... | collective-permute-start | bytes 1179656 | tf_op jit(solution)/shard_map/ppermute | solution.py:220
  30.2 1.4 %divide_reduce_fusion = (s32[4]{0:T(128)}, s32[4]{0:T(128)}) fusion(s32[4,768]{1,0:T(4,128)} %param.7), kind=kLoop, calls=%fused_computation.38 | loop fusion | flops 8 | bytes 48 | tf_op jit(solution)/shard_map/jit(floor_divide)/div | solution.py:236
  32.3 27.5 %all-to-all-done.1 = bf16[64,8,1152]{2,1,0:T(8,128)(2,1)S(1)} async-done(((bf16[64,8,1152]{2,1,0:T(8,128)(2,1)}), bf16[64,8,1152]{2,1,0:T(8,128)(2,1)S(1)}, u32[]{:S(2)}, u32[]{:S(2)}) %all-to-all-start.1) | async-done | bytes 1179680 | tf_op jit(solution)/shard_map/all_to_all | solution.py:210
  59.9 1.9 %collective-permute-start.4 = (bf16[512,1152]{1,0:T(8,128)(2,1)S(1)}, bf16[512,1152]{1,0:T(8,128)(2,1)S(1)}, u32[]{:S(2)}, u32[]{:S(2)}) collective-permute-start(bf16[512,1152]{1,0:T(8,128)(2,1)S(1)} %bitcast.57), channel_id=1, source_target_pairs={{0,1},{1,0},{2,3},{3,2},{4,5},{5,4},{6,7},{7,6},{8,9},{9,8},{10,11... | collective-permute-start | bytes 3538952 | tf_op jit(solution)/shard_map/ppermute | solution.py:212
  62.5 0.9 dynamic-slice_bitcast_fusion.3
  63.6 3.2 %collective-permute-start.1 = (bf16[2,2,3,2,16,256]{5,4,3,2,1,0:T(8,128)(2,1)S(1)}, bf16[2,2,3,2,16,256]{5,4,3,2,1,0:T(8,128)(2,1)S(1)}, u32[]{:S(2)}, u32[]{:S(2)}) collective-permute-start(bf16[2,2,3,2,16,256]{5,4,3,2,1,0:T(8,128)(2,1)S(1)} %bitcast.67), channel_id=1, source_target_pairs={{0,2},{2,0},{256,258},{258,256},{1,3},{3,1},{257,259},{259,257},{4... | collective-permute-start | bytes 589832 | tf_op jit(solution)/shard_map/ppermute | solution.py:229
  66.8 2.7 %collective-permute-start.2 = (bf16[2,2,3,2,16,256]{5,4,3,2,1,0:T(8,128)(2,1)S(1)}, bf16[2,2,3,2,16,256]{5,4,3,2,1,0:T(8,128)(2,1)S(1)}, u32[]{:S(2)}, u32[]{:S(2)}) collective-permute-start(bf16[2,2,3,2,16,256]{5,4,3,2,1,0:T(8,128)(2,1)S(1)} %bitcast.68), channel_id=1, source_target_pairs={{0,256},{2,258},{256,0},{258,2},{1,257},{3,259},{257,1},{259,3},{4... | collective-permute-start | bytes 589832 | tf_op jit(solution)/shard_map/ppermute | solution.py:229
  69.5 4.0 %collective-permute-start.3 = (bf16[2,2,3,2,16,256]{5,4,3,2,1,0:T(8,128)(2,1)S(1)}, bf16[2,2,3,2,16,256]{5,4,3,2,1,0:T(8,128)(2,1)S(1)}, u32[]{:S(2)}, u32[]{:S(2)}) collective-permute-start(bf16[2,2,3,2,16,256]{5,4,3,2,1,0:T(8,128)(2,1)S(1)} %bitcast.69), channel_id=1, source_target_pairs={{0,258},{2,256},{256,2},{258,0},{1,259},{3,257},{257,3},{259,1},{4... | collective-permute-start | bytes 589832 | tf_op jit(solution)/shard_map/ppermute | solution.py:229
  74.8 2.2 %collective-permute-done.2.refs_2_ = bf16[2,2,3,2,16,256]{5,4,3,2,1,0:T(8,128)(2,1)S(1)} collective-permute-done((bf16[2,2,3,2,16,256]{5,4,3,2,1,0:T(8,128)(2,1)S(1)}, bf16[2,2,3,2,16,256]{5,4,3,2,1,0:T(8,128)(2,1)S(1)}, u32[]{:S(2)}, u32[]{:S(2)}) %collective-permute-start.2) | collective-permute-done | bytes 196640 | tf_op jit(solution)/shard_map/ppermute | solution.py:229
  77.0 2.4 %collective-permute-done.3.refs_3_ = bf16[2,2,3,2,16,256]{5,4,3,2,1,0:T(8,128)(2,1)S(1)} collective-permute-done((bf16[2,2,3,2,16,256]{5,4,3,2,1,0:T(8,128)(2,1)S(1)}, bf16[2,2,3,2,16,256]{5,4,3,2,1,0:T(8,128)(2,1)S(1)}, u32[]{:S(2)}, u32[]{:S(2)}) %collective-permute-start.3) | collective-permute-done | bytes 196640 | tf_op jit(solution)/shard_map/ppermute | solution.py:229
  80.1 2.5 %shard_map.59 = (bf16[192,1024]{1,0:T(8,128)(2,1)}, bf16[192,1024]{1,0:T(8,128)(2,1)}, bf16[192,1024]{1,0:T(8,128)(2,1)}) custom-call(s32[2]{0:T(128)} %pad_add_fusion.1.at_ref, bf16[2,2,3,2,16,256]{5,4,3,2,1,0:T(8,128)(2,1)} %bitcast.59, bf16[2,2,3,2,16,256]{5,4,3,2,1,0:T(8,128)(2,1)} %copy-done.5, bf16[2,2,3,2,16,256]{5,4,3,2,1,0:T(8,128)(2,1)} %copy-done.6, ...), custom_call_target="tpu_custom_call" | custom-call | bytes 2000000 | tf_op jit(solution)/shard_map/pallas_call | solution.py:55
  82.6 1.0 copy-done
  83.6 1.0 copy-done.1
  84.5 1.0 copy-done.2
  85.5 5.8 %shard_map.60 = f32[16,6,128]{2,1,0:T(8,128)} custom-call(bf16[192,1024]{1,0:T(8,128)(2,1)S(1)} %copy-done, bf16[192,1024]{1,0:T(8,128)(2,1)S(1)} %copy-done.1, bf16[192,1024]{1,0:T(8,128)(2,1)S(1)} %copy-done.2, bf16[512,1152]{1,0:T(8,128)(2,1)S(1)} %bitcast.58, bf16[512,1152]{1,0:T(8,128)(2,1)S(1)} %collective-permute-done.4.oth_in), custom_call_target="tpu_custom_call" | custom-call | flops 1600000000 | bytes 4000000 | tf_op jit(solution)/shard_map/pallas_call | solution.py:147
  91.4 4.6 %all-to-all-start.2 = ((f32[16,6,128]{2,1,0:T(8,128)}), f32[16,6,128]{2,1,0:T(8,128)S(1)}, u32[]{:S(2)}, u32[]{:S(2)}) async-start(f32[16,6,128]{2,1,0:T(8,128)} %shard_map.60), calls=%async_computation.2 | async-start | bytes 131072 | tf_op jit(solution)/shard_map/all_to_all | solution.py:234
  96.0 6.1 %all-to-all-done.2.came_ref = f32[16,6,128]{2,1,0:T(8,128)S(1)} async-done(((f32[16,6,128]{2,1,0:T(8,128)}), f32[16,6,128]{2,1,0:T(8,128)S(1)}, u32[]{:S(2)}, u32[]{:S(2)}) %all-to-all-start.2) | async-done | bytes 49184 | tf_op jit(solution)/shard_map/all_to_all | solution.py:234
  102.1 1.6 %shard_map.61 = (f32[4,6,2,64]{3,2,1,0:T(2,128)}, f32[32,24,128]{2,1,0:T(8,128)S(1)}) custom-call(s32[10]{0:T(128)S(1)} %pad_add_fusion.at_ref, f32[16,6,128]{2,1,0:T(8,128)S(1)} %all-to-all-done.2.came_ref), custom_call_target="tpu_custom_call" | custom-call | tf_op jit(solution)/shard_map/pallas_call | solution.py:245
  103.8 23.1 %all_to_all.20.came_ref = f32[32,24,128]{2,1,0:T(8,128)S(1)} all-to-all(f32[32,24,128]{2,1,0:T(8,128)S(1)} %get-tuple-element.11), channel_id=1, replica_groups=mesh['xl'=2,'z'=8,'yh'=4,'yl'=2,'xh'=2,'c'=2] {'z','yh'}, dimensions={0} | all-to-all | bytes 786432 | tf_op jit(solution)/shard_map/all_to_all | solution.py:253
  126.9 1.6 %shard_map.62 = f32[4,6,2,64]{3,2,1,0:T(2,128)} custom-call(s32[4]{0:T(128)S(1)} %get-tuple-element.32.at_ref, f32[32,24,128]{2,1,0:T(8,128)S(1)} %all_to_all.20.came_ref), custom_call_target="tpu_custom_call" | custom-call | tf_op jit(solution)/shard_map/pallas_call | solution.py:255
  (34 shorter events, 3.9 us)
Async XLA Ops:
  0.6 9.7 %all-to-all-start = ((bf16[8,8,256]{2,1,0:T(8,128)(2,1)}), bf16[8,8,256]{2,1,0:T(8,128)(2,1)S(1)}, u32[]{:S(2)}, u32[]{:S(2)}) async-start(bf16[8,8,256]{2,1,0:T(8,128)(2,1)} %bitcast.70), calls=%async_computation | async-start | bytes 65536 | tf_op jit(solution)/shard_map/all_to_all | solution.py:201
  11.5 16.6 %copy-start.3 = (bf16[4,6,2,16,256]{4,3,2,1,0:T(8,128)(2,1)S(1)}, bf16[4,6,2,16,256]{4,3,2,1,0:T(8,128)(2,1)}, u32[]{:S(2)}) copy-start(bf16[4,6,2,16,256]{4,3,2,1,0:T(8,128)(2,1)} %param.5) | copy-start | bytes 1179652
  11.5 16.6 %copy-start.4 = (bf16[4,6,2,16,256]{4,3,2,1,0:T(8,128)(2,1)S(1)}, bf16[4,6,2,16,256]{4,3,2,1,0:T(8,128)(2,1)}, u32[]{:S(2)}) copy-start(bf16[4,6,2,16,256]{4,3,2,1,0:T(8,128)(2,1)} %param.4) | copy-start | bytes 1179652
  11.5 48.3 %all-to-all-start.1 = ((bf16[64,8,1152]{2,1,0:T(8,128)(2,1)}), bf16[64,8,1152]{2,1,0:T(8,128)(2,1)S(1)}, u32[]{:S(2)}, u32[]{:S(2)}) async-start(bf16[64,8,1152]{2,1,0:T(8,128)(2,1)} %broadcast_in_dim.3), calls=%async_computation.1 | async-start | bytes 2359296 | tf_op jit(solution)/shard_map/all_to_all | solution.py:210
  28.2 35.2 %collective-permute-start = (bf16[2,4,3,2,16,256]{5,4,3,2,1,0:T(8,128)(2,1)S(1)}, bf16[2,4,3,2,16,256]{5,4,3,2,1,0:T(8,128)(2,1)S(1)}, u32[]{:S(2)}, u32[]{:S(2)}) collective-permute-start(bf16[2,4,3,2,16,256]{5,4,3,2,1,0:T(8,128)(2,1)S(1)} %pad_maximum_fusion), channel_id=1, source_target_pairs={{0,1},{1,0},{2,3},{3,2},{4,5},{5,4},{6,7},{7,6},{8,9},{9,8},{10,11... | collective-permute-start | bytes 1179656 | tf_op jit(solution)/shard_map/ppermute | solution.py:220
  59.9 22.7 %collective-permute-start.4 = (bf16[512,1152]{1,0:T(8,128)(2,1)S(1)}, bf16[512,1152]{1,0:T(8,128)(2,1)S(1)}, u32[]{:S(2)}, u32[]{:S(2)}) collective-permute-start(bf16[512,1152]{1,0:T(8,128)(2,1)S(1)} %bitcast.57), channel_id=1, source_target_pairs={{0,1},{1,0},{2,3},{3,2},{4,5},{5,4},{6,7},{7,6},{8,9},{9,8},{10,11... | collective-permute-start | bytes 3538952 | tf_op jit(solution)/shard_map/ppermute | solution.py:212
  63.6 11.2 %collective-permute-start.1 = (bf16[2,2,3,2,16,256]{5,4,3,2,1,0:T(8,128)(2,1)S(1)}, bf16[2,2,3,2,16,256]{5,4,3,2,1,0:T(8,128)(2,1)S(1)}, u32[]{:S(2)}, u32[]{:S(2)}) collective-permute-start(bf16[2,2,3,2,16,256]{5,4,3,2,1,0:T(8,128)(2,1)S(1)} %bitcast.67), channel_id=1, source_target_pairs={{0,2},{2,0},{256,258},{258,256},{1,3},{3,1},{257,259},{259,257},{4... | collective-permute-start | bytes 589832 | tf_op jit(solution)/shard_map/ppermute | solution.py:229
  66.8 10.2 %collective-permute-start.2 = (bf16[2,2,3,2,16,256]{5,4,3,2,1,0:T(8,128)(2,1)S(1)}, bf16[2,2,3,2,16,256]{5,4,3,2,1,0:T(8,128)(2,1)S(1)}, u32[]{:S(2)}, u32[]{:S(2)}) collective-permute-start(bf16[2,2,3,2,16,256]{5,4,3,2,1,0:T(8,128)(2,1)S(1)} %bitcast.68), channel_id=1, source_target_pairs={{0,256},{2,258},{256,0},{258,2},{1,257},{3,259},{257,1},{259,3},{4... | collective-permute-start | bytes 589832 | tf_op jit(solution)/shard_map/ppermute | solution.py:229
  69.5 9.8 %collective-permute-start.3 = (bf16[2,2,3,2,16,256]{5,4,3,2,1,0:T(8,128)(2,1)S(1)}, bf16[2,2,3,2,16,256]{5,4,3,2,1,0:T(8,128)(2,1)S(1)}, u32[]{:S(2)}, u32[]{:S(2)}) collective-permute-start(bf16[2,2,3,2,16,256]{5,4,3,2,1,0:T(8,128)(2,1)S(1)} %bitcast.69), channel_id=1, source_target_pairs={{0,258},{2,256},{256,2},{258,0},{1,259},{3,257},{257,3},{259,1},{4... | collective-permute-start | bytes 589832 | tf_op jit(solution)/shard_map/ppermute | solution.py:229
  74.8 4.6 %copy-start.5 = (bf16[2,2,3,2,16,256]{5,4,3,2,1,0:T(8,128)(2,1)}, bf16[2,2,3,2,16,256]{5,4,3,2,1,0:T(8,128)(2,1)S(1)}, u32[]{:S(2)}) copy-start(bf16[2,2,3,2,16,256]{5,4,3,2,1,0:T(8,128)(2,1)S(1)} %collective-permute-done.1.refs_1_) | copy-start | bytes 589828
  77.0 2.4 %copy-start.6 = (bf16[2,2,3,2,16,256]{5,4,3,2,1,0:T(8,128)(2,1)}, bf16[2,2,3,2,16,256]{5,4,3,2,1,0:T(8,128)(2,1)S(1)}, u32[]{:S(2)}) copy-start(bf16[2,2,3,2,16,256]{5,4,3,2,1,0:T(8,128)(2,1)S(1)} %collective-permute-done.2.refs_2_) | copy-start | bytes 589828
  79.4 0.7 copy-start.7
  82.6 1.0 copy-start
  83.5 1.0 copy-start.1
  84.5 1.0 copy-start.2
  91.4 10.7 %all-to-all-start.2 = ((f32[16,6,128]{2,1,0:T(8,128)}), f32[16,6,128]{2,1,0:T(8,128)S(1)}, u32[]{:S(2)}, u32[]{:S(2)}) async-start(f32[16,6,128]{2,1,0:T(8,128)} %shard_map.60), calls=%async_computation.2 | async-start | bytes 131072 | tf_op jit(solution)/shard_map/all_to_all | solution.py:234

commit v6 on v4

--- a/solution.py
+++ b/solution.py
@@ -57,45 +57,68 @@
         out_shape=(flat, flat, flat),
         in_specs=[pl.BlockSpec(memory_space=pltpu.SMEM)] + [vm] * 4,
         out_specs=(vm, vm, vm),
+        compiler_params=pltpu.CompilerParams(vmem_limit_bytes=16 << 20),
         cost_estimate=pl.CostEstimate(flops=0, bytes_accessed=2_000_000, transcendentals=0),
     )(at, *pieces)
 
 
-def contract(left_ref, flip_ref, val_ref, own_ref, oth_ref, out_ref, p_ref, q_ref):
-    left = left_ref[...]
-    flipped = flip_ref[...]
-    rows = left.shape[0]
-    wrapped = jnp.concatenate([left, left[:, : 3 * BLK]], 1)
-    wrapped_flip = jnp.concatenate([flipped, flipped[:, : 3 * BLK]], 1)
-    for b in range(NB):
-        lo, hi = b * BLK, (b + 1) * BLK
-        far = wrapped[:, hi : hi + 3 * BLK]
-        far_flip = wrapped_flip[:, hi : hi + 3 * BLK]
-        own = own_ref[lo:hi, :]
-        oth = oth_ref[lo:hi, :]
-        p_back = nt(far_flip, own[:, BLK : 4 * BLK])
-        q_back = -nt(far, oth[:, BLK : 4 * BLK])
-        if b == 0:
-            p_ref[...] = jnp.zeros_like(p_ref)
-            q_ref[...] = jnp.zeros_like(q_ref)
-        p_ref[:, lo:hi] += p_back
-        q_ref[:, lo:hi] += q_back
-        p_fore = nn(left[:, lo:hi], own)
-        q_fore = nn(flipped[:, lo:hi], oth)
-        first = min(SENT, NB - b)
-        p_ref[:, lo : lo + first * BLK] += p_fore[:, : first * BLK]
-        q_ref[:, lo : lo + first * BLK] += q_fore[:, : first * BLK]
-        if first < SENT:
-            p_ref[:, : (SENT - first) * BLK] += p_fore[:, first * BLK :]
-            q_ref[:, : (SENT - first) * BLK] += q_fore[:, first * BLK :]
-    p = p_ref[...].reshape(KQ, 2, PAIR, NG)
-    q = q_ref[...].reshape(KQ, 2, PAIR, NG)
+def stacked(w_ref, j):
+    zero = jnp.zeros((BLK, BLK), BF)
+
+    def block(b, d):
+        half, i = b // 4, b % 4
+        if d < 0 or d > 4 - half:
+            return zero
+        lane = half * SENT * BLK + d * BLK
+        return w_ref[i * BLK : (i + 1) * BLK, lane : lane + BLK]
+
+    first = j - 4 if j >= 4 else j - 3
+    direct = jnp.concatenate(
+        [
+            jnp.concatenate([block(b % NB, j - b), block(b % NB, j + 1 - b)], 1)
+            for b in range(first, j + 2)
+        ],
+        0,
+    )
+    width = 4 if j >= 4 else 5
+    mirrored = jnp.concatenate(
+        [
+            jnp.concatenate([block(row, j + 1 + m - row) if j + 1 + m > row else zero for m in range(width)], 1)
+            for row in (j, j + 1)
+        ],
+        0,
+    )
+    return first, direct, width, mirrored
+
+
+def contract(left_ref, flip_ref, val_ref, own_ref, oth_ref, out_ref):
+    rows = left_ref.shape[0]
     half = rows // 2
-    x_real = (p[:, 0] + q[:, 1]).reshape(half, NG).astype(BF)
-    x_imag = (q[:, 0] - p[:, 1]).reshape(half, NG).astype(BF)
-    val = val_ref[...]
-    g1 = nt(x_real, val)
-    g2 = nt(x_imag, val)
+
+    def wrapped(ref):
+        x = ref[...]
+        return jnp.concatenate([x[:, 5 * BLK :], x, x[:, : 3 * BLK]], 1)
+
+    left, flipped = wrapped(left_ref), wrapped(flip_ref)
+
+    def lanes(x, begin, count):
+        return x[:, (begin + 3) * BLK : (begin + 3 + count) * BLK]
+
+    g1 = jnp.zeros((half, rows), F32)
+    g2 = jnp.zeros((half, rows), F32)
+    for j in range(0, NB, 2):
+        sums = []
+        for ref, ahead, behind in ((own_ref, left, flipped), (oth_ref, flipped, left)):
+            first, direct, width, mirrored = stacked(ref, j)
+            fore = nn(lanes(ahead, first, j + 2 - first), direct)
+            back = nt(lanes(behind, j + 1, width), mirrored)
+            sums.append((fore + back if ref is own_ref else fore - back).reshape(KQ, 2, PAIR, 2 * BLK))
+        p, q = sums
+        x_real = (p[:, 0] + q[:, 1]).reshape(half, 2 * BLK).astype(BF)
+        x_imag = (q[:, 0] - p[:, 1]).reshape(half, 2 * BLK).astype(BF)
+        val = val_ref[:, j * BLK : (j + 2) * BLK]
+        g1 += nt(x_real, val)
+        g2 += nt(x_imag, val)
     r = lax.broadcasted_iota(jnp.int32, (half, rows), 0)
     c = lax.broadcasted_iota(jnp.int32, (half, rows), 1)
     same = r // PAIR == c // (2 * PAIR)
@@ -122,26 +145,19 @@
 
 
 def contracted(left, flipped, val, own, oth):
-    vm = pl.BlockSpec(memory_space=pltpu.VMEM)
     return pl.pallas_call(
         contract,
         out_shape=jax.ShapeDtypeStruct((16, KQ, 128), F32),
-        in_specs=[vm] * 5,
-        out_specs=vm,
-        scratch_shapes=[
-            pltpu.VMEM((2 * KQ * PAIR, NG), F32),
-            pltpu.VMEM((2 * KQ * PAIR, NG), F32),
-        ],
+        in_specs=[pl.BlockSpec(memory_space=pltpu.VMEM)] * 5,
+        out_specs=pl.BlockSpec(memory_space=pltpu.VMEM),
+        compiler_params=pltpu.CompilerParams(vmem_limit_bytes=32 << 20),
         cost_estimate=pl.CostEstimate(
             flops=1_600_000_000, bytes_accessed=4_000_000, transcendentals=0
         ),
     )(left, flipped, val, own, oth)
 
 
-def pick_rows(at_ref, came_ref, fwd_ref, pay_ref, got_ref, sem):
-    copy = pltpu.make_async_copy(came_ref, got_ref, sem)
-    copy.start()
-    copy.wait()
+def pick_rows(at_ref, got_ref, fwd_ref, pay_ref):
     xl = at_ref[0]
     yl = at_ref[1]
     for q in range(Q):
@@ -160,15 +176,9 @@
         pay_ref[slot, :, :] = pay
 
 
-def pick_back(at_ref, came_ref, out_ref, got_ref, sem):
-    copies = [
-        pltpu.make_async_copy(came_ref.at[at_ref[q]], got_ref.at[q], sem.at[q]) for q in range(Q)
-    ]
-    for copy in copies:
-        copy.start()
+def pick_back(at_ref, came_ref, out_ref):
     for q in range(Q):
-        copies[q].wait()
-        rows = got_ref[q, q * KQ : (q + 1) * KQ, :]
+        rows = came_ref[at_ref[q], q * KQ : (q + 1) * KQ, :]
         out_ref[q, :, 0, :] = rows[:, :64]
         out_ref[q, :, 1, :] = rows[:, 64:]
 
@@ -180,12 +190,13 @@
     w = jnp.transpose(w.reshape(2, 4, 8, 256), (0, 2, 1, 3)).reshape(2, 8, NG)
     w = jnp.concatenate([w, w[:, :, : 4 * BLK]], 2)
     cut = [
-        lax.dynamic_slice_in_dim(w[i], (4 * i + z // 2) * BLK, SENT * BLK, 1) for i in range(2)
+        lax.dynamic_slice_in_dim(w[i], (4 * i + z // 2) * BLK, (SENT - i) * BLK, 1)
+        for i in range(2)
     ]
-    w = jnp.stack(cut, 0)
+    w = jnp.concatenate(cut, 1)
     w = jnp.broadcast_to(w, (64,) + w.shape)
     w = lax.all_to_all(w, ("z", "yh", "yl"), 0, 0)
-    own = jnp.transpose(w, (1, 0, 2, 3)).reshape(NG, SENT * BLK)
+    own = w.reshape(NG // 2, (2 * SENT - 1) * BLK)
     oth = lax.ppermute(own, "c", [(0, 1), (1, 0)])
 
     x = xl * 2 + lax.axis_index("xh")
@@ -217,14 +228,12 @@
     at = jnp.concatenate([jnp.stack([xl, yl]), other, begin]).astype(jnp.int32)
     vm = pl.BlockSpec(memory_space=pltpu.VMEM)
     sm = pl.BlockSpec(memory_space=pltpu.SMEM)
-    anywhere = pl.BlockSpec(memory_space=pl.ANY)
     out = jax.ShapeDtypeStruct((Q, KQ, 2, 64), F32)
     forward, pay = pl.pallas_call(
         pick_rows,
         out_shape=(out, jax.ShapeDtypeStruct((32, Q * KQ, 128), F32)),
-        in_specs=[sm, anywhere],
+        in_specs=[sm, vm],
         out_specs=(vm, vm),
-        scratch_shapes=[pltpu.VMEM((16, KQ, 128), F32), pltpu.SemaphoreType.DMA],
         compiler_params=pltpu.CompilerParams(vmem_limit_bytes=8 << 20),
     )(at, got)
     came = lax.all_to_all(pay, ("z", "yh"), 0, 0)
@@ -232,9 +241,8 @@
     back = pl.pallas_call(
         pick_back,
         out_shape=out,
-        in_specs=[sm, anywhere],
+        in_specs=[sm, vm],
         out_specs=vm,
-        scratch_shapes=[pltpu.VMEM((Q, Q * KQ, 128), F32), pltpu.SemaphoreType.DMA((Q,))],
         compiler_params=pltpu.CompilerParams(vmem_limit_bytes=8 << 20),
     )(source, came)
     return forward, back

time: 129 us -> 121 us (0.938)
  Pallas kernels: 11.2 us -> 6.86 us
  waiting for transfers between devices: 46.4 us -> 44.8 us
    all_to_all x1, waiting for transfers between devices: 30.4 us -> 27.5 us  [local(): w = lax.all_to_all(w, ('z', 'yh', 'yl'), 0, 0)]
    pallas_call x1, Pallas kernels: 5.51 us -> 3.24 us  [contracted(): pl.pallas_call(contract, out_shape=jax.ShapeDtypeStruct((16, KQ, 128), F3...]
    pallas_call x1, Pallas kernels: 2.47 us -> 0.78 us  [assembled(): pl.pallas_call(assemble, out_shape=(flat, flat, flat), in_specs=[pl.Block...]
  transfers between devices with their start and end apart: 8 -> 8, of which waited for: 5 -> 6; matrix products, arithmetic and copies ran while one was open for 4% -> 3% of each run, Pallas kernels for 2% -> 1%
where the time goes in v6:
time: 121 us; the launch traced here: 120 us
  waiting for transfers between devices  44.8 us (37%)
  starting transfers between devices  39.1 us (32%)
  blocking collectives  23.1 us (19%)
  Pallas kernels  6.86 us (6%)
  other arithmetic  3.21 us (3%)
  local copies, waits for them, and re-layouts  2.16 us (2%)
    all_to_all x1, waiting for transfers between devices, local(): w = lax.all_to_all(w, ('z', 'yh', 'yl'), 0, 0)  27.5 us
    all_to_all x1, blocking collectives, local(): came = lax.all_to_all(pay, ('z', 'yh'), 0, 0)  23.1 us
    all_to_all x1, starting transfers between devices, local(): w = lax.all_to_all(w, ('z', 'yh', 'yl'), 0, 0)  16.6 us
    ppermute x3, starting transfers between devices, local(): piece = lax.ppermute(piece, ('xl', 'xh'), [(i, i ^ s) for i in range(4)])  9.82 us
    all_to_all x1, waiting for transfers between devices, local(): got = lax.all_to_all(slots, ('xl', 'yl', 'xh', 'c'), 0, 0)  6.1 us
    ppermute x3, waiting for transfers between devices, local(): piece = lax.ppermute(piece, ('xl', 'xh'), [(i, i ^ s) for i in range(4)])  5.76 us
    all_to_all x1, waiting for transfers between devices, local(): w = lax.all_to_all(screened.reshape(8, 8, 256), ('xl', 'xh', 'c'), 0, 0)  5.36 us
    all_to_all x1, starting transfers between devices, local(): got = lax.all_to_all(slots, ('xl', 'yl', 'xh', 'c'), 0, 0)  4.54 us
  transfers between devices with their start and end apart: 8, of which 6 were waited for; matrix products, arithmetic and copies ran while one was open for 3% of the time, Pallas kernels for 1%

profile of v6, /device:TPU:16, one launch (start us, length us, event | category | flops | bytes accessed | tf_op | source)
XLA Modules:
  0.0 120.1 jit_solution(15473135238262774730)
XLA Ops:
  0.6 4.3 %all-to-all-start = ((bf16[8,8,256]{2,1,0:T(8,128)(2,1)}), bf16[8,8,256]{2,1,0:T(8,128)(2,1)S(1)}, u32[]{:S(2)}, u32[]{:S(2)}) async-start(bf16[8,8,256]{2,1,0:T(8,128)(2,1)} %bitcast.70), calls=%async_computation | async-start | bytes 65536 | tf_op jit(solution)/shard_map/all_to_all | solution.py:189
  4.9 5.4 %all-to-all-done = bf16[8,8,256]{2,1,0:T(8,128)(2,1)S(1)} async-done(((bf16[8,8,256]{2,1,0:T(8,128)(2,1)}), bf16[8,8,256]{2,1,0:T(8,128)(2,1)S(1)}, u32[]{:S(2)}, u32[]{:S(2)}) %all-to-all-start) | async-done | bytes 32800 | tf_op jit(solution)/shard_map/all_to_all | solution.py:189
  10.4 1.1 broadcast_in_dim.3
  11.5 16.6 %all-to-all-start.1 = ((bf16[64,8,1152]{2,1,0:T(8,128)(2,1)}), bf16[64,8,1152]{2,1,0:T(8,128)(2,1)S(1)}, u32[]{:S(2)}, u32[]{:S(2)}) async-start(bf16[64,8,1152]{2,1,0:T(8,128)(2,1)} %broadcast_in_dim.3), calls=%async_computation.1 | async-start | bytes 2359296 | tf_op jit(solution)/shard_map/all_to_all | solution.py:198
  28.2 1.9 %collective-permute-start = (bf16[2,4,3,2,16,256]{5,4,3,2,1,0:T(8,128)(2,1)S(1)}, bf16[2,4,3,2,16,256]{5,4,3,2,1,0:T(8,128)(2,1)S(1)}, u32[]{:S(2)}, u32[]{:S(2)}) collective-permute-start(bf16[2,4,3,2,16,256]{5,4,3,2,1,0:T(8,128)(2,1)S(1)} %pad_maximum_fusion), channel_id=1, source_target_pairs={{0,1},{1,0},{2,3},{3,2},{4,5},{5,4},{6,7},{7,6},{8,9},{9,8},{10,11... | collective-permute-start | bytes 1179656 | tf_op jit(solution)/shard_map/ppermute | solution.py:208
  30.2 1.4 %divide_reduce_fusion = (s32[4]{0:T(128)}, s32[4]{0:T(128)}) fusion(s32[4,768]{1,0:T(4,128)} %param.7), kind=kLoop, calls=%fused_computation.38 | loop fusion | flops 8 | bytes 48 | tf_op jit(solution)/shard_map/jit(floor_divide)/div | solution.py:224
  31.5 0.8 fusion.3
  32.3 27.5 %all-to-all-done.1 = bf16[64,8,1152]{2,1,0:T(8,128)(2,1)S(1)} async-done(((bf16[64,8,1152]{2,1,0:T(8,128)(2,1)}), bf16[64,8,1152]{2,1,0:T(8,128)(2,1)S(1)}, u32[]{:S(2)}, u32[]{:S(2)}) %all-to-all-start.1) | async-done | bytes 1179680 | tf_op jit(solution)/shard_map/all_to_all | solution.py:198
  59.9 1.9 %collective-permute-start.4 = (bf16[512,1152]{1,0:T(8,128)(2,1)S(1)}, bf16[512,1152]{1,0:T(8,128)(2,1)S(1)}, u32[]{:S(2)}, u32[]{:S(2)}) collective-permute-start(bf16[512,1152]{1,0:T(8,128)(2,1)S(1)} %bitcast.57), channel_id=1, source_target_pairs={{0,1},{1,0},{2,3},{3,2},{4,5},{5,4},{6,7},{7,6},{8,9},{9,8},{10,11... | collective-permute-start | bytes 3538952 | tf_op jit(solution)/shard_map/ppermute | solution.py:200
  61.8 0.7 and_select_fusion
  62.5 0.9 dynamic-slice_bitcast_fusion.3
  63.6 3.2 %collective-permute-start.1 = (bf16[2,2,3,2,16,256]{5,4,3,2,1,0:T(8,128)(2,1)S(1)}, bf16[2,2,3,2,16,256]{5,4,3,2,1,0:T(8,128)(2,1)S(1)}, u32[]{:S(2)}, u32[]{:S(2)}) collective-permute-start(bf16[2,2,3,2,16,256]{5,4,3,2,1,0:T(8,128)(2,1)S(1)} %bitcast.67), channel_id=1, source_target_pairs={{0,2},{2,0},{256,258},{258,256},{1,3},{3,1},{257,259},{259,257},{4... | collective-permute-start | bytes 589832 | tf_op jit(solution)/shard_map/ppermute | solution.py:217
  66.8 2.7 %collective-permute-start.2 = (bf16[2,2,3,2,16,256]{5,4,3,2,1,0:T(8,128)(2,1)S(1)}, bf16[2,2,3,2,16,256]{5,4,3,2,1,0:T(8,128)(2,1)S(1)}, u32[]{:S(2)}, u32[]{:S(2)}) collective-permute-start(bf16[2,2,3,2,16,256]{5,4,3,2,1,0:T(8,128)(2,1)S(1)} %bitcast.68), channel_id=1, source_target_pairs={{0,256},{2,258},{256,0},{258,2},{1,257},{3,259},{257,1},{259,3},{4... | collective-permute-start | bytes 589832 | tf_op jit(solution)/shard_map/ppermute | solution.py:217
  69.5 4.0 %collective-permute-start.3 = (bf16[2,2,3,2,16,256]{5,4,3,2,1,0:T(8,128)(2,1)S(1)}, bf16[2,2,3,2,16,256]{5,4,3,2,1,0:T(8,128)(2,1)S(1)}, u32[]{:S(2)}, u32[]{:S(2)}) collective-permute-start(bf16[2,2,3,2,16,256]{5,4,3,2,1,0:T(8,128)(2,1)S(1)} %bitcast.69), channel_id=1, source_target_pairs={{0,258},{2,256},{256,2},{258,0},{1,259},{3,257},{257,3},{259,1},{4... | collective-permute-start | bytes 589832 | tf_op jit(solution)/shard_map/ppermute | solution.py:217
  73.6 1.1 collective-permute-done.1.refs_1_
  74.8 2.2 %collective-permute-done.2.refs_2_ = bf16[2,2,3,2,16,256]{5,4,3,2,1,0:T(8,128)(2,1)S(1)} collective-permute-done((bf16[2,2,3,2,16,256]{5,4,3,2,1,0:T(8,128)(2,1)S(1)}, bf16[2,2,3,2,16,256]{5,4,3,2,1,0:T(8,128)(2,1)S(1)}, u32[]{:S(2)}, u32[]{:S(2)}) %collective-permute-start.2) | collective-permute-done | bytes 196640 | tf_op jit(solution)/shard_map/ppermute | solution.py:217
  77.0 2.4 %collective-permute-done.3.refs_3_ = bf16[2,2,3,2,16,256]{5,4,3,2,1,0:T(8,128)(2,1)S(1)} collective-permute-done((bf16[2,2,3,2,16,256]{5,4,3,2,1,0:T(8,128)(2,1)S(1)}, bf16[2,2,3,2,16,256]{5,4,3,2,1,0:T(8,128)(2,1)S(1)}, u32[]{:S(2)}, u32[]{:S(2)}) %collective-permute-start.3) | collective-permute-done | bytes 196640 | tf_op jit(solution)/shard_map/ppermute | solution.py:217
  79.4 0.8 shard_map.59
  80.2 3.2 %shard_map.60 = f32[16,6,128]{2,1,0:T(8,128)} custom-call(bf16[192,1024]{1,0:T(8,128)(2,1)S(1)} %get-tuple-element.7.left_ref, bf16[192,1024]{1,0:T(8,128)(2,1)S(1)} %get-tuple-element.8.flip_ref, bf16[192,1024]{1,0:T(8,128)(2,1)S(1)} %get-tuple-element.9.val_ref, bf16[512,1152]{1,0:T(8,128)(2,1)S(1)} %bitcast.58, ...), custom_call_target="tpu_custom_call" | custom-call | flops 1600000000 | bytes 4000000 | tf_op jit(solution)/shard_map/pallas_call | solution.py:148
  83.4 4.5 %all-to-all-start.2 = ((f32[16,6,128]{2,1,0:T(8,128)}), f32[16,6,128]{2,1,0:T(8,128)S(1)}, u32[]{:S(2)}, u32[]{:S(2)}) async-start(f32[16,6,128]{2,1,0:T(8,128)} %shard_map.60), calls=%async_computation.2 | async-start | bytes 131072 | tf_op jit(solution)/shard_map/all_to_all | solution.py:222
  88.0 6.1 %all-to-all-done.2.got_ref = f32[16,6,128]{2,1,0:T(8,128)S(1)} async-done(((f32[16,6,128]{2,1,0:T(8,128)}), f32[16,6,128]{2,1,0:T(8,128)S(1)}, u32[]{:S(2)}, u32[]{:S(2)}) %all-to-all-start.2) | async-done | bytes 49184 | tf_op jit(solution)/shard_map/all_to_all | solution.py:222
  94.1 1.6 %shard_map.61 = (f32[4,6,2,64]{3,2,1,0:T(2,128)}, f32[32,24,128]{2,1,0:T(8,128)S(1)}) custom-call(s32[10]{0:T(128)S(1)} %pad_add_fusion.at_ref, f32[16,6,128]{2,1,0:T(8,128)S(1)} %all-to-all-done.2.got_ref), custom_call_target="tpu_custom_call" | custom-call | tf_op jit(solution)/shard_map/pallas_call | solution.py:232
  95.7 23.1 %all_to_all.20.came_ref = f32[32,24,128]{2,1,0:T(8,128)S(1)} all-to-all(f32[32,24,128]{2,1,0:T(8,128)S(1)} %get-tuple-element.11), channel_id=1, replica_groups=mesh['xl'=2,'z'=8,'yh'=4,'yl'=2,'xh'=2,'c'=2] {'z','yh'}, dimensions={0} | all-to-all | bytes 786432 | tf_op jit(solution)/shard_map/all_to_all | solution.py:239
  118.8 1.2 %shard_map.62 = f32[4,6,2,64]{3,2,1,0:T(2,128)} custom-call(s32[4]{0:T(128)S(1)} %get-tuple-element.32.at_ref, f32[32,24,128]{2,1,0:T(8,128)S(1)} %all_to_all.20.came_ref), custom_call_target="tpu_custom_call" | custom-call | tf_op jit(solution)/shard_map/pallas_call | solution.py:241
  (22 shorter events, 0.5 us)
Async XLA Ops:
  0.6 9.7 %all-to-all-start = ((bf16[8,8,256]{2,1,0:T(8,128)(2,1)}), bf16[8,8,256]{2,1,0:T(8,128)(2,1)S(1)}, u32[]{:S(2)}, u32[]{:S(2)}) async-start(bf16[8,8,256]{2,1,0:T(8,128)(2,1)} %bitcast.70), calls=%async_computation | async-start | bytes 65536 | tf_op jit(solution)/shard_map/all_to_all | solution.py:189
  11.5 16.6 %copy-start = (bf16[4,6,2,16,256]{4,3,2,1,0:T(8,128)(2,1)S(1)}, bf16[4,6,2,16,256]{4,3,2,1,0:T(8,128)(2,1)}, u32[]{:S(2)}) copy-start(bf16[4,6,2,16,256]{4,3,2,1,0:T(8,128)(2,1)} %param.5) | copy-start | bytes 1179652
  11.5 16.6 %copy-start.1 = (bf16[4,6,2,16,256]{4,3,2,1,0:T(8,128)(2,1)S(1)}, bf16[4,6,2,16,256]{4,3,2,1,0:T(8,128)(2,1)}, u32[]{:S(2)}) copy-start(bf16[4,6,2,16,256]{4,3,2,1,0:T(8,128)(2,1)} %param.4) | copy-start | bytes 1179652
  11.5 48.3 %all-to-all-start.1 = ((bf16[64,8,1152]{2,1,0:T(8,128)(2,1)}), bf16[64,8,1152]{2,1,0:T(8,128)(2,1)S(1)}, u32[]{:S(2)}, u32[]{:S(2)}) async-start(bf16[64,8,1152]{2,1,0:T(8,128)(2,1)} %broadcast_in_dim.3), calls=%async_computation.1 | async-start | bytes 2359296 | tf_op jit(solution)/shard_map/all_to_all | solution.py:198
  28.2 35.2 %collective-permute-start = (bf16[2,4,3,2,16,256]{5,4,3,2,1,0:T(8,128)(2,1)S(1)}, bf16[2,4,3,2,16,256]{5,4,3,2,1,0:T(8,128)(2,1)S(1)}, u32[]{:S(2)}, u32[]{:S(2)}) collective-permute-start(bf16[2,4,3,2,16,256]{5,4,3,2,1,0:T(8,128)(2,1)S(1)} %pad_maximum_fusion), channel_id=1, source_target_pairs={{0,1},{1,0},{2,3},{3,2},{4,5},{5,4},{6,7},{7,6},{8,9},{9,8},{10,11... | collective-permute-start | bytes 1179656 | tf_op jit(solution)/shard_map/ppermute | solution.py:208
  59.9 20.3 %collective-permute-start.4 = (bf16[512,1152]{1,0:T(8,128)(2,1)S(1)}, bf16[512,1152]{1,0:T(8,128)(2,1)S(1)}, u32[]{:S(2)}, u32[]{:S(2)}) collective-permute-start(bf16[512,1152]{1,0:T(8,128)(2,1)S(1)} %bitcast.57), channel_id=1, source_target_pairs={{0,1},{1,0},{2,3},{3,2},{4,5},{5,4},{6,7},{7,6},{8,9},{9,8},{10,11... | collective-permute-start | bytes 3538952 | tf_op jit(solution)/shard_map/ppermute | solution.py:200
  63.6 11.2 %collective-permute-start.1 = (bf16[2,2,3,2,16,256]{5,4,3,2,1,0:T(8,128)(2,1)S(1)}, bf16[2,2,3,2,16,256]{5,4,3,2,1,0:T(8,128)(2,1)S(1)}, u32[]{:S(2)}, u32[]{:S(2)}) collective-permute-start(bf16[2,2,3,2,16,256]{5,4,3,2,1,0:T(8,128)(2,1)S(1)} %bitcast.67), channel_id=1, source_target_pairs={{0,2},{2,0},{256,258},{258,256},{1,3},{3,1},{257,259},{259,257},{4... | collective-permute-start | bytes 589832 | tf_op jit(solution)/shard_map/ppermute | solution.py:217
  66.8 10.2 %collective-permute-start.2 = (bf16[2,2,3,2,16,256]{5,4,3,2,1,0:T(8,128)(2,1)S(1)}, bf16[2,2,3,2,16,256]{5,4,3,2,1,0:T(8,128)(2,1)S(1)}, u32[]{:S(2)}, u32[]{:S(2)}) collective-permute-start(bf16[2,2,3,2,16,256]{5,4,3,2,1,0:T(8,128)(2,1)S(1)} %bitcast.68), channel_id=1, source_target_pairs={{0,256},{2,258},{256,0},{258,2},{1,257},{3,259},{257,1},{259,3},{4... | collective-permute-start | bytes 589832 | tf_op jit(solution)/shard_map/ppermute | solution.py:217
  69.5 9.8 %collective-permute-start.3 = (bf16[2,2,3,2,16,256]{5,4,3,2,1,0:T(8,128)(2,1)S(1)}, bf16[2,2,3,2,16,256]{5,4,3,2,1,0:T(8,128)(2,1)S(1)}, u32[]{:S(2)}, u32[]{:S(2)}) collective-permute-start(bf16[2,2,3,2,16,256]{5,4,3,2,1,0:T(8,128)(2,1)S(1)} %bitcast.69), channel_id=1, source_target_pairs={{0,258},{2,256},{256,2},{258,0},{1,259},{3,257},{257,3},{259,1},{4... | collective-permute-start | bytes 589832 | tf_op jit(solution)/shard_map/ppermute | solution.py:217
  83.4 10.7 %all-to-all-start.2 = ((f32[16,6,128]{2,1,0:T(8,128)}), f32[16,6,128]{2,1,0:T(8,128)S(1)}, u32[]{:S(2)}, u32[]{:S(2)}) async-start(f32[16,6,128]{2,1,0:T(8,128)} %shard_map.60), calls=%async_computation.2 | async-start | bytes 131072 | tf_op jit(solution)/shard_map/all_to_all | solution.py:222

commit v7 on v6

--- a/solution.py
+++ b/solution.py
@@ -25,6 +25,30 @@
 
 def nn(left, right, precision=None):
     return jnp.dot(left, right, preferred_element_type=F32, precision=precision)
+
+
+def fan(at_ref, w_ref, out_ref):
+    lane = 0
+    for xl in range(2):
+        for d in range(SENT - xl):
+            block = lax.rem(at_ref[0] + (4 * xl + d), NB)
+            lanes = pl.ds(pl.multiple_of((block % 2) * BLK, BLK), BLK)
+            out_ref[0, :, lane : lane + BLK] = w_ref[4 * xl + block // 2, :, lanes]
+            lane += BLK
+    piece = out_ref[0]
+    for slot in range(1, 64):
+        out_ref[slot, :, :] = piece
+
+
+def fanned(at, w):
+    vm = pl.BlockSpec(memory_space=pltpu.VMEM)
+    return pl.pallas_call(
+        fan,
+        out_shape=jax.ShapeDtypeStruct((64, 8, (2 * SENT - 1) * BLK), BF),
+        in_specs=[pl.BlockSpec(memory_space=pltpu.SMEM), vm],
+        out_specs=vm,
+        compiler_params=pltpu.CompilerParams(vmem_limit_bytes=16 << 20),
+    )(at, w)
 
 
 def assemble(at_ref, *refs):
@@ -91,32 +115,39 @@
     return first, direct, width, mirrored
 
 
-def contract(left_ref, flip_ref, val_ref, own_ref, oth_ref, out_ref):
+def wrapped(x):
+    return jnp.concatenate([x[:, 5 * BLK :], x, x[:, : 3 * BLK]], 1)
+
+
+def screened_pair(w_ref, ahead, behind, j):
+    def lanes(x, begin, count):
+        return x[:, (begin + 3) * BLK : (begin + 3 + count) * BLK]
+
+    first, direct, width, mirrored = stacked(w_ref, j)
+    return nn(lanes(ahead, first, j + 2 - first), direct), nt(lanes(behind, j + 1, width), mirrored)
+
+
+def contract_own(left_ref, flip_ref, own_ref, p_ref):
+    left, flipped = wrapped(left_ref[...]), wrapped(flip_ref[...])
+    for j in range(0, NB, 2):
+        fore, back = screened_pair(own_ref, left, flipped, j)
+        p_ref[:, j * BLK : (j + 2) * BLK] = fore + back
+
+
+def contract(left_ref, flip_ref, val_ref, p_ref, oth_ref, out_ref):
     rows = left_ref.shape[0]
     half = rows // 2
-
-    def wrapped(ref):
-        x = ref[...]
-        return jnp.concatenate([x[:, 5 * BLK :], x, x[:, : 3 * BLK]], 1)
-
-    left, flipped = wrapped(left_ref), wrapped(flip_ref)
-
-    def lanes(x, begin, count):
-        return x[:, (begin + 3) * BLK : (begin + 3 + count) * BLK]
-
+    left, flipped = wrapped(left_ref[...]), wrapped(flip_ref[...])
     g1 = jnp.zeros((half, rows), F32)
     g2 = jnp.zeros((half, rows), F32)
     for j in range(0, NB, 2):
-        sums = []
-        for ref, ahead, behind in ((own_ref, left, flipped), (oth_ref, flipped, left)):
-            first, direct, width, mirrored = stacked(ref, j)
-            fore = nn(lanes(ahead, first, j + 2 - first), direct)
-            back = nt(lanes(behind, j + 1, width), mirrored)
-            sums.append((fore + back if ref is own_ref else fore - back).reshape(KQ, 2, PAIR, 2 * BLK))
-        p, q = sums
+        columns = slice(j * BLK, (j + 2) * BLK)
+        fore, back = screened_pair(oth_ref, flipped, left, j)
+        q = (fore - back).reshape(KQ, 2, PAIR, 2 * BLK)
+        p = p_ref[:, columns].reshape(KQ, 2, PAIR, 2 * BLK)
         x_real = (p[:, 0] + q[:, 1]).reshape(half, 2 * BLK).astype(BF)
         x_imag = (q[:, 0] - p[:, 1]).reshape(half, 2 * BLK).astype(BF)
-        val = val_ref[:, j * BLK : (j + 2) * BLK]
+        val = val_ref[:, columns]
         g1 += nt(x_real, val)
         g2 += nt(x_imag, val)
     r = lax.broadcasted_iota(jnp.int32, (half, rows), 0)
@@ -144,41 +175,51 @@
         out_ref[slot, :, :] = block[g * 8 : g * 8 + KQ, :]
 
 
-def contracted(left, flipped, val, own, oth):
+def contracted(left, flipped, val, own):
+    vm = pl.BlockSpec(memory_space=pltpu.VMEM)
+    kept = pltpu.CompilerParams(vmem_limit_bytes=24 << 20)
+    cost = pl.CostEstimate(flops=800_000_000, bytes_accessed=2_000_000, transcendentals=0)
+    oth = lax.ppermute(own, "c", [(0, 1), (1, 0)])
+    p = pl.pallas_call(
+        contract_own,
+        out_shape=jax.ShapeDtypeStruct((2 * KQ * PAIR, NG), F32),
+        in_specs=[vm] * 3,
+        out_specs=vm,
+        compiler_params=kept,
+        cost_estimate=cost,
+    )(left, flipped, own)
     return pl.pallas_call(
         contract,
         out_shape=jax.ShapeDtypeStruct((16, KQ, 128), F32),
-        in_specs=[pl.BlockSpec(memory_space=pltpu.VMEM)] * 5,
-        out_specs=pl.BlockSpec(memory_space=pltpu.VMEM),
-        compiler_params=pltpu.CompilerParams(vmem_limit_bytes=32 << 20),
-        cost_estimate=pl.CostEstimate(
-            flops=1_600_000_000, bytes_accessed=4_000_000, transcendentals=0
-        ),
-    )(left, flipped, val, own, oth)
-
-
-def pick_rows(at_ref, got_ref, fwd_ref, pay_ref):
-    xl = at_ref[0]
-    yl = at_ref[1]
+        in_specs=[vm] * 5,
+        out_specs=vm,
+        compiler_params=kept,
+        cost_estimate=cost,
+    )(left, flipped, val, p, oth)
+
+
+def pick_rows(at_ref, got_ref, fwd_ref, pay_ref, row_ref):
+    xl = at_ref[2]
+    yl = at_ref[3]
     for q in range(Q):
         base = (q // 2) * 8 + (q % 2) * 2
-        other = at_ref[2 + q]
-        begin = at_ref[6 + q]
+        other = at_ref[4 + q]
+        begin = at_ref[8 + q]
         for t in range(KQ):
             row = got_ref[base + yl * 4 + t // 3, pl.ds(xl * 3 + t % 3, 1), :]
             fwd_ref[q, pl.ds(t, 1), 0, :] = row[:, :64]
             fwd_ref[q, pl.ds(t, 1), 1, :] = row[:, 64:]
             col = lax.rem(begin + t, 12)
             slot = base + (col // 6) * 4 + (col % 6) // 3
-            pay_ref[0, pl.ds(q * KQ + t, 1), :] = got_ref[slot, pl.ds(other * 3 + col % 3, 1), :]
-    pay = pay_ref[0]
-    for slot in range(1, 32):
+            row_ref[pl.ds(q * KQ + t, 1), :] = got_ref[slot, pl.ds(other * 3 + col % 3, 1), :]
+    pay = row_ref[...].astype(BF)
+    for slot in range(32):
         pay_ref[slot, :, :] = pay
 
 
 def pick_back(at_ref, came_ref, out_ref):
     for q in range(Q):
-        rows = came_ref[at_ref[q], q * KQ : (q + 1) * KQ, :]
+        rows = came_ref[at_ref[12 + q]].astype(F32)[q * KQ : (q + 1) * KQ, :]
         out_ref[q, :, 0, :] = rows[:, :64]
         out_ref[q, :, 1, :] = rows[:, 64:]
 
@@ -187,17 +228,9 @@
     xl, yl, core = lax.axis_index("xl"), lax.axis_index("yl"), lax.axis_index("c")
     z, yh = lax.axis_index("z"), lax.axis_index("yh")
     w = lax.all_to_all(screened.reshape(8, 8, 256), ("xl", "xh", "c"), 0, 0)
-    w = jnp.transpose(w.reshape(2, 4, 8, 256), (0, 2, 1, 3)).reshape(2, 8, NG)
-    w = jnp.concatenate([w, w[:, :, : 4 * BLK]], 2)
-    cut = [
-        lax.dynamic_slice_in_dim(w[i], (4 * i + z // 2) * BLK, (SENT - i) * BLK, 1)
-        for i in range(2)
-    ]
-    w = jnp.concatenate(cut, 1)
-    w = jnp.broadcast_to(w, (64,) + w.shape)
+    w = fanned((z // 2).astype(jnp.int32).reshape(1), w)
     w = lax.all_to_all(w, ("z", "yh", "yl"), 0, 0)
     own = w.reshape(NG // 2, (2 * SENT - 1) * BLK)
-    oth = lax.ppermute(own, "c", [(0, 1), (1, 0)])
 
     x = xl * 2 + lax.axis_index("xh")
 
@@ -216,35 +249,35 @@
         if s:
             piece = lax.ppermute(piece, ("xl", "xh"), [(i, i ^ s) for i in range(4)])
         pieces.append(piece)
-    here_x = jnp.stack([x, core]).astype(jnp.int32)
-    left, flipped, right = assembled(here_x, pieces)
-    slots = contracted(left, flipped, right, own, oth)
-    got = lax.all_to_all(slots, ("xl", "yl", "xh", "c"), 0, 0)
     corner = k_plus[:, 0]
     row_step, col_step = corner // 12, corner % 12
     here = z * 4 + yh
     other = xl ^ ((here + row_step) // 32 % 2)
     begin = (6 * yl - col_step + 12) % 12
-    at = jnp.concatenate([jnp.stack([xl, yl]), other, begin]).astype(jnp.int32)
+    source = (here - row_step) % 32
+    at = jnp.concatenate([jnp.stack([x, core, xl, yl]), other, begin, source]).astype(jnp.int32)
+    left, flipped, right = assembled(at, pieces)
+    slots = contracted(left, flipped, right, own)
+    got = lax.all_to_all(slots, ("xl", "yl", "xh", "c"), 0, 0)
     vm = pl.BlockSpec(memory_space=pltpu.VMEM)
     sm = pl.BlockSpec(memory_space=pltpu.SMEM)
     out = jax.ShapeDtypeStruct((Q, KQ, 2, 64), F32)
     forward, pay = pl.pallas_call(
         pick_rows,
-        out_shape=(out, jax.ShapeDtypeStruct((32, Q * KQ, 128), F32)),
+        out_shape=(out, jax.ShapeDtypeStruct((32, Q * KQ, 128), BF)),
         in_specs=[sm, vm],
         out_specs=(vm, vm),
+        scratch_shapes=[pltpu.VMEM((Q * KQ, 128), F32)],
         compiler_params=pltpu.CompilerParams(vmem_limit_bytes=8 << 20),
     )(at, got)
     came = lax.all_to_all(pay, ("z", "yh"), 0, 0)
-    source = ((here - row_step) % 32).astype(jnp.int32)
     back = pl.pallas_call(
         pick_back,
         out_shape=out,
         in_specs=[sm, vm],
         out_specs=vm,
         compiler_params=pltpu.CompilerParams(vmem_limit_bytes=8 << 20),
-    )(source, came)
+    )(at, came)
     return forward, back
 
 

time: 121 us -> 115 us (0.950)
  waiting for transfers between devices: 44.8 us -> 37.3 us
  blocking collectives: 23.1 us -> 29.6 us
  starting transfers between devices: 39.1 us -> 34.7 us
    all_to_all x0 -> x1, blocking collectives: none -> 10.6 us  [local(): got = lax.all_to_all(slots, ('xl', 'yl', 'xh', 'c'), 0, 0)]
    all_to_all x1 -> x0, waiting for transfers between devices: 6.1 us -> none  [local(): got = lax.all_to_all(slots, ('xl', 'yl', 'xh', 'c'), 0, 0)]
    all_to_all x1 -> x0, starting transfers between devices: 4.54 us -> none  [local(): got = lax.all_to_all(slots, ('xl', 'yl', 'xh', 'c'), 0, 0)]
    all_to_all x1, blocking collectives: 23.1 us -> 19 us  [local(): came = lax.all_to_all(pay, ('z', 'yh'), 0, 0)]
    pallas_call x0 -> x2, Pallas kernels: none -> 1.99 us  [the longest x1 1.14 us: fanned(): pl.pallas_call(fan, out_shape=jax.ShapeDtypeStruct((64, 8, (2 * SENT - 1)...]
    div x1 -> x0, other arithmetic: 1.35 us -> none  [local(): row_step, col_step = (corner // 12, corner % 12)]
    pallas_call x1, Pallas kernels: 3.24 us -> 1.89 us  [contracted(): pl.pallas_call(contract, out_shape=jax.ShapeDtypeStruct((16, KQ, 128), F3...]
  transfers between devices with their start and end apart: 8 -> 7, of which waited for: 6 -> 4; matrix products, arithmetic and copies ran while one was open for 3% -> 4% of each run, Pallas kernels for 1% -> 1%
where the time goes in v7:
time: 115 us
  waiting for transfers between devices  37.3 us (32%)
  starting transfers between devices  34.7 us (30%)
  blocking collectives  29.6 us (26%)
  Pallas kernels  7.5 us (7%)
  other arithmetic  3.09 us (3%)
  local copies, waits for them, and re-layouts  1.6 us (1%)
    all_to_all x1, waiting for transfers between devices, local(): w = lax.all_to_all(w, ('z', 'yh', 'yl'), 0, 0)  27.3 us
    all_to_all x1, blocking collectives, local(): came = lax.all_to_all(pay, ('z', 'yh'), 0, 0)  19 us
    all_to_all x1, starting transfers between devices, local(): w = lax.all_to_all(w, ('z', 'yh', 'yl'), 0, 0)  16.6 us
    all_to_all x1, blocking collectives, local(): got = lax.all_to_all(slots, ('xl', 'yl', 'xh', 'c'), 0, 0)  10.6 us
    ppermute x3, starting transfers between devices, local(): piece = lax.ppermute(piece, ('xl', 'xh'), [(i, i ^ s) for i in range(4)])  9.81 us
    all_to_all x1, waiting for transfers between devices, local(): w = lax.all_to_all(screened.reshape(8, 8, 256), ('xl', 'xh', 'c'), 0, 0)  5.36 us
    ppermute x3, waiting for transfers between devices, local(): piece = lax.ppermute(piece, ('xl', 'xh'), [(i, i ^ s) for i in range(4)])  4.66 us
    all_to_all x1, starting transfers between devices, local(): w = lax.all_to_all(screened.reshape(8, 8, 256), ('xl', 'xh', 'c'), 0, 0)  4.31 us
  transfers between devices with their start and end apart: 7, of which 4 were waited for; matrix products, arithmetic and copies ran while one was open for 4% of the time, Pallas kernels for 1%

profile of v7, /device:TPU:16, one launch (start us, length us, event | category | flops | bytes accessed | tf_op | source)
XLA Modules:
  0.0 114.7 jit_solution(9785834064252477490)
XLA Ops:
  0.6 4.3 %all-to-all-start = ((bf16[8,8,256]{2,1,0:T(8,128)(2,1)}), bf16[8,8,256]{2,1,0:T(8,128)(2,1)S(1)}, u32[]{:S(2)}, u32[]{:S(2)}) async-start(bf16[8,8,256]{2,1,0:T(8,128)(2,1)} %bitcast.58), calls=%async_computation | async-start | bytes 65536 | tf_op jit(solution)/shard_map/all_to_all | solution.py:230
  4.9 5.4 %all-to-all-done.w_ref = bf16[8,8,256]{2,1,0:T(8,128)(2,1)S(1)} async-done(((bf16[8,8,256]{2,1,0:T(8,128)(2,1)}), bf16[8,8,256]{2,1,0:T(8,128)(2,1)S(1)}, u32[]{:S(2)}, u32[]{:S(2)}) %all-to-all-start) | async-done | bytes 32800 | tf_op jit(solution)/shard_map/all_to_all | solution.py:230
  10.3 1.1 shard_map.60
  11.4 16.6 %all-to-all-start.1 = ((bf16[64,8,1152]{2,1,0:T(8,128)(2,1)}), bf16[64,8,1152]{2,1,0:T(8,128)(2,1)S(1)}, u32[]{:S(2)}, u32[]{:S(2)}) async-start(bf16[64,8,1152]{2,1,0:T(8,128)(2,1)} %shard_map.60), calls=%async_computation.1 | async-start | bytes 2359296 | tf_op jit(solution)/shard_map/all_to_all | solution.py:232
  28.2 1.9 %collective-permute-start = (bf16[2,4,3,2,16,256]{5,4,3,2,1,0:T(8,128)(2,1)S(1)}, bf16[2,4,3,2,16,256]{5,4,3,2,1,0:T(8,128)(2,1)S(1)}, u32[]{:S(2)}, u32[]{:S(2)}) collective-permute-start(bf16[2,4,3,2,16,256]{5,4,3,2,1,0:T(8,128)(2,1)S(1)} %pad_maximum_fusion), channel_id=1, source_target_pairs={{0,1},{1,0},{2,3},{3,2},{4,5},{5,4},{6,7},{7,6},{8,9},{9,8},{10,11... | collective-permute-start | bytes 1179656 | tf_op jit(solution)/shard_map/ppermute | solution.py:241
  30.1 0.8 fusion
  30.9 0.8 remainder_reduce_fusion
  31.8 0.7 dynamic-slice_bitcast_fusion.3
  32.5 27.3 %all-to-all-done.1 = bf16[64,8,1152]{2,1,0:T(8,128)(2,1)S(1)} async-done(((bf16[64,8,1152]{2,1,0:T(8,128)(2,1)}), bf16[64,8,1152]{2,1,0:T(8,128)(2,1)S(1)}, u32[]{:S(2)}, u32[]{:S(2)}) %all-to-all-start.1) | async-done | bytes 1179680 | tf_op jit(solution)/shard_map/all_to_all | solution.py:232
  59.8 2.1 %collective-permute-start.4 = (bf16[512,1152]{1,0:T(8,128)(2,1)S(1)}, bf16[512,1152]{1,0:T(8,128)(2,1)S(1)}, u32[]{:S(2)}, u32[]{:S(2)}) collective-permute-start(bf16[512,1152]{1,0:T(8,128)(2,1)S(1)} %bitcast.49), channel_id=1, source_target_pairs={{0,1},{1,0},{2,3},{3,2},{4,5},{5,4},{6,7},{7,6},{8,9},{9,8},{10,11... | collective-permute-start | bytes 3538952 | tf_op jit(solution)/shard_map/ppermute | solution.py:182
  62.0 3.2 %collective-permute-start.1 = (bf16[2,2,3,2,16,256]{5,4,3,2,1,0:T(8,128)(2,1)S(1)}, bf16[2,2,3,2,16,256]{5,4,3,2,1,0:T(8,128)(2,1)S(1)}, u32[]{:S(2)}, u32[]{:S(2)}) collective-permute-start(bf16[2,2,3,2,16,256]{5,4,3,2,1,0:T(8,128)(2,1)S(1)} %bitcast.56), channel_id=1, source_target_pairs={{0,2},{2,0},{256,258},{258,256},{1,3},{3,1},{257,259},{259,257},{4... | collective-permute-start | bytes 589832 | tf_op jit(solution)/shard_map/ppermute | solution.py:250
  65.2 2.7 %collective-permute-start.2 = (bf16[2,2,3,2,16,256]{5,4,3,2,1,0:T(8,128)(2,1)S(1)}, bf16[2,2,3,2,16,256]{5,4,3,2,1,0:T(8,128)(2,1)S(1)}, u32[]{:S(2)}, u32[]{:S(2)}) collective-permute-start(bf16[2,2,3,2,16,256]{5,4,3,2,1,0:T(8,128)(2,1)S(1)} %bitcast.57), channel_id=1, source_target_pairs={{0,256},{2,258},{256,0},{258,2},{1,257},{3,259},{257,1},{259,3},{4... | collective-permute-start | bytes 589832 | tf_op jit(solution)/shard_map/ppermute | solution.py:250
  67.9 0.7 pad_maximum_fusion.4
  68.6 4.0 %collective-permute-start.3 = (bf16[2,2,3,2,16,256]{5,4,3,2,1,0:T(8,128)(2,1)}, bf16[2,2,3,2,16,256]{5,4,3,2,1,0:T(8,128)(2,1)S(1)}, u32[]{:S(2)}, u32[]{:S(2)}) collective-permute-start(bf16[2,2,3,2,16,256]{5,4,3,2,1,0:T(8,128)(2,1)} %bitcast.27), channel_id=1, source_target_pairs={{0,258},{2,256},{256,2},{258,0},{1,259},{3,257},{257,3},{259,1},{4... | collective-permute-start | bytes 589832 | tf_op jit(solution)/shard_map/ppermute | solution.py:250
  73.2 0.8 concatenate.3.at_ref
  74.0 1.4 %collective-permute-done.2.refs_2_ = bf16[2,2,3,2,16,256]{5,4,3,2,1,0:T(8,128)(2,1)S(1)} collective-permute-done((bf16[2,2,3,2,16,256]{5,4,3,2,1,0:T(8,128)(2,1)S(1)}, bf16[2,2,3,2,16,256]{5,4,3,2,1,0:T(8,128)(2,1)S(1)}, u32[]{:S(2)}, u32[]{:S(2)}) %collective-permute-start.2) | collective-permute-done | bytes 196640 | tf_op jit(solution)/shard_map/ppermute | solution.py:250
  75.4 3.3 %collective-permute-done.3.refs_3_ = bf16[2,2,3,2,16,256]{5,4,3,2,1,0:T(8,128)(2,1)S(1)} collective-permute-done((bf16[2,2,3,2,16,256]{5,4,3,2,1,0:T(8,128)(2,1)}, bf16[2,2,3,2,16,256]{5,4,3,2,1,0:T(8,128)(2,1)S(1)}, u32[]{:S(2)}, u32[]{:S(2)}) %collective-permute-start.3) | collective-permute-done | bytes 196640 | tf_op jit(solution)/shard_map/ppermute | solution.py:250
  78.7 0.8 shard_map.59
  79.5 0.9 shard_map.61.p_ref
  80.4 1.9 %shard_map.62 = f32[16,6,128]{2,1,0:T(8,128)S(1)} custom-call(bf16[192,1024]{1,0:T(8,128)(2,1)S(1)} %get-tuple-element.7.left_ref, bf16[192,1024]{1,0:T(8,128)(2,1)S(1)} %get-tuple-element.8.flip_ref, bf16[192,1024]{1,0:T(8,128)(2,1)S(1)} %get-tuple-element.9.val_ref, f32[192,1024]{1,0:T(8,128)S(1)} %shard_map.61.p_ref, ...), custom_call_target="tpu_custom_call" | custom-call | flops 800000000 | bytes 2000000 | tf_op jit(solution)/shard_map/pallas_call | solution.py:191
  82.3 10.6 %all_to_all.20.got_ref = f32[16,6,128]{2,1,0:T(8,128)S(1)} all-to-all(f32[16,6,128]{2,1,0:T(8,128)S(1)} %shard_map.62), channel_id=1, replica_groups=mesh['xl'=2,'z'=8,'yh'=4,'yl'=2,'xh'=2,'c'=2] {'xl','yl','xh','c'}, dimensions={0} | all-to-all | bytes 98304 | tf_op jit(solution)/shard_map/all_to_all | solution.py:261
  92.8 1.6 %shard_map.63 = (f32[4,6,2,64]{3,2,1,0:T(2,128)}, bf16[32,24,128]{2,1,0:T(8,128)(2,1)S(1)}) custom-call(s32[16]{0:T(128)S(1)} %concatenate.3.at_ref, f32[16,6,128]{2,1,0:T(8,128)S(1)} %all_to_all.20.got_ref), custom_call_target="tpu_custom_call" | custom-call | tf_op jit(solution)/shard_map/pallas_call | solution.py:265
  94.4 19.0 %all_to_all.21.came_ref = bf16[32,24,128]{2,1,0:T(8,128)(2,1)S(1)} all-to-all(bf16[32,24,128]{2,1,0:T(8,128)(2,1)S(1)} %get-tuple-element.11), channel_id=1, replica_groups=mesh['xl'=2,'z'=8,'yh'=4,'yl'=2,'xh'=2,'c'=2] {'z','yh'}, dimensions={0} | all-to-all | bytes 393216 | tf_op jit(solution)/shard_map/all_to_all | solution.py:273
  113.4 1.2 %shard_map.64 = f32[4,6,2,64]{3,2,1,0:T(2,128)} custom-call(s32[16]{0:T(128)S(1)} %concatenate.3.at_ref, bf16[32,24,128]{2,1,0:T(8,128)(2,1)S(1)} %all_to_all.21.came_ref), custom_call_target="tpu_custom_call" | custom-call | tf_op jit(solution)/shard_map/pallas_call | solution.py:274
  (24 shorter events, 0.9 us)
Async XLA Ops:
  0.6 9.7 %all-to-all-start = ((bf16[8,8,256]{2,1,0:T(8,128)(2,1)}), bf16[8,8,256]{2,1,0:T(8,128)(2,1)S(1)}, u32[]{:S(2)}, u32[]{:S(2)}) async-start(bf16[8,8,256]{2,1,0:T(8,128)(2,1)} %bitcast.58), calls=%async_computation | async-start | bytes 65536 | tf_op jit(solution)/shard_map/all_to_all | solution.py:230
  11.4 16.6 %copy-start = (bf16[4,6,2,16,256]{4,3,2,1,0:T(8,128)(2,1)S(1)}, bf16[4,6,2,16,256]{4,3,2,1,0:T(8,128)(2,1)}, u32[]{:S(2)}) copy-start(bf16[4,6,2,16,256]{4,3,2,1,0:T(8,128)(2,1)} %param.5) | copy-start | bytes 1179652
  11.4 16.6 %copy-start.1 = (bf16[4,6,2,16,256]{4,3,2,1,0:T(8,128)(2,1)S(1)}, bf16[4,6,2,16,256]{4,3,2,1,0:T(8,128)(2,1)}, u32[]{:S(2)}) copy-start(bf16[4,6,2,16,256]{4,3,2,1,0:T(8,128)(2,1)} %param.4) | copy-start | bytes 1179652
  11.4 48.3 %all-to-all-start.1 = ((bf16[64,8,1152]{2,1,0:T(8,128)(2,1)}), bf16[64,8,1152]{2,1,0:T(8,128)(2,1)S(1)}, u32[]{:S(2)}, u32[]{:S(2)}) async-start(bf16[64,8,1152]{2,1,0:T(8,128)(2,1)} %shard_map.60), calls=%async_computation.1 | async-start | bytes 2359296 | tf_op jit(solution)/shard_map/all_to_all | solution.py:232
  28.2 33.7 %collective-permute-start = (bf16[2,4,3,2,16,256]{5,4,3,2,1,0:T(8,128)(2,1)S(1)}, bf16[2,4,3,2,16,256]{5,4,3,2,1,0:T(8,128)(2,1)S(1)}, u32[]{:S(2)}, u32[]{:S(2)}) collective-permute-start(bf16[2,4,3,2,16,256]{5,4,3,2,1,0:T(8,128)(2,1)S(1)} %pad_maximum_fusion), channel_id=1, source_target_pairs={{0,1},{1,0},{2,3},{3,2},{4,5},{5,4},{6,7},{7,6},{8,9},{9,8},{10,11... | collective-permute-start | bytes 1179656 | tf_op jit(solution)/shard_map/ppermute | solution.py:241
  59.8 5.4 %copy-start.4 = (bf16[1,3,2,16,256]{4,3,2,1,0:T(8,128)(2,1)S(1)}, bf16[1,3,2,16,256]{4,3,2,1,0:T(8,128)(2,1)}, u32[]{:S(2)}) copy-start(bf16[1,3,2,16,256]{4,3,2,1,0:T(8,128)(2,1)} %get-tuple-element.19) | copy-start | bytes 147460
  59.8 5.4 %copy-start.5 = (bf16[1,3,2,16,256]{4,3,2,1,0:T(8,128)(2,1)S(1)}, bf16[1,3,2,16,256]{4,3,2,1,0:T(8,128)(2,1)}, u32[]{:S(2)}) copy-start(bf16[1,3,2,16,256]{4,3,2,1,0:T(8,128)(2,1)} %get-tuple-element.39) | copy-start | bytes 147460
  59.8 8.1 %copy-start.2 = (bf16[1,3,2,16,256]{4,3,2,1,0:T(8,128)(2,1)S(1)}, bf16[1,3,2,16,256]{4,3,2,1,0:T(8,128)(2,1)}, u32[]{:S(2)}) copy-start(bf16[1,3,2,16,256]{4,3,2,1,0:T(8,128)(2,1)} %get-tuple-element.18) | copy-start | bytes 147460
  59.8 8.1 %copy-start.3 = (bf16[1,3,2,16,256]{4,3,2,1,0:T(8,128)(2,1)S(1)}, bf16[1,3,2,16,256]{4,3,2,1,0:T(8,128)(2,1)}, u32[]{:S(2)}) copy-start(bf16[1,3,2,16,256]{4,3,2,1,0:T(8,128)(2,1)} %get-tuple-element.40) | copy-start | bytes 147460
  59.8 20.6 %collective-permute-start.4 = (bf16[512,1152]{1,0:T(8,128)(2,1)S(1)}, bf16[512,1152]{1,0:T(8,128)(2,1)S(1)}, u32[]{:S(2)}, u32[]{:S(2)}) collective-permute-start(bf16[512,1152]{1,0:T(8,128)(2,1)S(1)} %bitcast.49), channel_id=1, source_target_pairs={{0,1},{1,0},{2,3},{3,2},{4,5},{5,4},{6,7},{7,6},{8,9},{9,8},{10,11... | collective-permute-start | bytes 3538952 | tf_op jit(solution)/shard_map/ppermute | solution.py:182
  62.0 12.0 %collective-permute-start.1 = (bf16[2,2,3,2,16,256]{5,4,3,2,1,0:T(8,128)(2,1)S(1)}, bf16[2,2,3,2,16,256]{5,4,3,2,1,0:T(8,128)(2,1)S(1)}, u32[]{:S(2)}, u32[]{:S(2)}) collective-permute-start(bf16[2,2,3,2,16,256]{5,4,3,2,1,0:T(8,128)(2,1)S(1)} %bitcast.56), channel_id=1, source_target_pairs={{0,2},{2,0},{256,258},{258,256},{1,3},{3,1},{257,259},{259,257},{4... | collective-permute-start | bytes 589832 | tf_op jit(solution)/shard_map/ppermute | solution.py:250
  65.2 10.2 %collective-permute-start.2 = (bf16[2,2,3,2,16,256]{5,4,3,2,1,0:T(8,128)(2,1)S(1)}, bf16[2,2,3,2,16,256]{5,4,3,2,1,0:T(8,128)(2,1)S(1)}, u32[]{:S(2)}, u32[]{:S(2)}) collective-permute-start(bf16[2,2,3,2,16,256]{5,4,3,2,1,0:T(8,128)(2,1)S(1)} %bitcast.57), channel_id=1, source_target_pairs={{0,256},{2,258},{256,0},{258,2},{1,257},{3,259},{257,1},{259,3},{4... | collective-permute-start | bytes 589832 | tf_op jit(solution)/shard_map/ppermute | solution.py:250
  68.6 10.0 %collective-permute-start.3 = (bf16[2,2,3,2,16,256]{5,4,3,2,1,0:T(8,128)(2,1)}, bf16[2,2,3,2,16,256]{5,4,3,2,1,0:T(8,128)(2,1)S(1)}, u32[]{:S(2)}, u32[]{:S(2)}) collective-permute-start(bf16[2,2,3,2,16,256]{5,4,3,2,1,0:T(8,128)(2,1)} %bitcast.27), channel_id=1, source_target_pairs={{0,258},{2,256},{256,2},{258,0},{1,259},{3,257},{257,3},{259,1},{4... | collective-permute-start | bytes 589832 | tf_op jit(solution)/shard_map/ppermute | solution.py:250

commit v8 on v7

--- a/solution.py
+++ b/solution.py
@@ -36,7 +36,7 @@
             out_ref[0, :, lane : lane + BLK] = w_ref[4 * xl + block // 2, :, lanes]
             lane += BLK
     piece = out_ref[0]
-    for slot in range(1, 64):
+    for slot in range(1, 16):
         out_ref[slot, :, :] = piece
 
 
@@ -44,11 +44,31 @@
     vm = pl.BlockSpec(memory_space=pltpu.VMEM)
     return pl.pallas_call(
         fan,
-        out_shape=jax.ShapeDtypeStruct((64, 8, (2 * SENT - 1) * BLK), BF),
+        out_shape=jax.ShapeDtypeStruct((16, 8, (2 * SENT - 1) * BLK), BF),
         in_specs=[pl.BlockSpec(memory_space=pltpu.SMEM), vm],
         out_specs=vm,
         compiler_params=pltpu.CompilerParams(vmem_limit_bytes=16 << 20),
     )(at, w)
+
+
+def weave(at_ref, *refs):
+    pieces, out_ref = refs[:4], refs[4]
+    for s in range(4):
+        zl = at_ref[16] ^ (s // 2)
+        yl = at_ref[3] ^ (s % 2)
+        for i in range(16):
+            out_ref[(i // 4) * 16 + zl * 8 + (i % 4) * 2 + yl, :, :] = pieces[s][i]
+
+
+def woven(at, pieces):
+    vm = pl.BlockSpec(memory_space=pltpu.VMEM)
+    return pl.pallas_call(
+        weave,
+        out_shape=jax.ShapeDtypeStruct((64, 8, (2 * SENT - 1) * BLK), BF),
+        in_specs=[pl.BlockSpec(memory_space=pltpu.SMEM)] + [vm] * 4,
+        out_specs=vm,
+        compiler_params=pltpu.CompilerParams(vmem_limit_bytes=16 << 20),
+    )(at, *pieces)
 
 
 def assemble(at_ref, *refs):
@@ -226,12 +246,14 @@
 
 def local(cond, val, screened, k_plus):
     xl, yl, core = lax.axis_index("xl"), lax.axis_index("yl"), lax.axis_index("c")
-    z, yh = lax.axis_index("z"), lax.axis_index("yh")
+    zh, zl, yh = lax.axis_index("zh"), lax.axis_index("zl"), lax.axis_index("yh")
+    z = zh * 2 + zl
     w = lax.all_to_all(screened.reshape(8, 8, 256), ("xl", "xh", "c"), 0, 0)
-    w = fanned((z // 2).astype(jnp.int32).reshape(1), w)
-    w = lax.all_to_all(w, ("z", "yh", "yl"), 0, 0)
-    own = w.reshape(NG // 2, (2 * SENT - 1) * BLK)
-
+    w = fanned(zh.astype(jnp.int32).reshape(1), w)
+    w = lax.all_to_all(w, ("zh", "yh"), 0, 0)
+    classes = [w]
+    for s in range(1, 4):
+        classes.append(lax.ppermute(w, ("zl", "yl"), [(i, i ^ s) for i in range(4)]))
     x = xl * 2 + lax.axis_index("xh")
 
     slots = [pairs.reshape(4, 2, 3, 2, PAIR, 256) for pairs in (cond, val)]
@@ -255,8 +277,9 @@
     other = xl ^ ((here + row_step) // 32 % 2)
     begin = (6 * yl - col_step + 12) % 12
     source = (here - row_step) % 32
-    at = jnp.concatenate([jnp.stack([x, core, xl, yl]), other, begin, source]).astype(jnp.int32)
+    at = jnp.concatenate([jnp.stack([x, core, xl, yl]), other, begin, source, zl[None]]).astype(jnp.int32)
     left, flipped, right = assembled(at, pieces)
+    own = woven(at, classes).reshape(NG // 2, (2 * SENT - 1) * BLK)
     slots = contracted(left, flipped, right, own)
     got = lax.all_to_all(slots, ("xl", "yl", "xh", "c"), 0, 0)
     vm = pl.BlockSpec(memory_space=pltpu.VMEM)
@@ -270,7 +293,7 @@
         scratch_shapes=[pltpu.VMEM((Q * KQ, 128), F32)],
         compiler_params=pltpu.CompilerParams(vmem_limit_bytes=8 << 20),
     )(at, got)
-    came = lax.all_to_all(pay, ("z", "yh"), 0, 0)
+    came = lax.all_to_all(pay, ("zh", "zl", "yh"), 0, 0)
     back = pl.pallas_call(
         pick_back,
         out_shape=out,
@@ -282,8 +305,8 @@
 
 
 def solution(mesh):
-    fine = Mesh(mesh.devices.reshape(2, 8, 4, 2, 2, 2), ("xl", "z", "yh", "yl", "xh", "c"))
-    ka, ga = ("xl", "z", "yh", "yl"), ("xh", "c")
+    fine = Mesh(mesh.devices.reshape(2, 4, 2, 4, 2, 2, 2), ("xl", "zh", "zl", "yh", "yl", "xh", "c"))
+    ka, ga = ("xl", "zh", "zl", "yh", "yl"), ("xh", "c")
     in_specs = (
         P(None, ka, None, None, ga),
         P(None, ka, None, None, ga),

time: 115 us -> 112 us (0.974)
  starting transfers between devices: 34.7 us -> 43.1 us
  waiting for transfers between devices: 37.3 us -> 29 us
  blocking collectives: 29.6 us -> 28 us
  other arithmetic: 3.09 us -> 1.81 us
    all_to_all x1, waiting for transfers between devices: 27.3 us -> 10.6 us  [local(): w = lax.all_to_all(w, ('zh', 'yh'), 0, 0)]
    ppermute x0 -> x3, starting transfers between devices: none -> 9.2 us  [local(): lax.ppermute(w, ('zl', 'yl'), [(i, i ^ s) for i in range(4)])]
    ppermute x0 -> x3, waiting for transfers between devices: none -> 7.24 us  [local(): lax.ppermute(w, ('zl', 'yl'), [(i, i ^ s) for i in range(4)])]
    ppermute x3, waiting for transfers between devices: 4.66 us -> 5.82 us  [local(): piece = lax.ppermute(piece, ('xl', 'xh'), [(i, i ^ s) for i in range(4)])]
  transfers between devices with their start and end apart: 7 -> 10, of which waited for: 4 -> 7; matrix products, arithmetic and copies ran while one was open for 4% -> 3% of each run, Pallas kernels for 1% -> 2%
where the time goes in v8:
time: 112 us
  starting transfers between devices  43.1 us (38%)
  waiting for transfers between devices  29 us (26%)
  blocking collectives  28 us (25%)
  Pallas kernels  7.75 us (7%)
  other arithmetic  1.81 us (2%)
  local copies, waits for them, and re-layouts  1.26 us (1%)
    all_to_all x1, blocking collectives, local(): came = lax.all_to_all(pay, ('zh', 'zl', 'yh'), 0, 0)  18.5 us
    all_to_all x1, starting transfers between devices, local(): w = lax.all_to_all(w, ('zh', 'yh'), 0, 0)  15.9 us
    all_to_all x1, waiting for transfers between devices, local(): w = lax.all_to_all(w, ('zh', 'yh'), 0, 0)  10.6 us
    ppermute x3, starting transfers between devices, local(): piece = lax.ppermute(piece, ('xl', 'xh'), [(i, i ^ s) for i in range(4)])  9.82 us
    all_to_all x1, blocking collectives, local(): got = lax.all_to_all(slots, ('xl', 'yl', 'xh', 'c'), 0, 0)  9.49 us
    ppermute x3, starting transfers between devices, local(): lax.ppermute(w, ('zl', 'yl'), [(i, i ^ s) for i in range(4)])  9.2 us
    ppermute x3, waiting for transfers between devices, local(): lax.ppermute(w, ('zl', 'yl'), [(i, i ^ s) for i in range(4)])  7.24 us
    ppermute x3, waiting for transfers between devices, local(): piece = lax.ppermute(piece, ('xl', 'xh'), [(i, i ^ s) for i in range(4)])  5.82 us
  transfers between devices with their start and end apart: 10, of which 7 were waited for; matrix products, arithmetic and copies ran while one was open for 3% of the time, Pallas kernels for 2%

profile of v8, /device:TPU:16, one launch (start us, length us, event | category | flops | bytes accessed | tf_op | source)
XLA Modules:
  0.0 111.8 jit_solution(3057747659243124626)
XLA Ops:
  0.6 4.3 %all-to-all-start = ((bf16[8,8,256]{2,1,0:T(8,128)(2,1)}), bf16[8,8,256]{2,1,0:T(8,128)(2,1)S(1)}, u32[]{:S(2)}, u32[]{:S(2)}) async-start(bf16[8,8,256]{2,1,0:T(8,128)(2,1)} %bitcast.60), calls=%async_computation | async-start | bytes 65536 | tf_op jit(solution)/shard_map/all_to_all | solution.py:251
  4.9 5.4 %all-to-all-done.w_ref = bf16[8,8,256]{2,1,0:T(8,128)(2,1)S(1)} async-done(((bf16[8,8,256]{2,1,0:T(8,128)(2,1)}), bf16[8,8,256]{2,1,0:T(8,128)(2,1)S(1)}, u32[]{:S(2)}, u32[]{:S(2)}) %all-to-all-start) | async-done | bytes 32800 | tf_op jit(solution)/shard_map/all_to_all | solution.py:251
  11.1 15.9 %all-to-all-start.1 = ((bf16[16,8,1152]{2,1,0:T(8,128)(2,1)}), bf16[16,8,1152]{2,1,0:T(8,128)(2,1)S(1)}, u32[]{:S(2)}, u32[]{:S(2)}) async-start(bf16[16,8,1152]{2,1,0:T(8,128)(2,1)} %shard_map.60), calls=%async_computation.1 | async-start | bytes 589824 | tf_op jit(solution)/shard_map/all_to_all | solution.py:253
  27.0 1.0 dynamic-slice_bitcast_fusion
  28.1 1.9 %collective-permute-start = (bf16[2,4,3,2,16,256]{5,4,3,2,1,0:T(8,128)(2,1)S(1)}, bf16[2,4,3,2,16,256]{5,4,3,2,1,0:T(8,128)(2,1)S(1)}, u32[]{:S(2)}, u32[]{:S(2)}) collective-permute-start(bf16[2,4,3,2,16,256]{5,4,3,2,1,0:T(8,128)(2,1)S(1)} %pad_maximum_fusion), channel_id=1, source_target_pairs={{0,1},{1,0},{2,3},{3,2},{4,5},{5,4},{6,7},{7,6},{8,9},{9,8},{10,11... | collective-permute-start | bytes 1179656 | tf_op jit(solution)/shard_map/ppermute | solution.py:263
  30.8 10.6 %all-to-all-done.1.refs_0_ = bf16[16,8,1152]{2,1,0:T(8,128)(2,1)S(1)} async-done(((bf16[16,8,1152]{2,1,0:T(8,128)(2,1)}), bf16[16,8,1152]{2,1,0:T(8,128)(2,1)S(1)}, u32[]{:S(2)}, u32[]{:S(2)}) %all-to-all-start.1) | async-done | bytes 294944 | tf_op jit(solution)/shard_map/all_to_all | solution.py:253
  41.4 2.0 %collective-permute-start.6 = (bf16[16,8,1152]{2,1,0:T(8,128)(2,1)S(1)}, bf16[16,8,1152]{2,1,0:T(8,128)(2,1)S(1)}, u32[]{:S(2)}, u32[]{:S(2)}) collective-permute-start(bf16[16,8,1152]{2,1,0:T(8,128)(2,1)S(1)} %all-to-all-done.1.refs_0_), channel_id=1, source_target_pairs={{0,36},{4,32},{32,4},{36,0},{1,37},{5,33},{33,5},{37,1},{2,38},{6,... | collective-permute-start | bytes 884744 | tf_op jit(solution)/shard_map/ppermute | solution.py:256
  43.5 3.3 %collective-permute-start.5 = (bf16[16,8,1152]{2,1,0:T(8,128)(2,1)S(1)}, bf16[16,8,1152]{2,1,0:T(8,128)(2,1)S(1)}, u32[]{:S(2)}, u32[]{:S(2)}) collective-permute-start(bf16[16,8,1152]{2,1,0:T(8,128)(2,1)S(1)} %all-to-all-done.1.refs_0_), channel_id=1, source_target_pairs={{0,32},{4,36},{32,0},{36,4},{1,33},{5,37},{33,1},{37,5},{2,34},{6,... | collective-permute-start | bytes 884744 | tf_op jit(solution)/shard_map/ppermute | solution.py:256
  46.8 3.9 %collective-permute-start.4 = (bf16[16,8,1152]{2,1,0:T(8,128)(2,1)S(1)}, bf16[16,8,1152]{2,1,0:T(8,128)(2,1)S(1)}, u32[]{:S(2)}, u32[]{:S(2)}) collective-permute-start(bf16[16,8,1152]{2,1,0:T(8,128)(2,1)S(1)} %all-to-all-done.1.refs_0_), channel_id=1, source_target_pairs={{0,4},{4,0},{32,36},{36,32},{1,5},{5,1},{33,37},{37,33},{2,6},{6,2... | collective-permute-start | bytes 884744 | tf_op jit(solution)/shard_map/ppermute | solution.py:256
  51.6 2.4 %collective-permute-done.6.refs_3_ = bf16[16,8,1152]{2,1,0:T(8,128)(2,1)S(1)} collective-permute-done((bf16[16,8,1152]{2,1,0:T(8,128)(2,1)S(1)}, bf16[16,8,1152]{2,1,0:T(8,128)(2,1)S(1)}, u32[]{:S(2)}, u32[]{:S(2)}) %collective-permute-start.6) | collective-permute-done | bytes 294944 | tf_op jit(solution)/shard_map/ppermute | solution.py:256
  54.0 4.8 %collective-permute-done.5.refs_2_ = bf16[16,8,1152]{2,1,0:T(8,128)(2,1)S(1)} collective-permute-done((bf16[16,8,1152]{2,1,0:T(8,128)(2,1)S(1)}, bf16[16,8,1152]{2,1,0:T(8,128)(2,1)S(1)}, u32[]{:S(2)}, u32[]{:S(2)}) %collective-permute-start.5) | collective-permute-done | bytes 294944 | tf_op jit(solution)/shard_map/ppermute | solution.py:256
  59.5 1.9 %collective-permute-start.7 = (bf16[512,1152]{1,0:T(8,128)(2,1)S(1)}, bf16[512,1152]{1,0:T(8,128)(2,1)S(1)}, u32[]{:S(2)}, u32[]{:S(2)}) collective-permute-start(bf16[512,1152]{1,0:T(8,128)(2,1)S(1)} %bitcast.50), channel_id=1, source_target_pairs={{0,1},{1,0},{2,3},{3,2},{4,5},{5,4},{6,7},{7,6},{8,9},{9,8},{10,11... | collective-permute-start | bytes 3538952 | tf_op jit(solution)/shard_map/ppermute | solution.py:202
  61.7 3.2 %collective-permute-start.1 = (bf16[2,2,3,2,16,256]{5,4,3,2,1,0:T(8,128)(2,1)S(1)}, bf16[2,2,3,2,16,256]{5,4,3,2,1,0:T(8,128)(2,1)S(1)}, u32[]{:S(2)}, u32[]{:S(2)}) collective-permute-start(bf16[2,2,3,2,16,256]{5,4,3,2,1,0:T(8,128)(2,1)S(1)} %bitcast.57), channel_id=1, source_target_pairs={{0,2},{2,0},{256,258},{258,256},{1,3},{3,1},{257,259},{259,257},{4... | collective-permute-start | bytes 589832 | tf_op jit(solution)/shard_map/ppermute | solution.py:272
  64.9 2.7 %collective-permute-start.2 = (bf16[2,2,3,2,16,256]{5,4,3,2,1,0:T(8,128)(2,1)S(1)}, bf16[2,2,3,2,16,256]{5,4,3,2,1,0:T(8,128)(2,1)S(1)}, u32[]{:S(2)}, u32[]{:S(2)}) collective-permute-start(bf16[2,2,3,2,16,256]{5,4,3,2,1,0:T(8,128)(2,1)S(1)} %bitcast.58), channel_id=1, source_target_pairs={{0,256},{2,258},{256,0},{258,2},{1,257},{3,259},{257,1},{259,3},{4... | collective-permute-start | bytes 589832 | tf_op jit(solution)/shard_map/ppermute | solution.py:272
  67.6 4.0 %collective-permute-start.3 = (bf16[2,2,3,2,16,256]{5,4,3,2,1,0:T(8,128)(2,1)S(1)}, bf16[2,2,3,2,16,256]{5,4,3,2,1,0:T(8,128)(2,1)S(1)}, u32[]{:S(2)}, u32[]{:S(2)}) collective-permute-start(bf16[2,2,3,2,16,256]{5,4,3,2,1,0:T(8,128)(2,1)S(1)} %bitcast.59), channel_id=1, source_target_pairs={{0,258},{2,256},{256,2},{258,0},{1,259},{3,257},{257,3},{259,1},{4... | collective-permute-start | bytes 589832 | tf_op jit(solution)/shard_map/ppermute | solution.py:272
  71.6 1.2 %collective-permute-done.1.refs_1_ = bf16[2,2,3,2,16,256]{5,4,3,2,1,0:T(8,128)(2,1)S(1)} collective-permute-done((bf16[2,2,3,2,16,256]{5,4,3,2,1,0:T(8,128)(2,1)S(1)}, bf16[2,2,3,2,16,256]{5,4,3,2,1,0:T(8,128)(2,1)S(1)}, u32[]{:S(2)}, u32[]{:S(2)}) %collective-permute-start.1) | collective-permute-done | bytes 196640 | tf_op jit(solution)/shard_map/ppermute | solution.py:272
  72.8 2.2 %collective-permute-done.2.refs_2_ = bf16[2,2,3,2,16,256]{5,4,3,2,1,0:T(8,128)(2,1)S(1)} collective-permute-done((bf16[2,2,3,2,16,256]{5,4,3,2,1,0:T(8,128)(2,1)S(1)}, bf16[2,2,3,2,16,256]{5,4,3,2,1,0:T(8,128)(2,1)S(1)}, u32[]{:S(2)}, u32[]{:S(2)}) %collective-permute-start.2) | collective-permute-done | bytes 196640 | tf_op jit(solution)/shard_map/ppermute | solution.py:272
  75.1 2.4 %collective-permute-done.3.refs_3_ = bf16[2,2,3,2,16,256]{5,4,3,2,1,0:T(8,128)(2,1)S(1)} collective-permute-done((bf16[2,2,3,2,16,256]{5,4,3,2,1,0:T(8,128)(2,1)S(1)}, bf16[2,2,3,2,16,256]{5,4,3,2,1,0:T(8,128)(2,1)S(1)}, u32[]{:S(2)}, u32[]{:S(2)}) %collective-permute-start.3) | collective-permute-done | bytes 196640 | tf_op jit(solution)/shard_map/ppermute | solution.py:272
  78.2 0.9 shard_map.62.p_ref
  79.1 1.9 %shard_map.63 = f32[16,6,128]{2,1,0:T(8,128)S(1)} custom-call(bf16[192,1024]{1,0:T(8,128)(2,1)S(1)} %get-tuple-element.7.left_ref, bf16[192,1024]{1,0:T(8,128)(2,1)S(1)} %get-tuple-element.8.flip_ref, bf16[192,1024]{1,0:T(8,128)(2,1)S(1)} %get-tuple-element.9.val_ref, f32[192,1024]{1,0:T(8,128)S(1)} %shard_map.62.p_ref, ...), custom_call_target="tpu_custom_call" | custom-call | flops 800000000 | bytes 2000000 | tf_op jit(solution)/shard_map/pallas_call | solution.py:211
  81.0 9.5 %all_to_all.20.got_ref = f32[16,6,128]{2,1,0:T(8,128)S(1)} all-to-all(f32[16,6,128]{2,1,0:T(8,128)S(1)} %shard_map.63), channel_id=1, replica_groups=mesh['xl'=2,'zh'=4,'zl'=2,'yh'=4,'yl'=2,'xh'=2,'c'=2] {'xl','yl','xh','c'}, dimensions={0} | all-to-all | bytes 98304 | tf_op jit(solution)/shard_map/all_to_all | solution.py:284
  90.5 1.6 %shard_map.64 = (f32[4,6,2,64]{3,2,1,0:T(2,128)}, bf16[32,24,128]{2,1,0:T(8,128)(2,1)S(1)}) custom-call(s32[17]{0:T(128)S(1)} %concatenate.3.at_ref, f32[16,6,128]{2,1,0:T(8,128)S(1)} %all_to_all.20.got_ref), custom_call_target="tpu_custom_call" | custom-call | tf_op jit(solution)/shard_map/pallas_call | solution.py:288
  92.1 18.5 %all_to_all.21.came_ref = bf16[32,24,128]{2,1,0:T(8,128)(2,1)S(1)} all-to-all(bf16[32,24,128]{2,1,0:T(8,128)(2,1)S(1)} %get-tuple-element.11), channel_id=1, replica_groups=mesh['xl'=2,'zh'=4,'zl'=2,'yh'=4,'yl'=2,'xh'=2,'c'=2] {'zh','zl','yh'}, dimensions={0} | all-to-all | bytes 393216 | tf_op jit(solution)/shard_map/all_to_all | solution.py:296
  110.6 1.2 %shard_map.65 = f32[4,6,2,64]{3,2,1,0:T(2,128)} custom-call(s32[17]{0:T(128)S(1)} %concatenate.3.at_ref, bf16[32,24,128]{2,1,0:T(8,128)(2,1)S(1)} %all_to_all.21.came_ref), custom_call_target="tpu_custom_call" | custom-call | tf_op jit(solution)/shard_map/pallas_call | solution.py:297
  (23 shorter events, 4.2 us)
Async XLA Ops:
  0.6 9.7 %all-to-all-start = ((bf16[8,8,256]{2,1,0:T(8,128)(2,1)}), bf16[8,8,256]{2,1,0:T(8,128)(2,1)S(1)}, u32[]{:S(2)}, u32[]{:S(2)}) async-start(bf16[8,8,256]{2,1,0:T(8,128)(2,1)} %bitcast.60), calls=%async_computation | async-start | bytes 65536 | tf_op jit(solution)/shard_map/all_to_all | solution.py:251
  11.1 30.4 %all-to-all-start.1 = ((bf16[16,8,1152]{2,1,0:T(8,128)(2,1)}), bf16[16,8,1152]{2,1,0:T(8,128)(2,1)S(1)}, u32[]{:S(2)}, u32[]{:S(2)}) async-start(bf16[16,8,1152]{2,1,0:T(8,128)(2,1)} %shard_map.60), calls=%async_computation.1 | async-start | bytes 589824 | tf_op jit(solution)/shard_map/all_to_all | solution.py:253
  28.1 33.4 %collective-permute-start = (bf16[2,4,3,2,16,256]{5,4,3,2,1,0:T(8,128)(2,1)S(1)}, bf16[2,4,3,2,16,256]{5,4,3,2,1,0:T(8,128)(2,1)S(1)}, u32[]{:S(2)}, u32[]{:S(2)}) collective-permute-start(bf16[2,4,3,2,16,256]{5,4,3,2,1,0:T(8,128)(2,1)S(1)} %pad_maximum_fusion), channel_id=1, source_target_pairs={{0,1},{1,0},{2,3},{3,2},{4,5},{5,4},{6,7},{7,6},{8,9},{9,8},{10,11... | collective-permute-start | bytes 1179656 | tf_op jit(solution)/shard_map/ppermute | solution.py:263
  41.4 12.6 %collective-permute-start.6 = (bf16[16,8,1152]{2,1,0:T(8,128)(2,1)S(1)}, bf16[16,8,1152]{2,1,0:T(8,128)(2,1)S(1)}, u32[]{:S(2)}, u32[]{:S(2)}) collective-permute-start(bf16[16,8,1152]{2,1,0:T(8,128)(2,1)S(1)} %all-to-all-done.1.refs_0_), channel_id=1, source_target_pairs={{0,36},{4,32},{32,4},{36,0},{1,37},{5,33},{33,5},{37,1},{2,38},{6,... | collective-permute-start | bytes 884744 | tf_op jit(solution)/shard_map/ppermute | solution.py:256
  43.5 15.4 %collective-permute-start.5 = (bf16[16,8,1152]{2,1,0:T(8,128)(2,1)S(1)}, bf16[16,8,1152]{2,1,0:T(8,128)(2,1)S(1)}, u32[]{:S(2)}, u32[]{:S(2)}) collective-permute-start(bf16[16,8,1152]{2,1,0:T(8,128)(2,1)S(1)} %all-to-all-done.1.refs_0_), channel_id=1, source_target_pairs={{0,32},{4,36},{32,0},{36,4},{1,33},{5,37},{33,1},{37,5},{2,34},{6,... | collective-permute-start | bytes 884744 | tf_op jit(solution)/shard_map/ppermute | solution.py:256
  46.8 12.1 %collective-permute-start.4 = (bf16[16,8,1152]{2,1,0:T(8,128)(2,1)S(1)}, bf16[16,8,1152]{2,1,0:T(8,128)(2,1)S(1)}, u32[]{:S(2)}, u32[]{:S(2)}) collective-permute-start(bf16[16,8,1152]{2,1,0:T(8,128)(2,1)S(1)} %all-to-all-done.1.refs_0_), channel_id=1, source_target_pairs={{0,4},{4,0},{32,36},{36,32},{1,5},{5,1},{33,37},{37,33},{2,6},{6,2... | collective-permute-start | bytes 884744 | tf_op jit(solution)/shard_map/ppermute | solution.py:256
  51.6 9.8 %copy-start = (bf16[4,6,2,16,256]{4,3,2,1,0:T(8,128)(2,1)S(1)}, bf16[4,6,2,16,256]{4,3,2,1,0:T(8,128)(2,1)}, u32[]{:S(2)}) copy-start(bf16[4,6,2,16,256]{4,3,2,1,0:T(8,128)(2,1)} %param.5) | copy-start | bytes 1179652
  51.6 9.8 %copy-start.1 = (bf16[4,6,2,16,256]{4,3,2,1,0:T(8,128)(2,1)S(1)}, bf16[4,6,2,16,256]{4,3,2,1,0:T(8,128)(2,1)}, u32[]{:S(2)}) copy-start(bf16[4,6,2,16,256]{4,3,2,1,0:T(8,128)(2,1)} %param.4) | copy-start | bytes 1179652
  59.5 19.6 %collective-permute-start.7 = (bf16[512,1152]{1,0:T(8,128)(2,1)S(1)}, bf16[512,1152]{1,0:T(8,128)(2,1)S(1)}, u32[]{:S(2)}, u32[]{:S(2)}) collective-permute-start(bf16[512,1152]{1,0:T(8,128)(2,1)S(1)} %bitcast.50), channel_id=1, source_target_pairs={{0,1},{1,0},{2,3},{3,2},{4,5},{5,4},{6,7},{7,6},{8,9},{9,8},{10,11... | collective-permute-start | bytes 3538952 | tf_op jit(solution)/shard_map/ppermute | solution.py:202
  61.7 11.2 %collective-permute-start.1 = (bf16[2,2,3,2,16,256]{5,4,3,2,1,0:T(8,128)(2,1)S(1)}, bf16[2,2,3,2,16,256]{5,4,3,2,1,0:T(8,128)(2,1)S(1)}, u32[]{:S(2)}, u32[]{:S(2)}) collective-permute-start(bf16[2,2,3,2,16,256]{5,4,3,2,1,0:T(8,128)(2,1)S(1)} %bitcast.57), channel_id=1, source_target_pairs={{0,2},{2,0},{256,258},{258,256},{1,3},{3,1},{257,259},{259,257},{4... | collective-permute-start | bytes 589832 | tf_op jit(solution)/shard_map/ppermute | solution.py:272
  64.9 10.2 %collective-permute-start.2 = (bf16[2,2,3,2,16,256]{5,4,3,2,1,0:T(8,128)(2,1)S(1)}, bf16[2,2,3,2,16,256]{5,4,3,2,1,0:T(8,128)(2,1)S(1)}, u32[]{:S(2)}, u32[]{:S(2)}) collective-permute-start(bf16[2,2,3,2,16,256]{5,4,3,2,1,0:T(8,128)(2,1)S(1)} %bitcast.58), channel_id=1, source_target_pairs={{0,256},{2,258},{256,0},{258,2},{1,257},{3,259},{257,1},{259,3},{4... | collective-permute-start | bytes 589832 | tf_op jit(solution)/shard_map/ppermute | solution.py:272
  67.6 9.8 %collective-permute-start.3 = (bf16[2,2,3,2,16,256]{5,4,3,2,1,0:T(8,128)(2,1)S(1)}, bf16[2,2,3,2,16,256]{5,4,3,2,1,0:T(8,128)(2,1)S(1)}, u32[]{:S(2)}, u32[]{:S(2)}) collective-permute-start(bf16[2,2,3,2,16,256]{5,4,3,2,1,0:T(8,128)(2,1)S(1)} %bitcast.59), channel_id=1, source_target_pairs={{0,258},{2,256},{256,2},{258,0},{1,259},{3,257},{257,3},{259,1},{4... | collective-permute-start | bytes 589832 | tf_op jit(solution)/shard_map/ppermute | solution.py:272

commit v9 on v7

--- a/solution.py
+++ b/solution.py
@@ -198,28 +198,29 @@
     )(left, flipped, val, p, oth)
 
 
-def pick_rows(at_ref, got_ref, fwd_ref, pay_ref, row_ref):
-    xl = at_ref[2]
-    yl = at_ref[3]
-    for q in range(Q):
-        base = (q // 2) * 8 + (q % 2) * 2
-        other = at_ref[4 + q]
-        begin = at_ref[8 + q]
-        for t in range(KQ):
-            row = got_ref[base + yl * 4 + t // 3, pl.ds(xl * 3 + t % 3, 1), :]
-            fwd_ref[q, pl.ds(t, 1), 0, :] = row[:, :64]
-            fwd_ref[q, pl.ds(t, 1), 1, :] = row[:, 64:]
-            col = lax.rem(begin + t, 12)
-            slot = base + (col // 6) * 4 + (col % 6) // 3
-            row_ref[pl.ds(q * KQ + t, 1), :] = got_ref[slot, pl.ds(other * 3 + col % 3, 1), :]
+def pick_rows(at_ref, got_ref, pay_ref, row_ref):
+    for i in range(Q * KQ):
+        row = got_ref[at_ref[2 + i], pl.ds(at_ref[2 + Q * KQ + i], 1), :]
+        row_ref[pl.ds(i, 1), :] = row
     pay = row_ref[...].astype(BF)
     for slot in range(32):
         pay_ref[slot, :, :] = pay
 
 
+def pick_forward(at_ref, got_ref, out_ref):
+    last = 2 + 2 * Q * KQ + Q
+    xl, yl = at_ref[last], at_ref[last + 1]
+    for q in range(Q):
+        base = (q // 2) * 8 + (q % 2) * 2 + yl * 4
+        for c in range(2):
+            rows = got_ref[base + c, pl.ds(xl * 3, 3), :]
+            out_ref[q, c * 3 : c * 3 + 3, 0, :] = rows[:, :64]
+            out_ref[q, c * 3 : c * 3 + 3, 1, :] = rows[:, 64:]
+
+
 def pick_back(at_ref, came_ref, out_ref):
     for q in range(Q):
-        rows = came_ref[at_ref[12 + q]].astype(F32)[q * KQ : (q + 1) * KQ, :]
+        rows = came_ref[at_ref[2 + 2 * Q * KQ + q]].astype(F32)[q * KQ : (q + 1) * KQ, :]
         out_ref[q, :, 0, :] = rows[:, :64]
         out_ref[q, :, 1, :] = rows[:, 64:]
 
@@ -255,22 +256,31 @@
     other = xl ^ ((here + row_step) // 32 % 2)
     begin = (6 * yl - col_step + 12) % 12
     source = (here - row_step) % 32
-    at = jnp.concatenate([jnp.stack([x, core, xl, yl]), other, begin, source]).astype(jnp.int32)
+    col = (begin[:, None] + jnp.arange(KQ)) % 12
+    base = jnp.array([0, 2, 8, 10])[:, None]
+    slot = base + col // 6 * 4 + col % 6 // 3
+    row = other[:, None] * 3 + col % 3
+    parts = [jnp.stack([x, core]), slot.reshape(-1), row.reshape(-1), source, jnp.stack([xl, yl])]
+    at = jnp.concatenate(parts).astype(jnp.int32)
     left, flipped, right = assembled(at, pieces)
     slots = contracted(left, flipped, right, own)
     got = lax.all_to_all(slots, ("xl", "yl", "xh", "c"), 0, 0)
     vm = pl.BlockSpec(memory_space=pltpu.VMEM)
     sm = pl.BlockSpec(memory_space=pltpu.SMEM)
     out = jax.ShapeDtypeStruct((Q, KQ, 2, 64), F32)
-    forward, pay = pl.pallas_call(
+    kept = pltpu.CompilerParams(vmem_limit_bytes=8 << 20)
+    pay = pl.pallas_call(
         pick_rows,
-        out_shape=(out, jax.ShapeDtypeStruct((32, Q * KQ, 128), BF)),
+        out_shape=jax.ShapeDtypeStruct((32, Q * KQ, 128), BF),
         in_specs=[sm, vm],
-        out_specs=(vm, vm),
+        out_specs=vm,
         scratch_shapes=[pltpu.VMEM((Q * KQ, 128), F32)],
-        compiler_params=pltpu.CompilerParams(vmem_limit_bytes=8 << 20),
+        compiler_params=kept,
     )(at, got)
     came = lax.all_to_all(pay, ("z", "yh"), 0, 0)
+    forward = pl.pallas_call(
+        pick_forward, out_shape=out, in_specs=[sm, vm], out_specs=vm, compiler_params=kept
+    )(at, got)
     back = pl.pallas_call(
         pick_back,
         out_shape=out,

time: 115 us -> 115 us (level)
  blocking collectives: 29.6 us -> 10.6 us
  waiting for transfers between devices: 37.3 us -> 47.7 us
  starting transfers between devices: 34.7 us -> 41.2 us
    all_to_all x1 -> x0, blocking collectives: 19 us -> none  [local(): came = lax.all_to_all(pay, ('z', 'yh'), 0, 0)]
    all_to_all x0 -> x1, waiting for transfers between devices: none -> 11.5 us  [local(): came = lax.all_to_all(pay, ('z', 'yh'), 0, 0)]
    all_to_all x0 -> x1, starting transfers between devices: none -> 6.49 us  [local(): came = lax.all_to_all(pay, ('z', 'yh'), 0, 0)]
    div x0 -> x1, other arithmetic: none -> 1.39 us  [local(): row_step, col_step = (corner // 12, corner % 12)]
    pallas_call x1 -> x2, Pallas kernels: 1.59 us -> 2.51 us  [the longest x1 1.27 us: local(): pl.pallas_call(pick_rows, out_shape=jax.ShapeDtypeStruct((32, Q * KQ, 128...]
  transfers between devices with their start and end apart: 7 -> 8, of which waited for: 4 -> 5; matrix products, arithmetic and copies ran while one was open for 4% -> 5% of each run, Pallas kernels for 1% -> 3%
where the time goes in v9:
time: 115 us
  waiting for transfers between devices  47.7 us (41%)
  starting transfers between devices  41.2 us (36%)
  blocking collectives  10.6 us (9%)
  Pallas kernels  8.42 us (7%)
  other arithmetic  3.75 us (3%)
  local copies, waits for them, and re-layouts  1.99 us (2%)
    all_to_all x1, waiting for transfers between devices, local(): w = lax.all_to_all(w, ('z', 'yh', 'yl'), 0, 0)  26.3 us
    all_to_all x1, starting transfers between devices, local(): w = lax.all_to_all(w, ('z', 'yh', 'yl'), 0, 0)  16.6 us
    all_to_all x1, waiting for transfers between devices, local(): came = lax.all_to_all(pay, ('z', 'yh'), 0, 0)  11.5 us
    all_to_all x1, blocking collectives, local(): got = lax.all_to_all(slots, ('xl', 'yl', 'xh', 'c'), 0, 0)  10.6 us
    ppermute x3, starting transfers between devices, local(): piece = lax.ppermute(piece, ('xl', 'xh'), [(i, i ^ s) for i in range(4)])  9.81 us
    all_to_all x1, starting transfers between devices, local(): came = lax.all_to_all(pay, ('z', 'yh'), 0, 0)  6.49 us
    all_to_all x1, waiting for transfers between devices, local(): w = lax.all_to_all(screened.reshape(8, 8, 256), ('xl', 'xh', 'c'), 0, 0)  5.36 us
    ppermute x3, waiting for transfers between devices, local(): piece = lax.ppermute(piece, ('xl', 'xh'), [(i, i ^ s) for i in range(4)])  4.66 us
  transfers between devices with their start and end apart: 8, of which 5 were waited for; matrix products, arithmetic and copies ran while one was open for 5% of the time, Pallas kernels for 3%

profile of v9, /device:TPU:16, one launch (start us, length us, event | category | flops | bytes accessed | tf_op | source)
XLA Modules:
  0.0 114.5 jit_solution(5378130552522523337)
XLA Ops:
  0.6 4.3 %all-to-all-start = ((bf16[8,8,256]{2,1,0:T(8,128)(2,1)}), bf16[8,8,256]{2,1,0:T(8,128)(2,1)S(1)}, u32[]{:S(2)}, u32[]{:S(2)}) async-start(bf16[8,8,256]{2,1,0:T(8,128)(2,1)} %bitcast.58), calls=%async_computation | async-start | bytes 65536 | tf_op jit(solution)/shard_map/all_to_all | solution.py:231
  4.9 5.4 %all-to-all-done.w_ref = bf16[8,8,256]{2,1,0:T(8,128)(2,1)S(1)} async-done(((bf16[8,8,256]{2,1,0:T(8,128)(2,1)}), bf16[8,8,256]{2,1,0:T(8,128)(2,1)S(1)}, u32[]{:S(2)}, u32[]{:S(2)}) %all-to-all-start) | async-done | bytes 32800 | tf_op jit(solution)/shard_map/all_to_all | solution.py:231
  10.3 1.1 shard_map.69
  11.4 16.6 %all-to-all-start.1 = ((bf16[64,8,1152]{2,1,0:T(8,128)(2,1)}), bf16[64,8,1152]{2,1,0:T(8,128)(2,1)S(1)}, u32[]{:S(2)}, u32[]{:S(2)}) async-start(bf16[64,8,1152]{2,1,0:T(8,128)(2,1)} %shard_map.69), calls=%async_computation.1 | async-start | bytes 2359296 | tf_op jit(solution)/shard_map/all_to_all | solution.py:233
  28.2 1.9 %collective-permute-start = (bf16[2,4,3,2,16,256]{5,4,3,2,1,0:T(8,128)(2,1)S(1)}, bf16[2,4,3,2,16,256]{5,4,3,2,1,0:T(8,128)(2,1)S(1)}, u32[]{:S(2)}, u32[]{:S(2)}) collective-permute-start(bf16[2,4,3,2,16,256]{5,4,3,2,1,0:T(8,128)(2,1)S(1)} %pad_maximum_fusion), channel_id=1, source_target_pairs={{0,1},{1,0},{2,3},{3,2},{4,5},{5,4},{6,7},{7,6},{8,9},{9,8},{10,11... | collective-permute-start | bytes 1179656 | tf_op jit(solution)/shard_map/ppermute | solution.py:242
  30.1 0.8 fusion.17
  30.9 1.4 %fusion.16 = (s32[4]{0:T(128)}, s32[4]{0:T(128)S(1)}, s32[4]{0:T(128)S(1)}) fusion(s32[4,768]{1,0:T(4,128)} %param.8, pred[4,1]{1,0:T(4,128)(4,1)S(1)} %get-tuple-element.12, s32[]{:T(128)S(6)} %add.210, s32[]{:T(128)} %axis_index.63, s32[]{:T(128)S(6)} %mul.19), kind=kLoop, calls=%fused_computation.63 | loop fusion | flops 184 | bytes 80 | tf_op jit(solution)/shard_map/jit(floor_divide)/div | solution.py:254
  33.5 26.3 %all-to-all-done.1 = bf16[64,8,1152]{2,1,0:T(8,128)(2,1)S(1)} async-done(((bf16[64,8,1152]{2,1,0:T(8,128)(2,1)}), bf16[64,8,1152]{2,1,0:T(8,128)(2,1)S(1)}, u32[]{:S(2)}, u32[]{:S(2)}) %all-to-all-start.1) | async-done | bytes 1179680 | tf_op jit(solution)/shard_map/all_to_all | solution.py:233
  59.8 2.1 %collective-permute-start.4 = (bf16[512,1152]{1,0:T(8,128)(2,1)S(1)}, bf16[512,1152]{1,0:T(8,128)(2,1)S(1)}, u32[]{:S(2)}, u32[]{:S(2)}) collective-permute-start(bf16[512,1152]{1,0:T(8,128)(2,1)S(1)} %bitcast.49), channel_id=1, source_target_pairs={{0,1},{1,0},{2,3},{3,2},{4,5},{5,4},{6,7},{7,6},{8,9},{9,8},{10,11... | collective-permute-start | bytes 3538952 | tf_op jit(solution)/shard_map/ppermute | solution.py:182
  62.0 3.2 %collective-permute-start.1 = (bf16[2,2,3,2,16,256]{5,4,3,2,1,0:T(8,128)(2,1)S(1)}, bf16[2,2,3,2,16,256]{5,4,3,2,1,0:T(8,128)(2,1)S(1)}, u32[]{:S(2)}, u32[]{:S(2)}) collective-permute-start(bf16[2,2,3,2,16,256]{5,4,3,2,1,0:T(8,128)(2,1)S(1)} %bitcast.56), channel_id=1, source_target_pairs={{0,2},{2,0},{256,258},{258,256},{1,3},{3,1},{257,259},{259,257},{4... | collective-permute-start | bytes 589832 | tf_op jit(solution)/shard_map/ppermute | solution.py:251
  65.2 2.7 %collective-permute-start.2 = (bf16[2,2,3,2,16,256]{5,4,3,2,1,0:T(8,128)(2,1)S(1)}, bf16[2,2,3,2,16,256]{5,4,3,2,1,0:T(8,128)(2,1)S(1)}, u32[]{:S(2)}, u32[]{:S(2)}) collective-permute-start(bf16[2,2,3,2,16,256]{5,4,3,2,1,0:T(8,128)(2,1)S(1)} %bitcast.57), channel_id=1, source_target_pairs={{0,256},{2,258},{256,0},{258,2},{1,257},{3,259},{257,1},{259,3},{4... | collective-permute-start | bytes 589832 | tf_op jit(solution)/shard_map/ppermute | solution.py:251
  68.6 4.0 %collective-permute-start.3 = (bf16[2,2,3,2,16,256]{5,4,3,2,1,0:T(8,128)(2,1)}, bf16[2,2,3,2,16,256]{5,4,3,2,1,0:T(8,128)(2,1)S(1)}, u32[]{:S(2)}, u32[]{:S(2)}) collective-permute-start(bf16[2,2,3,2,16,256]{5,4,3,2,1,0:T(8,128)(2,1)} %bitcast.27), channel_id=1, source_target_pairs={{0,258},{2,256},{256,2},{258,0},{1,259},{3,257},{257,3},{259,1},{4... | collective-permute-start | bytes 589832 | tf_op jit(solution)/shard_map/ppermute | solution.py:251
  73.2 0.8 concatenate.3.at_ref
  74.0 1.4 %collective-permute-done.2.refs_2_ = bf16[2,2,3,2,16,256]{5,4,3,2,1,0:T(8,128)(2,1)S(1)} collective-permute-done((bf16[2,2,3,2,16,256]{5,4,3,2,1,0:T(8,128)(2,1)S(1)}, bf16[2,2,3,2,16,256]{5,4,3,2,1,0:T(8,128)(2,1)S(1)}, u32[]{:S(2)}, u32[]{:S(2)}) %collective-permute-start.2) | collective-permute-done | bytes 196640 | tf_op jit(solution)/shard_map/ppermute | solution.py:251
  75.4 3.3 %collective-permute-done.3.refs_3_ = bf16[2,2,3,2,16,256]{5,4,3,2,1,0:T(8,128)(2,1)S(1)} collective-permute-done((bf16[2,2,3,2,16,256]{5,4,3,2,1,0:T(8,128)(2,1)}, bf16[2,2,3,2,16,256]{5,4,3,2,1,0:T(8,128)(2,1)S(1)}, u32[]{:S(2)}, u32[]{:S(2)}) %collective-permute-start.3) | collective-permute-done | bytes 196640 | tf_op jit(solution)/shard_map/ppermute | solution.py:251
  78.7 0.8 shard_map.68
  79.5 0.9 shard_map.70.p_ref
  80.4 1.9 %shard_map.71 = f32[16,6,128]{2,1,0:T(8,128)S(1)} custom-call(bf16[192,1024]{1,0:T(8,128)(2,1)S(1)} %get-tuple-element.5.left_ref, bf16[192,1024]{1,0:T(8,128)(2,1)S(1)} %get-tuple-element.6.flip_ref, bf16[192,1024]{1,0:T(8,128)(2,1)S(1)} %get-tuple-element.7.val_ref, f32[192,1024]{1,0:T(8,128)S(1)} %shard_map.70.p_ref, ...), custom_call_target="tpu_custom_call" | custom-call | flops 800000000 | bytes 2000000 | tf_op jit(solution)/shard_map/pallas_call | solution.py:191
  82.3 10.6 %all_to_all.20.got_ref = f32[16,6,128]{2,1,0:T(8,128)S(1)} all-to-all(f32[16,6,128]{2,1,0:T(8,128)S(1)} %shard_map.71), channel_id=1, replica_groups=mesh['xl'=2,'z'=8,'yh'=4,'yl'=2,'xh'=2,'c'=2] {'xl','yl','xh','c'}, dimensions={0} | all-to-all | bytes 98304 | tf_op jit(solution)/shard_map/all_to_all | solution.py:267
  92.8 1.3 %shard_map.73 = bf16[32,24,128]{2,1,0:T(8,128)(2,1)} custom-call(s32[56]{0:T(128)S(1)} %concatenate.3.at_ref, f32[16,6,128]{2,1,0:T(8,128)S(1)} %all_to_all.20.got_ref), custom_call_target="tpu_custom_call" | custom-call | tf_op jit(solution)/shard_map/pallas_call | solution.py:272
  94.1 6.5 %all-to-all-start.3 = ((bf16[32,24,128]{2,1,0:T(8,128)(2,1)}), bf16[32,24,128]{2,1,0:T(8,128)(2,1)S(1)}, u32[]{:S(2)}, u32[]{:S(2)}) async-start(bf16[32,24,128]{2,1,0:T(8,128)(2,1)} %shard_map.73), calls=%async_computation.3 | async-start | bytes 393216 | tf_op jit(solution)/shard_map/all_to_all | solution.py:280
  100.6 1.2 %shard_map.72 = f32[4,6,2,64]{3,2,1,0:T(2,128)} custom-call(s32[56]{0:T(128)S(1)} %concatenate.3.at_ref, f32[16,6,128]{2,1,0:T(8,128)S(1)} %all_to_all.20.got_ref), custom_call_target="tpu_custom_call" | custom-call | tf_op jit(solution)/shard_map/pallas_call | solution.py:281
  101.8 11.5 %all-to-all-done.3.came_ref = bf16[32,24,128]{2,1,0:T(8,128)(2,1)S(1)} async-done(((bf16[32,24,128]{2,1,0:T(8,128)(2,1)}), bf16[32,24,128]{2,1,0:T(8,128)(2,1)S(1)}, u32[]{:S(2)}, u32[]{:S(2)}) %all-to-all-start.3) | async-done | bytes 196640 | tf_op jit(solution)/shard_map/all_to_all | solution.py:280
  113.3 1.2 %shard_map.74 = f32[4,6,2,64]{3,2,1,0:T(2,128)} custom-call(s32[56]{0:T(128)S(1)} %concatenate.3.at_ref, bf16[32,24,128]{2,1,0:T(8,128)(2,1)S(1)} %all-to-all-done.3.came_ref), custom_call_target="tpu_custom_call" | custom-call | tf_op jit(solution)/shard_map/pallas_call | solution.py:284
  (37 shorter events, 2.8 us)
Async XLA Ops:
  0.6 9.7 %all-to-all-start = ((bf16[8,8,256]{2,1,0:T(8,128)(2,1)}), bf16[8,8,256]{2,1,0:T(8,128)(2,1)S(1)}, u32[]{:S(2)}, u32[]{:S(2)}) async-start(bf16[8,8,256]{2,1,0:T(8,128)(2,1)} %bitcast.58), calls=%async_computation | async-start | bytes 65536 | tf_op jit(solution)/shard_map/all_to_all | solution.py:231
  11.4 16.6 %copy-start = (bf16[4,6,2,16,256]{4,3,2,1,0:T(8,128)(2,1)S(1)}, bf16[4,6,2,16,256]{4,3,2,1,0:T(8,128)(2,1)}, u32[]{:S(2)}) copy-start(bf16[4,6,2,16,256]{4,3,2,1,0:T(8,128)(2,1)} %param.6) | copy-start | bytes 1179652
  11.4 16.6 %copy-start.1 = (bf16[4,6,2,16,256]{4,3,2,1,0:T(8,128)(2,1)S(1)}, bf16[4,6,2,16,256]{4,3,2,1,0:T(8,128)(2,1)}, u32[]{:S(2)}) copy-start(bf16[4,6,2,16,256]{4,3,2,1,0:T(8,128)(2,1)} %param.5) | copy-start | bytes 1179652
  11.4 48.3 %all-to-all-start.1 = ((bf16[64,8,1152]{2,1,0:T(8,128)(2,1)}), bf16[64,8,1152]{2,1,0:T(8,128)(2,1)S(1)}, u32[]{:S(2)}, u32[]{:S(2)}) async-start(bf16[64,8,1152]{2,1,0:T(8,128)(2,1)} %shard_map.69), calls=%async_computation.1 | async-start | bytes 2359296 | tf_op jit(solution)/shard_map/all_to_all | solution.py:233
  28.0 4.6 %copy-start.7 = (s32[4]{0:T(128)S(1)}, s32[4]{0:T(128)}, u32[]{:S(2)}) copy-start(s32[4]{0:T(128)} %constant.403.clone) | copy-start | bytes 52
  28.2 33.7 %collective-permute-start = (bf16[2,4,3,2,16,256]{5,4,3,2,1,0:T(8,128)(2,1)S(1)}, bf16[2,4,3,2,16,256]{5,4,3,2,1,0:T(8,128)(2,1)S(1)}, u32[]{:S(2)}, u32[]{:S(2)}) collective-permute-start(bf16[2,4,3,2,16,256]{5,4,3,2,1,0:T(8,128)(2,1)S(1)} %pad_maximum_fusion), channel_id=1, source_target_pairs={{0,1},{1,0},{2,3},{3,2},{4,5},{5,4},{6,7},{7,6},{8,9},{9,8},{10,11... | collective-permute-start | bytes 1179656 | tf_op jit(solution)/shard_map/ppermute | solution.py:242
  59.8 5.4 %copy-start.4 = (bf16[1,3,2,16,256]{4,3,2,1,0:T(8,128)(2,1)S(1)}, bf16[1,3,2,16,256]{4,3,2,1,0:T(8,128)(2,1)}, u32[]{:S(2)}) copy-start(bf16[1,3,2,16,256]{4,3,2,1,0:T(8,128)(2,1)} %get-tuple-element.18) | copy-start | bytes 147460
  59.8 5.4 %copy-start.5 = (bf16[1,3,2,16,256]{4,3,2,1,0:T(8,128)(2,1)S(1)}, bf16[1,3,2,16,256]{4,3,2,1,0:T(8,128)(2,1)}, u32[]{:S(2)}) copy-start(bf16[1,3,2,16,256]{4,3,2,1,0:T(8,128)(2,1)} %get-tuple-element.37) | copy-start | bytes 147460
  59.8 8.1 %copy-start.2 = (bf16[1,3,2,16,256]{4,3,2,1,0:T(8,128)(2,1)S(1)}, bf16[1,3,2,16,256]{4,3,2,1,0:T(8,128)(2,1)}, u32[]{:S(2)}) copy-start(bf16[1,3,2,16,256]{4,3,2,1,0:T(8,128)(2,1)} %get-tuple-element.17) | copy-start | bytes 147460
  59.8 8.2 %copy-start.3 = (bf16[1,3,2,16,256]{4,3,2,1,0:T(8,128)(2,1)S(1)}, bf16[1,3,2,16,256]{4,3,2,1,0:T(8,128)(2,1)}, u32[]{:S(2)}) copy-start(bf16[1,3,2,16,256]{4,3,2,1,0:T(8,128)(2,1)} %get-tuple-element.38) | copy-start | bytes 147460
  59.8 20.6 %collective-permute-start.4 = (bf16[512,1152]{1,0:T(8,128)(2,1)S(1)}, bf16[512,1152]{1,0:T(8,128)(2,1)S(1)}, u32[]{:S(2)}, u32[]{:S(2)}) collective-permute-start(bf16[512,1152]{1,0:T(8,128)(2,1)S(1)} %bitcast.49), channel_id=1, source_target_pairs={{0,1},{1,0},{2,3},{3,2},{4,5},{5,4},{6,7},{7,6},{8,9},{9,8},{10,11... | collective-permute-start | bytes 3538952 | tf_op jit(solution)/shard_map/ppermute | solution.py:182
  61.9 10.7 %copy-start.6 = (s32[4]{0:T(128)S(1)}, s32[4]{0:T(128)}, u32[]{:S(2)}) copy-start(s32[4]{0:T(128)} %get-tuple-element.8) | copy-start | bytes 52
  62.0 12.0 %collective-permute-start.1 = (bf16[2,2,3,2,16,256]{5,4,3,2,1,0:T(8,128)(2,1)S(1)}, bf16[2,2,3,2,16,256]{5,4,3,2,1,0:T(8,128)(2,1)S(1)}, u32[]{:S(2)}, u32[]{:S(2)}) collective-permute-start(bf16[2,2,3,2,16,256]{5,4,3,2,1,0:T(8,128)(2,1)S(1)} %bitcast.56), channel_id=1, source_target_pairs={{0,2},{2,0},{256,258},{258,256},{1,3},{3,1},{257,259},{259,257},{4... | collective-permute-start | bytes 589832 | tf_op jit(solution)/shard_map/ppermute | solution.py:251
  65.2 10.2 %collective-permute-start.2 = (bf16[2,2,3,2,16,256]{5,4,3,2,1,0:T(8,128)(2,1)S(1)}, bf16[2,2,3,2,16,256]{5,4,3,2,1,0:T(8,128)(2,1)S(1)}, u32[]{:S(2)}, u32[]{:S(2)}) collective-permute-start(bf16[2,2,3,2,16,256]{5,4,3,2,1,0:T(8,128)(2,1)S(1)} %bitcast.57), channel_id=1, source_target_pairs={{0,256},{2,258},{256,0},{258,2},{1,257},{3,259},{257,1},{259,3},{4... | collective-permute-start | bytes 589832 | tf_op jit(solution)/shard_map/ppermute | solution.py:251
  68.6 10.0 %collective-permute-start.3 = (bf16[2,2,3,2,16,256]{5,4,3,2,1,0:T(8,128)(2,1)}, bf16[2,2,3,2,16,256]{5,4,3,2,1,0:T(8,128)(2,1)S(1)}, u32[]{:S(2)}, u32[]{:S(2)}) collective-permute-start(bf16[2,2,3,2,16,256]{5,4,3,2,1,0:T(8,128)(2,1)} %bitcast.27), channel_id=1, source_target_pairs={{0,258},{2,256},{256,2},{258,0},{1,259},{3,257},{257,3},{259,1},{4... | collective-permute-start | bytes 589832 | tf_op jit(solution)/shard_map/ppermute | solution.py:251
  94.1 19.2 %all-to-all-start.3 = ((bf16[32,24,128]{2,1,0:T(8,128)(2,1)}), bf16[32,24,128]{2,1,0:T(8,128)(2,1)S(1)}, u32[]{:S(2)}, u32[]{:S(2)}) async-start(bf16[32,24,128]{2,1,0:T(8,128)(2,1)} %shard_map.73), calls=%async_computation.3 | async-start | bytes 393216 | tf_op jit(solution)/shard_map/all_to_all | solution.py:280

commit v10 on v9

--- a/solution.py
+++ b/solution.py
@@ -17,14 +17,20 @@
 F32 = jnp.float32
 
 
-def nt(left, right, precision=None):
-    return lax.dot_general(
-        left, right, (((1,), (1,)), ((), ())), preferred_element_type=F32, precision=precision
-    )
-
-
-def nn(left, right, precision=None):
-    return jnp.dot(left, right, preferred_element_type=F32, precision=precision)
+def nt(left, right):
+    return lax.dot_general(left, right, (((1,), (1,)), ((), ())), preferred_element_type=F32)
+
+
+def nn(left, right):
+    return jnp.dot(left, right, preferred_element_type=F32)
+
+
+def exact_terms(x, axis):
+    high = x.astype(BF)
+    rest = x - high.astype(F32)
+    middle = rest.astype(BF)
+    low = (rest - middle.astype(F32)).astype(BF)
+    return jnp.concatenate([high, middle, low], axis)
 
 
 def fan(at_ref, w_ref, out_ref):
@@ -152,24 +158,24 @@
         g2 += nt(x_imag, val)
     r = lax.broadcasted_iota(jnp.int32, (half, rows), 0)
     c = lax.broadcasted_iota(jnp.int32, (half, rows), 1)
-    same = r // PAIR == c // (2 * PAIR)
-    g1 = jnp.where(same, g1, 0.0)
-    g2 = jnp.where(same, g2, 0.0)
+    same = (r >> 4) == (c >> 5)
+    both = jnp.concatenate([jnp.where(same, g1, 0.0), jnp.where(same, g2, 0.0)], 1)
     c = lax.broadcasted_iota(jnp.int32, (rows, 128), 0)
     l = lax.broadcasted_iota(jnp.int32, (rows, 128), 1)
-    hit = c % PAIR == l % PAIR
-    part = (c // PAIR) % 2
-    want = l // 64
+    hit = (c & 15) == (l & 15)
+    part = (c >> 4) & 1
+    want = l >> 6
     e1 = jnp.where(hit & (part == want), 1.0, 0.0)
     e2 = jnp.where(hit & (part != want), jnp.where(want == 0, -1.0, 1.0), 0.0)
-    t = nn(g1, e1, lax.Precision.HIGHEST) + nn(g2, e2, lax.Precision.HIGHEST)
+    e12 = jnp.concatenate([e1, e2], 0).astype(BF)
+    t = nn(exact_terms(both, 1), jnp.concatenate([e12] * 3, 0))
     r = lax.broadcasted_iota(jnp.int32, (half, 128), 0)
     l = lax.broadcasted_iota(jnp.int32, (half, 128), 1)
-    t = jnp.where(r % 4 == (l // PAIR) % 4, t, 0.0)
+    t = jnp.where((r & 3) == ((l >> 4) & 3), t, 0.0)
     o = lax.broadcasted_iota(jnp.int32, (4 * 8, half), 0)
     r = lax.broadcasted_iota(jnp.int32, (4 * 8, half), 1)
-    e3 = jnp.where((r // PAIR == o % 8) & ((r % PAIR) // 4 == o // 8), 1.0, 0.0)
-    block = nn(e3, t, lax.Precision.HIGHEST)
+    e3 = jnp.where(((r >> 4) == (o & 7)) & (((r & 15) >> 2) == (o >> 3)), 1.0, 0.0).astype(BF)
+    block = nn(jnp.concatenate([e3] * 3, 1), exact_terms(t, 0))
     for slot in range(16):
         g = slot % 4
         out_ref[slot, :, :] = block[g * 8 : g * 8 + KQ, :]

time: 115 us -> 115 us (level)
  no operation moved by 1% of the time
where the time goes in v10:
time: 115 us; the launch traced here: 114 us
  waiting for transfers between devices  47.7 us (41%)
  starting transfers between devices  41.2 us (36%)
  blocking collectives  10.5 us (9%)
  Pallas kernels  8.21 us (7%)
  other arithmetic  3.75 us (3%)
  local copies, waits for them, and re-layouts  1.99 us (2%)
    all_to_all x1, waiting for transfers between devices, local(): w = lax.all_to_all(w, ('z', 'yh', 'yl'), 0, 0)  26.3 us
    all_to_all x1, starting transfers between devices, local(): w = lax.all_to_all(w, ('z', 'yh', 'yl'), 0, 0)  16.6 us
    all_to_all x1, waiting for transfers between devices, local(): came = lax.all_to_all(pay, ('z', 'yh'), 0, 0)  11.5 us
    all_to_all x1, blocking collectives, local(): got = lax.all_to_all(slots, ('xl', 'yl', 'xh', 'c'), 0, 0)  10.5 us
    ppermute x3, starting transfers between devices, local(): piece = lax.ppermute(piece, ('xl', 'xh'), [(i, i ^ s) for i in range(4)])  9.81 us
    all_to_all x1, starting transfers between devices, local(): came = lax.all_to_all(pay, ('z', 'yh'), 0, 0)  6.49 us
    all_to_all x1, waiting for transfers between devices, local(): w = lax.all_to_all(screened.reshape(8, 8, 256), ('xl', 'xh', 'c'), 0, 0)  5.36 us
    ppermute x3, waiting for transfers between devices, local(): piece = lax.ppermute(piece, ('xl', 'xh'), [(i, i ^ s) for i in range(4)])  4.66 us
  transfers between devices with their start and end apart: 8, of which 5 were waited for; matrix products, arithmetic and copies ran while one was open for 5% of the time, Pallas kernels for 3%

profile of v10, /device:TPU:16, one launch (start us, length us, event | category | flops | bytes accessed | tf_op | source)
XLA Modules:
  0.0 114.3 jit_solution(9907227708160635408)
XLA Ops:
  0.6 4.3 %all-to-all-start = ((bf16[8,8,256]{2,1,0:T(8,128)(2,1)}), bf16[8,8,256]{2,1,0:T(8,128)(2,1)S(1)}, u32[]{:S(2)}, u32[]{:S(2)}) async-start(bf16[8,8,256]{2,1,0:T(8,128)(2,1)} %bitcast.58), calls=%async_computation | async-start | bytes 65536 | tf_op jit(solution)/shard_map/all_to_all | solution.py:237
  4.9 5.4 %all-to-all-done.w_ref = bf16[8,8,256]{2,1,0:T(8,128)(2,1)S(1)} async-done(((bf16[8,8,256]{2,1,0:T(8,128)(2,1)}), bf16[8,8,256]{2,1,0:T(8,128)(2,1)S(1)}, u32[]{:S(2)}, u32[]{:S(2)}) %all-to-all-start) | async-done | bytes 32800 | tf_op jit(solution)/shard_map/all_to_all | solution.py:237
  10.3 1.1 shard_map.69
  11.4 16.6 %all-to-all-start.1 = ((bf16[64,8,1152]{2,1,0:T(8,128)(2,1)}), bf16[64,8,1152]{2,1,0:T(8,128)(2,1)S(1)}, u32[]{:S(2)}, u32[]{:S(2)}) async-start(bf16[64,8,1152]{2,1,0:T(8,128)(2,1)} %shard_map.69), calls=%async_computation.1 | async-start | bytes 2359296 | tf_op jit(solution)/shard_map/all_to_all | solution.py:239
  28.2 1.9 %collective-permute-start = (bf16[2,4,3,2,16,256]{5,4,3,2,1,0:T(8,128)(2,1)S(1)}, bf16[2,4,3,2,16,256]{5,4,3,2,1,0:T(8,128)(2,1)S(1)}, u32[]{:S(2)}, u32[]{:S(2)}) collective-permute-start(bf16[2,4,3,2,16,256]{5,4,3,2,1,0:T(8,128)(2,1)S(1)} %pad_maximum_fusion), channel_id=1, source_target_pairs={{0,1},{1,0},{2,3},{3,2},{4,5},{5,4},{6,7},{7,6},{8,9},{9,8},{10,11... | collective-permute-start | bytes 1179656 | tf_op jit(solution)/shard_map/ppermute | solution.py:248
  30.1 0.8 fusion.17
  30.9 1.4 %fusion.16 = (s32[4]{0:T(128)}, s32[4]{0:T(128)S(1)}, s32[4]{0:T(128)S(1)}) fusion(s32[4,768]{1,0:T(4,128)} %param.8, pred[4,1]{1,0:T(4,128)(4,1)S(1)} %get-tuple-element.12, s32[]{:T(128)S(6)} %add.210, s32[]{:T(128)} %axis_index.63, s32[]{:T(128)S(6)} %mul.19), kind=kLoop, calls=%fused_computation.63 | loop fusion | flops 184 | bytes 80 | tf_op jit(solution)/shard_map/jit(floor_divide)/div | solution.py:260
  33.5 26.3 %all-to-all-done.1 = bf16[64,8,1152]{2,1,0:T(8,128)(2,1)S(1)} async-done(((bf16[64,8,1152]{2,1,0:T(8,128)(2,1)}), bf16[64,8,1152]{2,1,0:T(8,128)(2,1)S(1)}, u32[]{:S(2)}, u32[]{:S(2)}) %all-to-all-start.1) | async-done | bytes 1179680 | tf_op jit(solution)/shard_map/all_to_all | solution.py:239
  59.8 2.1 %collective-permute-start.4 = (bf16[512,1152]{1,0:T(8,128)(2,1)S(1)}, bf16[512,1152]{1,0:T(8,128)(2,1)S(1)}, u32[]{:S(2)}, u32[]{:S(2)}) collective-permute-start(bf16[512,1152]{1,0:T(8,128)(2,1)S(1)} %bitcast.49), channel_id=1, source_target_pairs={{0,1},{1,0},{2,3},{3,2},{4,5},{5,4},{6,7},{7,6},{8,9},{9,8},{10,11... | collective-permute-start | bytes 3538952 | tf_op jit(solution)/shard_map/ppermute | solution.py:188
  62.0 3.2 %collective-permute-start.1 = (bf16[2,2,3,2,16,256]{5,4,3,2,1,0:T(8,128)(2,1)S(1)}, bf16[2,2,3,2,16,256]{5,4,3,2,1,0:T(8,128)(2,1)S(1)}, u32[]{:S(2)}, u32[]{:S(2)}) collective-permute-start(bf16[2,2,3,2,16,256]{5,4,3,2,1,0:T(8,128)(2,1)S(1)} %bitcast.56), channel_id=1, source_target_pairs={{0,2},{2,0},{256,258},{258,256},{1,3},{3,1},{257,259},{259,257},{4... | collective-permute-start | bytes 589832 | tf_op jit(solution)/shard_map/ppermute | solution.py:257
  65.2 2.7 %collective-permute-start.2 = (bf16[2,2,3,2,16,256]{5,4,3,2,1,0:T(8,128)(2,1)S(1)}, bf16[2,2,3,2,16,256]{5,4,3,2,1,0:T(8,128)(2,1)S(1)}, u32[]{:S(2)}, u32[]{:S(2)}) collective-permute-start(bf16[2,2,3,2,16,256]{5,4,3,2,1,0:T(8,128)(2,1)S(1)} %bitcast.57), channel_id=1, source_target_pairs={{0,256},{2,258},{256,0},{258,2},{1,257},{3,259},{257,1},{259,3},{4... | collective-permute-start | bytes 589832 | tf_op jit(solution)/shard_map/ppermute | solution.py:257
  68.6 4.0 %collective-permute-start.3 = (bf16[2,2,3,2,16,256]{5,4,3,2,1,0:T(8,128)(2,1)}, bf16[2,2,3,2,16,256]{5,4,3,2,1,0:T(8,128)(2,1)S(1)}, u32[]{:S(2)}, u32[]{:S(2)}) collective-permute-start(bf16[2,2,3,2,16,256]{5,4,3,2,1,0:T(8,128)(2,1)} %bitcast.27), channel_id=1, source_target_pairs={{0,258},{2,256},{256,2},{258,0},{1,259},{3,257},{257,3},{259,1},{4... | collective-permute-start | bytes 589832 | tf_op jit(solution)/shard_map/ppermute | solution.py:257
  73.2 0.8 concatenate.3.at_ref
  74.0 1.4 %collective-permute-done.2.refs_2_ = bf16[2,2,3,2,16,256]{5,4,3,2,1,0:T(8,128)(2,1)S(1)} collective-permute-done((bf16[2,2,3,2,16,256]{5,4,3,2,1,0:T(8,128)(2,1)S(1)}, bf16[2,2,3,2,16,256]{5,4,3,2,1,0:T(8,128)(2,1)S(1)}, u32[]{:S(2)}, u32[]{:S(2)}) %collective-permute-start.2) | collective-permute-done | bytes 196640 | tf_op jit(solution)/shard_map/ppermute | solution.py:257
  75.4 3.3 %collective-permute-done.3.refs_3_ = bf16[2,2,3,2,16,256]{5,4,3,2,1,0:T(8,128)(2,1)S(1)} collective-permute-done((bf16[2,2,3,2,16,256]{5,4,3,2,1,0:T(8,128)(2,1)}, bf16[2,2,3,2,16,256]{5,4,3,2,1,0:T(8,128)(2,1)S(1)}, u32[]{:S(2)}, u32[]{:S(2)}) %collective-permute-start.3) | collective-permute-done | bytes 196640 | tf_op jit(solution)/shard_map/ppermute | solution.py:257
  78.7 0.8 shard_map.68
  79.5 0.9 shard_map.70.p_ref
  80.4 1.7 %shard_map.71 = f32[16,6,128]{2,1,0:T(8,128)S(1)} custom-call(bf16[192,1024]{1,0:T(8,128)(2,1)S(1)} %get-tuple-element.5.left_ref, bf16[192,1024]{1,0:T(8,128)(2,1)S(1)} %get-tuple-element.6.flip_ref, bf16[192,1024]{1,0:T(8,128)(2,1)S(1)} %get-tuple-element.7.val_ref, f32[192,1024]{1,0:T(8,128)S(1)} %shard_map.70.p_ref, ...), custom_call_target="tpu_custom_call" | custom-call | flops 800000000 | bytes 2000000 | tf_op jit(solution)/shard_map/pallas_call | solution.py:197
  82.0 10.5 %all_to_all.20.got_ref = f32[16,6,128]{2,1,0:T(8,128)S(1)} all-to-all(f32[16,6,128]{2,1,0:T(8,128)S(1)} %shard_map.71), channel_id=1, replica_groups=mesh['xl'=2,'z'=8,'yh'=4,'yl'=2,'xh'=2,'c'=2] {'xl','yl','xh','c'}, dimensions={0} | all-to-all | bytes 98304 | tf_op jit(solution)/shard_map/all_to_all | solution.py:273
  92.6 1.3 %shard_map.73 = bf16[32,24,128]{2,1,0:T(8,128)(2,1)} custom-call(s32[56]{0:T(128)S(1)} %concatenate.3.at_ref, f32[16,6,128]{2,1,0:T(8,128)S(1)} %all_to_all.20.got_ref), custom_call_target="tpu_custom_call" | custom-call | tf_op jit(solution)/shard_map/pallas_call | solution.py:278
  93.8 6.5 %all-to-all-start.3 = ((bf16[32,24,128]{2,1,0:T(8,128)(2,1)}), bf16[32,24,128]{2,1,0:T(8,128)(2,1)S(1)}, u32[]{:S(2)}, u32[]{:S(2)}) async-start(bf16[32,24,128]{2,1,0:T(8,128)(2,1)} %shard_map.73), calls=%async_computation.3 | async-start | bytes 393216 | tf_op jit(solution)/shard_map/all_to_all | solution.py:286
  100.3 1.2 %shard_map.72 = f32[4,6,2,64]{3,2,1,0:T(2,128)} custom-call(s32[56]{0:T(128)S(1)} %concatenate.3.at_ref, f32[16,6,128]{2,1,0:T(8,128)S(1)} %all_to_all.20.got_ref), custom_call_target="tpu_custom_call" | custom-call | tf_op jit(solution)/shard_map/pallas_call | solution.py:287
  101.6 11.5 %all-to-all-done.3.came_ref = bf16[32,24,128]{2,1,0:T(8,128)(2,1)S(1)} async-done(((bf16[32,24,128]{2,1,0:T(8,128)(2,1)}), bf16[32,24,128]{2,1,0:T(8,128)(2,1)S(1)}, u32[]{:S(2)}, u32[]{:S(2)}) %all-to-all-start.3) | async-done | bytes 196640 | tf_op jit(solution)/shard_map/all_to_all | solution.py:286
  113.0 1.2 %shard_map.74 = f32[4,6,2,64]{3,2,1,0:T(2,128)} custom-call(s32[56]{0:T(128)S(1)} %concatenate.3.at_ref, bf16[32,24,128]{2,1,0:T(8,128)(2,1)S(1)} %all-to-all-done.3.came_ref), custom_call_target="tpu_custom_call" | custom-call | tf_op jit(solution)/shard_map/pallas_call | solution.py:290
  (37 shorter events, 2.8 us)
Async XLA Ops:
  0.6 9.7 %all-to-all-start = ((bf16[8,8,256]{2,1,0:T(8,128)(2,1)}), bf16[8,8,256]{2,1,0:T(8,128)(2,1)S(1)}, u32[]{:S(2)}, u32[]{:S(2)}) async-start(bf16[8,8,256]{2,1,0:T(8,128)(2,1)} %bitcast.58), calls=%async_computation | async-start | bytes 65536 | tf_op jit(solution)/shard_map/all_to_all | solution.py:237
  11.4 16.6 %copy-start = (bf16[4,6,2,16,256]{4,3,2,1,0:T(8,128)(2,1)S(1)}, bf16[4,6,2,16,256]{4,3,2,1,0:T(8,128)(2,1)}, u32[]{:S(2)}) copy-start(bf16[4,6,2,16,256]{4,3,2,1,0:T(8,128)(2,1)} %param.6) | copy-start | bytes 1179652
  11.4 16.6 %copy-start.1 = (bf16[4,6,2,16,256]{4,3,2,1,0:T(8,128)(2,1)S(1)}, bf16[4,6,2,16,256]{4,3,2,1,0:T(8,128)(2,1)}, u32[]{:S(2)}) copy-start(bf16[4,6,2,16,256]{4,3,2,1,0:T(8,128)(2,1)} %param.5) | copy-start | bytes 1179652
  11.4 48.3 %all-to-all-start.1 = ((bf16[64,8,1152]{2,1,0:T(8,128)(2,1)}), bf16[64,8,1152]{2,1,0:T(8,128)(2,1)S(1)}, u32[]{:S(2)}, u32[]{:S(2)}) async-start(bf16[64,8,1152]{2,1,0:T(8,128)(2,1)} %shard_map.69), calls=%async_computation.1 | async-start | bytes 2359296 | tf_op jit(solution)/shard_map/all_to_all | solution.py:239
  28.0 4.6 %copy-start.7 = (s32[4]{0:T(128)S(1)}, s32[4]{0:T(128)}, u32[]{:S(2)}) copy-start(s32[4]{0:T(128)} %constant.403.clone) | copy-start | bytes 52
  28.2 33.7 %collective-permute-start = (bf16[2,4,3,2,16,256]{5,4,3,2,1,0:T(8,128)(2,1)S(1)}, bf16[2,4,3,2,16,256]{5,4,3,2,1,0:T(8,128)(2,1)S(1)}, u32[]{:S(2)}, u32[]{:S(2)}) collective-permute-start(bf16[2,4,3,2,16,256]{5,4,3,2,1,0:T(8,128)(2,1)S(1)} %pad_maximum_fusion), channel_id=1, source_target_pairs={{0,1},{1,0},{2,3},{3,2},{4,5},{5,4},{6,7},{7,6},{8,9},{9,8},{10,11... | collective-permute-start | bytes 1179656 | tf_op jit(solution)/shard_map/ppermute | solution.py:248
  59.8 5.4 %copy-start.4 = (bf16[1,3,2,16,256]{4,3,2,1,0:T(8,128)(2,1)S(1)}, bf16[1,3,2,16,256]{4,3,2,1,0:T(8,128)(2,1)}, u32[]{:S(2)}) copy-start(bf16[1,3,2,16,256]{4,3,2,1,0:T(8,128)(2,1)} %get-tuple-element.18) | copy-start | bytes 147460
  59.8 5.4 %copy-start.5 = (bf16[1,3,2,16,256]{4,3,2,1,0:T(8,128)(2,1)S(1)}, bf16[1,3,2,16,256]{4,3,2,1,0:T(8,128)(2,1)}, u32[]{:S(2)}) copy-start(bf16[1,3,2,16,256]{4,3,2,1,0:T(8,128)(2,1)} %get-tuple-element.37) | copy-start | bytes 147460
  59.8 8.1 %copy-start.2 = (bf16[1,3,2,16,256]{4,3,2,1,0:T(8,128)(2,1)S(1)}, bf16[1,3,2,16,256]{4,3,2,1,0:T(8,128)(2,1)}, u32[]{:S(2)}) copy-start(bf16[1,3,2,16,256]{4,3,2,1,0:T(8,128)(2,1)} %get-tuple-element.17) | copy-start | bytes 147460
  59.8 8.2 %copy-start.3 = (bf16[1,3,2,16,256]{4,3,2,1,0:T(8,128)(2,1)S(1)}, bf16[1,3,2,16,256]{4,3,2,1,0:T(8,128)(2,1)}, u32[]{:S(2)}) copy-start(bf16[1,3,2,16,256]{4,3,2,1,0:T(8,128)(2,1)} %get-tuple-element.38) | copy-start | bytes 147460
  59.8 20.6 %collective-permute-start.4 = (bf16[512,1152]{1,0:T(8,128)(2,1)S(1)}, bf16[512,1152]{1,0:T(8,128)(2,1)S(1)}, u32[]{:S(2)}, u32[]{:S(2)}) collective-permute-start(bf16[512,1152]{1,0:T(8,128)(2,1)S(1)} %bitcast.49), channel_id=1, source_target_pairs={{0,1},{1,0},{2,3},{3,2},{4,5},{5,4},{6,7},{7,6},{8,9},{9,8},{10,11... | collective-permute-start | bytes 3538952 | tf_op jit(solution)/shard_map/ppermute | solution.py:188
  61.9 10.7 %copy-start.6 = (s32[4]{0:T(128)S(1)}, s32[4]{0:T(128)}, u32[]{:S(2)}) copy-start(s32[4]{0:T(128)} %get-tuple-element.8) | copy-start | bytes 52
  62.0 12.0 %collective-permute-start.1 = (bf16[2,2,3,2,16,256]{5,4,3,2,1,0:T(8,128)(2,1)S(1)}, bf16[2,2,3,2,16,256]{5,4,3,2,1,0:T(8,128)(2,1)S(1)}, u32[]{:S(2)}, u32[]{:S(2)}) collective-permute-start(bf16[2,2,3,2,16,256]{5,4,3,2,1,0:T(8,128)(2,1)S(1)} %bitcast.56), channel_id=1, source_target_pairs={{0,2},{2,0},{256,258},{258,256},{1,3},{3,1},{257,259},{259,257},{4... | collective-permute-start | bytes 589832 | tf_op jit(solution)/shard_map/ppermute | solution.py:257
  65.2 10.2 %collective-permute-start.2 = (bf16[2,2,3,2,16,256]{5,4,3,2,1,0:T(8,128)(2,1)S(1)}, bf16[2,2,3,2,16,256]{5,4,3,2,1,0:T(8,128)(2,1)S(1)}, u32[]{:S(2)}, u32[]{:S(2)}) collective-permute-start(bf16[2,2,3,2,16,256]{5,4,3,2,1,0:T(8,128)(2,1)S(1)} %bitcast.57), channel_id=1, source_target_pairs={{0,256},{2,258},{256,0},{258,2},{1,257},{3,259},{257,1},{259,3},{4... | collective-permute-start | bytes 589832 | tf_op jit(solution)/shard_map/ppermute | solution.py:257
  68.6 10.0 %collective-permute-start.3 = (bf16[2,2,3,2,16,256]{5,4,3,2,1,0:T(8,128)(2,1)}, bf16[2,2,3,2,16,256]{5,4,3,2,1,0:T(8,128)(2,1)S(1)}, u32[]{:S(2)}, u32[]{:S(2)}) collective-permute-start(bf16[2,2,3,2,16,256]{5,4,3,2,1,0:T(8,128)(2,1)} %bitcast.27), channel_id=1, source_target_pairs={{0,258},{2,256},{256,2},{258,0},{1,259},{3,257},{257,3},{259,1},{4... | collective-permute-start | bytes 589832 | tf_op jit(solution)/shard_map/ppermute | solution.py:257
  93.8 19.2 %all-to-all-start.3 = ((bf16[32,24,128]{2,1,0:T(8,128)(2,1)}), bf16[32,24,128]{2,1,0:T(8,128)(2,1)S(1)}, u32[]{:S(2)}, u32[]{:S(2)}) async-start(bf16[32,24,128]{2,1,0:T(8,128)(2,1)} %shard_map.73), calls=%async_computation.3 | async-start | bytes 393216 | tf_op jit(solution)/shard_map/all_to_all | solution.py:286

commit v11 on v9

--- a/solution.py
+++ b/solution.py
@@ -94,7 +94,8 @@
         if d < 0 or d > 4 - half:
             return zero
         lane = half * SENT * BLK + d * BLK
-        return w_ref[i * BLK : (i + 1) * BLK, lane : lane + BLK]
+        starts = [yh * 128 + i * 32 + zl * 16 for zl in range(2) for yh in range(4)]
+        return jnp.concatenate([w_ref[at : at + 16, lane : lane + BLK] for at in starts], 0)
 
     first = j - 4 if j >= 4 else j - 3
     direct = jnp.concatenate(
@@ -230,7 +231,7 @@
     z, yh = lax.axis_index("z"), lax.axis_index("yh")
     w = lax.all_to_all(screened.reshape(8, 8, 256), ("xl", "xh", "c"), 0, 0)
     w = fanned((z // 2).astype(jnp.int32).reshape(1), w)
-    w = lax.all_to_all(w, ("z", "yh", "yl"), 0, 0)
+    w = lax.all_to_all(w, ("yh", "z", "yl"), 0, 0)
     own = w.reshape(NG // 2, (2 * SENT - 1) * BLK)
 
     x = xl * 2 + lax.axis_index("xh")
@@ -256,6 +257,7 @@
     other = xl ^ ((here + row_step) // 32 % 2)
     begin = (6 * yl - col_step + 12) % 12
     source = (here - row_step) % 32
+    source = source % 4 * 8 + source // 4
     col = (begin[:, None] + jnp.arange(KQ)) % 12
     base = jnp.array([0, 2, 8, 10])[:, None]
     slot = base + col // 6 * 4 + col % 6 // 3
@@ -277,7 +279,7 @@
         scratch_shapes=[pltpu.VMEM((Q * KQ, 128), F32)],
         compiler_params=kept,
     )(at, got)
-    came = lax.all_to_all(pay, ("z", "yh"), 0, 0)
+    came = lax.all_to_all(pay, ("yh", "z"), 0, 0)
     forward = pl.pallas_call(
         pick_forward, out_shape=out, in_specs=[sm, vm], out_specs=vm, compiler_params=kept
     )(at, got)

time: 115 us -> 115 us (level)
  the two profiles are of different devices: /device:TPU:16 before, /device:TPU:8 now
where the time goes in v11:
time: 115 us; the launch traced here: 114 us
  waiting for transfers between devices  48.6 us (42%)
  starting transfers between devices  40.6 us (35%)
  blocking collectives  9.72 us (8%)
  Pallas kernels  8.42 us (7%)
  other arithmetic  3.76 us (3%)
  local copies, waits for them, and re-layouts  1.99 us (2%)
    all_to_all x1, waiting for transfers between devices, local(): w = lax.all_to_all(w, ('yh', 'z', 'yl'), 0, 0)  26.3 us
    all_to_all x1, starting transfers between devices, local(): w = lax.all_to_all(w, ('yh', 'z', 'yl'), 0, 0)  16.7 us
    all_to_all x1, waiting for transfers between devices, local(): came = lax.all_to_all(pay, ('yh', 'z'), 0, 0)  12.3 us
    ppermute x3, starting transfers between devices, local(): piece = lax.ppermute(piece, ('xl', 'xh'), [(i, i ^ s) for i in range(4)])  9.81 us
    all_to_all x1, blocking collectives, local(): got = lax.all_to_all(slots, ('xl', 'yl', 'xh', 'c'), 0, 0)  9.72 us
    all_to_all x1, starting transfers between devices, local(): came = lax.all_to_all(pay, ('yh', 'z'), 0, 0)  5.77 us
    all_to_all x1, waiting for transfers between devices, local(): w = lax.all_to_all(screened.reshape(8, 8, 256), ('xl', 'xh', 'c'), 0, 0)  5.36 us
    ppermute x3, waiting for transfers between devices, local(): piece = lax.ppermute(piece, ('xl', 'xh'), [(i, i ^ s) for i in range(4)])  4.65 us
  transfers between devices with their start and end apart: 8, of which 5 were waited for; matrix products, arithmetic and copies ran while one was open for 5% of the time, Pallas kernels for 3%

profile of v11, /device:TPU:8, one launch (start us, length us, event | category | flops | bytes accessed | tf_op | source)
XLA Modules:
  0.0 114.0 jit_solution(7726454477408231813)
XLA Ops:
  0.6 4.3 %all-to-all-start = ((bf16[8,8,256]{2,1,0:T(8,128)(2,1)}), bf16[8,8,256]{2,1,0:T(8,128)(2,1)S(1)}, u32[]{:S(2)}, u32[]{:S(2)}) async-start(bf16[8,8,256]{2,1,0:T(8,128)(2,1)} %bitcast.58), calls=%async_computation | async-start | bytes 65536 | tf_op jit(solution)/shard_map/all_to_all | solution.py:232
  4.9 5.4 %all-to-all-done.w_ref = bf16[8,8,256]{2,1,0:T(8,128)(2,1)S(1)} async-done(((bf16[8,8,256]{2,1,0:T(8,128)(2,1)}), bf16[8,8,256]{2,1,0:T(8,128)(2,1)S(1)}, u32[]{:S(2)}, u32[]{:S(2)}) %all-to-all-start) | async-done | bytes 32800 | tf_op jit(solution)/shard_map/all_to_all | solution.py:232
  10.3 1.1 shard_map.69
  11.4 16.7 %all-to-all-start.1 = ((bf16[64,8,1152]{2,1,0:T(8,128)(2,1)}), bf16[64,8,1152]{2,1,0:T(8,128)(2,1)S(1)}, u32[]{:S(2)}, u32[]{:S(2)}) async-start(bf16[64,8,1152]{2,1,0:T(8,128)(2,1)} %shard_map.69), calls=%async_computation.1 | async-start | bytes 2359296 | tf_op jit(solution)/shard_map/all_to_all | solution.py:234
  28.3 1.9 %collective-permute-start = (bf16[2,4,3,2,16,256]{5,4,3,2,1,0:T(8,128)(2,1)S(1)}, bf16[2,4,3,2,16,256]{5,4,3,2,1,0:T(8,128)(2,1)S(1)}, u32[]{:S(2)}, u32[]{:S(2)}) collective-permute-start(bf16[2,4,3,2,16,256]{5,4,3,2,1,0:T(8,128)(2,1)S(1)} %pad_maximum_fusion), channel_id=1, source_target_pairs={{0,1},{1,0},{2,3},{3,2},{4,5},{5,4},{6,7},{7,6},{8,9},{9,8},{10,11... | collective-permute-start | bytes 1179656 | tf_op jit(solution)/shard_map/ppermute | solution.py:243
  30.2 0.8 fusion.19
  31.0 1.4 %fusion.18 = (s32[4]{0:T(128)}, s32[4]{0:T(128)S(1)}, s32[4]{0:T(128)S(1)}) fusion(s32[4,768]{1,0:T(4,128)} %param.8, pred[4,1]{1,0:T(4,128)(4,1)S(1)} %get-tuple-element.12, s32[]{:T(128)S(6)} %add.218, s32[]{:T(128)} %axis_index.63, s32[]{:T(128)S(6)} %mul.22), kind=kLoop, calls=%fused_computation.70 | loop fusion | flops 184 | bytes 80 | tf_op jit(solution)/shard_map/jit(floor_divide)/div | solution.py:255
  33.6 26.3 %all-to-all-done.1 = bf16[64,8,1152]{2,1,0:T(8,128)(2,1)S(1)} async-done(((bf16[64,8,1152]{2,1,0:T(8,128)(2,1)}), bf16[64,8,1152]{2,1,0:T(8,128)(2,1)S(1)}, u32[]{:S(2)}, u32[]{:S(2)}) %all-to-all-start.1) | async-done | bytes 1179680 | tf_op jit(solution)/shard_map/all_to_all | solution.py:234
  59.9 2.1 %collective-permute-start.4 = (bf16[512,1152]{1,0:T(8,128)(2,1)S(1)}, bf16[512,1152]{1,0:T(8,128)(2,1)S(1)}, u32[]{:S(2)}, u32[]{:S(2)}) collective-permute-start(bf16[512,1152]{1,0:T(8,128)(2,1)S(1)} %bitcast.49), channel_id=1, source_target_pairs={{0,1},{1,0},{2,3},{3,2},{4,5},{5,4},{6,7},{7,6},{8,9},{9,8},{10,11... | collective-permute-start | bytes 3538952 | tf_op jit(solution)/shard_map/ppermute | solution.py:183
  62.2 3.2 %collective-permute-start.1 = (bf16[2,2,3,2,16,256]{5,4,3,2,1,0:T(8,128)(2,1)S(1)}, bf16[2,2,3,2,16,256]{5,4,3,2,1,0:T(8,128)(2,1)S(1)}, u32[]{:S(2)}, u32[]{:S(2)}) collective-permute-start(bf16[2,2,3,2,16,256]{5,4,3,2,1,0:T(8,128)(2,1)S(1)} %bitcast.56), channel_id=1, source_target_pairs={{0,2},{2,0},{256,258},{258,256},{1,3},{3,1},{257,259},{259,257},{4... | collective-permute-start | bytes 589832 | tf_op jit(solution)/shard_map/ppermute | solution.py:252
  65.4 2.7 %collective-permute-start.2 = (bf16[2,2,3,2,16,256]{5,4,3,2,1,0:T(8,128)(2,1)S(1)}, bf16[2,2,3,2,16,256]{5,4,3,2,1,0:T(8,128)(2,1)S(1)}, u32[]{:S(2)}, u32[]{:S(2)}) collective-permute-start(bf16[2,2,3,2,16,256]{5,4,3,2,1,0:T(8,128)(2,1)S(1)} %bitcast.57), channel_id=1, source_target_pairs={{0,256},{2,258},{256,0},{258,2},{1,257},{3,259},{257,1},{259,3},{4... | collective-permute-start | bytes 589832 | tf_op jit(solution)/shard_map/ppermute | solution.py:252
  68.8 4.0 %collective-permute-start.3 = (bf16[2,2,3,2,16,256]{5,4,3,2,1,0:T(8,128)(2,1)}, bf16[2,2,3,2,16,256]{5,4,3,2,1,0:T(8,128)(2,1)S(1)}, u32[]{:S(2)}, u32[]{:S(2)}) collective-permute-start(bf16[2,2,3,2,16,256]{5,4,3,2,1,0:T(8,128)(2,1)} %bitcast.27), channel_id=1, source_target_pairs={{0,258},{2,256},{256,2},{258,0},{1,259},{3,257},{257,3},{259,1},{4... | collective-permute-start | bytes 589832 | tf_op jit(solution)/shard_map/ppermute | solution.py:252
  73.4 0.8 concatenate.3.at_ref
  74.2 1.4 %collective-permute-done.2.refs_2_ = bf16[2,2,3,2,16,256]{5,4,3,2,1,0:T(8,128)(2,1)S(1)} collective-permute-done((bf16[2,2,3,2,16,256]{5,4,3,2,1,0:T(8,128)(2,1)S(1)}, bf16[2,2,3,2,16,256]{5,4,3,2,1,0:T(8,128)(2,1)S(1)}, u32[]{:S(2)}, u32[]{:S(2)}) %collective-permute-start.2) | collective-permute-done | bytes 196640 | tf_op jit(solution)/shard_map/ppermute | solution.py:252
  75.6 3.3 %collective-permute-done.3.refs_3_ = bf16[2,2,3,2,16,256]{5,4,3,2,1,0:T(8,128)(2,1)S(1)} collective-permute-done((bf16[2,2,3,2,16,256]{5,4,3,2,1,0:T(8,128)(2,1)}, bf16[2,2,3,2,16,256]{5,4,3,2,1,0:T(8,128)(2,1)S(1)}, u32[]{:S(2)}, u32[]{:S(2)}) %collective-permute-start.3) | collective-permute-done | bytes 196640 | tf_op jit(solution)/shard_map/ppermute | solution.py:252
  78.8 0.8 shard_map.68
  79.6 0.9 shard_map.70.p_ref
  80.5 1.9 %shard_map.71 = f32[16,6,128]{2,1,0:T(8,128)S(1)} custom-call(bf16[192,1024]{1,0:T(8,128)(2,1)S(1)} %get-tuple-element.5.left_ref, bf16[192,1024]{1,0:T(8,128)(2,1)S(1)} %get-tuple-element.6.flip_ref, bf16[192,1024]{1,0:T(8,128)(2,1)S(1)} %get-tuple-element.7.val_ref, f32[192,1024]{1,0:T(8,128)S(1)} %shard_map.70.p_ref, ...), custom_call_target="tpu_custom_call" | custom-call | flops 800000000 | bytes 2000000 | tf_op jit(solution)/shard_map/pallas_call | solution.py:192
  82.4 9.7 %all_to_all.20.got_ref = f32[16,6,128]{2,1,0:T(8,128)S(1)} all-to-all(f32[16,6,128]{2,1,0:T(8,128)S(1)} %shard_map.71), channel_id=1, replica_groups=mesh['xl'=2,'z'=8,'yh'=4,'yl'=2,'xh'=2,'c'=2] {'xl','yl','xh','c'}, dimensions={0} | all-to-all | bytes 98304 | tf_op jit(solution)/shard_map/all_to_all | solution.py:269
  92.1 1.3 %shard_map.73 = bf16[32,24,128]{2,1,0:T(8,128)(2,1)} custom-call(s32[56]{0:T(128)S(1)} %concatenate.3.at_ref, f32[16,6,128]{2,1,0:T(8,128)S(1)} %all_to_all.20.got_ref), custom_call_target="tpu_custom_call" | custom-call | tf_op jit(solution)/shard_map/pallas_call | solution.py:274
  93.4 5.8 %all-to-all-start.3 = ((bf16[32,24,128]{2,1,0:T(8,128)(2,1)}), bf16[32,24,128]{2,1,0:T(8,128)(2,1)S(1)}, u32[]{:S(2)}, u32[]{:S(2)}) async-start(bf16[32,24,128]{2,1,0:T(8,128)(2,1)} %shard_map.73), calls=%async_computation.3 | async-start | bytes 393216 | tf_op jit(solution)/shard_map/all_to_all | solution.py:282
  99.2 1.2 %shard_map.72 = f32[4,6,2,64]{3,2,1,0:T(2,128)} custom-call(s32[56]{0:T(128)S(1)} %concatenate.3.at_ref, f32[16,6,128]{2,1,0:T(8,128)S(1)} %all_to_all.20.got_ref), custom_call_target="tpu_custom_call" | custom-call | tf_op jit(solution)/shard_map/pallas_call | solution.py:283
  100.4 12.3 %all-to-all-done.3.came_ref = bf16[32,24,128]{2,1,0:T(8,128)(2,1)S(1)} async-done(((bf16[32,24,128]{2,1,0:T(8,128)(2,1)}), bf16[32,24,128]{2,1,0:T(8,128)(2,1)S(1)}, u32[]{:S(2)}, u32[]{:S(2)}) %all-to-all-start.3) | async-done | bytes 196640 | tf_op jit(solution)/shard_map/all_to_all | solution.py:282
  112.7 1.2 %shard_map.74 = f32[4,6,2,64]{3,2,1,0:T(2,128)} custom-call(s32[56]{0:T(128)S(1)} %concatenate.3.at_ref, bf16[32,24,128]{2,1,0:T(8,128)(2,1)S(1)} %all-to-all-done.3.came_ref), custom_call_target="tpu_custom_call" | custom-call | tf_op jit(solution)/shard_map/pallas_call | solution.py:286
  (37 shorter events, 2.8 us)
Async XLA Ops:
  0.6 9.7 %all-to-all-start = ((bf16[8,8,256]{2,1,0:T(8,128)(2,1)}), bf16[8,8,256]{2,1,0:T(8,128)(2,1)S(1)}, u32[]{:S(2)}, u32[]{:S(2)}) async-start(bf16[8,8,256]{2,1,0:T(8,128)(2,1)} %bitcast.58), calls=%async_computation | async-start | bytes 65536 | tf_op jit(solution)/shard_map/all_to_all | solution.py:232
  11.4 16.7 %copy-start = (bf16[4,6,2,16,256]{4,3,2,1,0:T(8,128)(2,1)S(1)}, bf16[4,6,2,16,256]{4,3,2,1,0:T(8,128)(2,1)}, u32[]{:S(2)}) copy-start(bf16[4,6,2,16,256]{4,3,2,1,0:T(8,128)(2,1)} %param.6) | copy-start | bytes 1179652
  11.4 16.8 %copy-start.1 = (bf16[4,6,2,16,256]{4,3,2,1,0:T(8,128)(2,1)S(1)}, bf16[4,6,2,16,256]{4,3,2,1,0:T(8,128)(2,1)}, u32[]{:S(2)}) copy-start(bf16[4,6,2,16,256]{4,3,2,1,0:T(8,128)(2,1)} %param.5) | copy-start | bytes 1179652
  11.4 48.5 %all-to-all-start.1 = ((bf16[64,8,1152]{2,1,0:T(8,128)(2,1)}), bf16[64,8,1152]{2,1,0:T(8,128)(2,1)S(1)}, u32[]{:S(2)}, u32[]{:S(2)}) async-start(bf16[64,8,1152]{2,1,0:T(8,128)(2,1)} %shard_map.69), calls=%async_computation.1 | async-start | bytes 2359296 | tf_op jit(solution)/shard_map/all_to_all | solution.py:234
  28.2 4.6 %copy-start.7 = (s32[4]{0:T(128)S(1)}, s32[4]{0:T(128)}, u32[]{:S(2)}) copy-start(s32[4]{0:T(128)} %constant.421.clone) | copy-start | bytes 52
  28.3 33.7 %collective-permute-start = (bf16[2,4,3,2,16,256]{5,4,3,2,1,0:T(8,128)(2,1)S(1)}, bf16[2,4,3,2,16,256]{5,4,3,2,1,0:T(8,128)(2,1)S(1)}, u32[]{:S(2)}, u32[]{:S(2)}) collective-permute-start(bf16[2,4,3,2,16,256]{5,4,3,2,1,0:T(8,128)(2,1)S(1)} %pad_maximum_fusion), channel_id=1, source_target_pairs={{0,1},{1,0},{2,3},{3,2},{4,5},{5,4},{6,7},{7,6},{8,9},{9,8},{10,11... | collective-permute-start | bytes 1179656 | tf_op jit(solution)/shard_map/ppermute | solution.py:243
  59.9 5.4 %copy-start.4 = (bf16[1,3,2,16,256]{4,3,2,1,0:T(8,128)(2,1)S(1)}, bf16[1,3,2,16,256]{4,3,2,1,0:T(8,128)(2,1)}, u32[]{:S(2)}) copy-start(bf16[1,3,2,16,256]{4,3,2,1,0:T(8,128)(2,1)} %get-tuple-element.18) | copy-start | bytes 147460
  59.9 5.4 %copy-start.5 = (bf16[1,3,2,16,256]{4,3,2,1,0:T(8,128)(2,1)S(1)}, bf16[1,3,2,16,256]{4,3,2,1,0:T(8,128)(2,1)}, u32[]{:S(2)}) copy-start(bf16[1,3,2,16,256]{4,3,2,1,0:T(8,128)(2,1)} %get-tuple-element.37) | copy-start | bytes 147460
  59.9 8.1 %copy-start.2 = (bf16[1,3,2,16,256]{4,3,2,1,0:T(8,128)(2,1)S(1)}, bf16[1,3,2,16,256]{4,3,2,1,0:T(8,128)(2,1)}, u32[]{:S(2)}) copy-start(bf16[1,3,2,16,256]{4,3,2,1,0:T(8,128)(2,1)} %get-tuple-element.17) | copy-start | bytes 147460
  59.9 8.2 %copy-start.3 = (bf16[1,3,2,16,256]{4,3,2,1,0:T(8,128)(2,1)S(1)}, bf16[1,3,2,16,256]{4,3,2,1,0:T(8,128)(2,1)}, u32[]{:S(2)}) copy-start(bf16[1,3,2,16,256]{4,3,2,1,0:T(8,128)(2,1)} %get-tuple-element.38) | copy-start | bytes 147460
  59.9 20.6 %collective-permute-start.4 = (bf16[512,1152]{1,0:T(8,128)(2,1)S(1)}, bf16[512,1152]{1,0:T(8,128)(2,1)S(1)}, u32[]{:S(2)}, u32[]{:S(2)}) collective-permute-start(bf16[512,1152]{1,0:T(8,128)(2,1)S(1)} %bitcast.49), channel_id=1, source_target_pairs={{0,1},{1,0},{2,3},{3,2},{4,5},{5,4},{6,7},{7,6},{8,9},{9,8},{10,11... | collective-permute-start | bytes 3538952 | tf_op jit(solution)/shard_map/ppermute | solution.py:183
  62.0 10.7 %copy-start.6 = (s32[4]{0:T(128)S(1)}, s32[4]{0:T(128)}, u32[]{:S(2)}) copy-start(s32[4]{0:T(128)} %get-tuple-element.8) | copy-start | bytes 52
  62.2 12.0 %collective-permute-start.1 = (bf16[2,2,3,2,16,256]{5,4,3,2,1,0:T(8,128)(2,1)S(1)}, bf16[2,2,3,2,16,256]{5,4,3,2,1,0:T(8,128)(2,1)S(1)}, u32[]{:S(2)}, u32[]{:S(2)}) collective-permute-start(bf16[2,2,3,2,16,256]{5,4,3,2,1,0:T(8,128)(2,1)S(1)} %bitcast.56), channel_id=1, source_target_pairs={{0,2},{2,0},{256,258},{258,256},{1,3},{3,1},{257,259},{259,257},{4... | collective-permute-start | bytes 589832 | tf_op jit(solution)/shard_map/ppermute | solution.py:252
  65.4 10.2 %collective-permute-start.2 = (bf16[2,2,3,2,16,256]{5,4,3,2,1,0:T(8,128)(2,1)S(1)}, bf16[2,2,3,2,16,256]{5,4,3,2,1,0:T(8,128)(2,1)S(1)}, u32[]{:S(2)}, u32[]{:S(2)}) collective-permute-start(bf16[2,2,3,2,16,256]{5,4,3,2,1,0:T(8,128)(2,1)S(1)} %bitcast.57), channel_id=1, source_target_pairs={{0,256},{2,258},{256,0},{258,2},{1,257},{3,259},{257,1},{259,3},{4... | collective-permute-start | bytes 589832 | tf_op jit(solution)/shard_map/ppermute | solution.py:252
  68.8 10.0 %collective-permute-start.3 = (bf16[2,2,3,2,16,256]{5,4,3,2,1,0:T(8,128)(2,1)}, bf16[2,2,3,2,16,256]{5,4,3,2,1,0:T(8,128)(2,1)S(1)}, u32[]{:S(2)}, u32[]{:S(2)}) collective-permute-start(bf16[2,2,3,2,16,256]{5,4,3,2,1,0:T(8,128)(2,1)} %bitcast.27), channel_id=1, source_target_pairs={{0,258},{2,256},{256,2},{258,0},{1,259},{3,257},{257,3},{259,1},{4... | collective-permute-start | bytes 589832 | tf_op jit(solution)/shard_map/ppermute | solution.py:252
  93.4 19.3 %all-to-all-start.3 = ((bf16[32,24,128]{2,1,0:T(8,128)(2,1)}), bf16[32,24,128]{2,1,0:T(8,128)(2,1)S(1)}, u32[]{:S(2)}, u32[]{:S(2)}) async-start(bf16[32,24,128]{2,1,0:T(8,128)(2,1)} %shard_map.73), calls=%async_computation.3 | async-start | bytes 393216 | tf_op jit(solution)/shard_map/all_to_all | solution.py:282

commit v12 on v11

--- a/solution.py
+++ b/solution.py
@@ -128,14 +128,31 @@
     return nn(lanes(ahead, first, j + 2 - first), direct), nt(lanes(behind, j + 1, width), mirrored)
 
 
-def contract_own(left_ref, flip_ref, own_ref, p_ref):
+def contract_own(left_ref, flip_ref, own_ref, p_ref, same_ref, e1_ref, e2_ref, e3_ref):
     left, flipped = wrapped(left_ref[...]), wrapped(flip_ref[...])
     for j in range(0, NB, 2):
         fore, back = screened_pair(own_ref, left, flipped, j)
         p_ref[:, j * BLK : (j + 2) * BLK] = fore + back
 
 
-def contract(left_ref, flip_ref, val_ref, p_ref, oth_ref, out_ref):
+    rows = left_ref.shape[0]
+    half = rows // 2
+    r = lax.broadcasted_iota(jnp.int32, (half, rows), 0)
+    c = lax.broadcasted_iota(jnp.int32, (half, rows), 1)
+    same_ref[...] = jnp.where((r >> 4) == (c >> 5), 1.0, 0.0)
+    c = lax.broadcasted_iota(jnp.int32, (rows, 128), 0)
+    l = lax.broadcasted_iota(jnp.int32, (rows, 128), 1)
+    hit = (c & 15) == (l & 15)
+    part = (c >> 4) & 1
+    want = l >> 6
+    e1_ref[...] = jnp.where(hit & (part == want), 1.0, 0.0)
+    e2_ref[...] = jnp.where(hit & (part != want), jnp.where(want == 0, -1.0, 1.0), 0.0)
+    o = lax.broadcasted_iota(jnp.int32, (4 * 8, half), 0)
+    r = lax.broadcasted_iota(jnp.int32, (4 * 8, half), 1)
+    e3_ref[...] = jnp.where(((r >> 4) == (o & 7)) & (((r & 15) >> 2) == (o >> 3)), 1.0, 0.0)
+
+
+def contract(left_ref, flip_ref, val_ref, p_ref, same_ref, e1_ref, e2_ref, e3_ref, oth_ref, out_ref):
     rows = left_ref.shape[0]
     half = rows // 2
     left, flipped = wrapped(left_ref[...]), wrapped(flip_ref[...])
@@ -151,26 +168,14 @@
         val = val_ref[:, columns]
         g1 += nt(x_real, val)
         g2 += nt(x_imag, val)
-    r = lax.broadcasted_iota(jnp.int32, (half, rows), 0)
-    c = lax.broadcasted_iota(jnp.int32, (half, rows), 1)
-    same = r // PAIR == c // (2 * PAIR)
+    same = same_ref[...] > 0.0
     g1 = jnp.where(same, g1, 0.0)
     g2 = jnp.where(same, g2, 0.0)
-    c = lax.broadcasted_iota(jnp.int32, (rows, 128), 0)
-    l = lax.broadcasted_iota(jnp.int32, (rows, 128), 1)
-    hit = c % PAIR == l % PAIR
-    part = (c // PAIR) % 2
-    want = l // 64
-    e1 = jnp.where(hit & (part == want), 1.0, 0.0)
-    e2 = jnp.where(hit & (part != want), jnp.where(want == 0, -1.0, 1.0), 0.0)
-    t = nn(g1, e1, lax.Precision.HIGHEST) + nn(g2, e2, lax.Precision.HIGHEST)
+    t = nn(g1, e1_ref[...], lax.Precision.HIGHEST) + nn(g2, e2_ref[...], lax.Precision.HIGHEST)
     r = lax.broadcasted_iota(jnp.int32, (half, 128), 0)
     l = lax.broadcasted_iota(jnp.int32, (half, 128), 1)
-    t = jnp.where(r % 4 == (l // PAIR) % 4, t, 0.0)
-    o = lax.broadcasted_iota(jnp.int32, (4 * 8, half), 0)
-    r = lax.broadcasted_iota(jnp.int32, (4 * 8, half), 1)
-    e3 = jnp.where((r // PAIR == o % 8) & ((r % PAIR) // 4 == o // 8), 1.0, 0.0)
-    block = nn(e3, t, lax.Precision.HIGHEST)
+    t = jnp.where((r & 3) == ((l >> 4) & 3), t, 0.0)
+    block = nn(e3_ref[...], t, lax.Precision.HIGHEST)
     for slot in range(16):
         g = slot % 4
         out_ref[slot, :, :] = block[g * 8 : g * 8 + KQ, :]
@@ -181,22 +186,23 @@
     kept = pltpu.CompilerParams(vmem_limit_bytes=24 << 20)
     cost = pl.CostEstimate(flops=800_000_000, bytes_accessed=2_000_000, transcendentals=0)
     oth = lax.ppermute(own, "c", [(0, 1), (1, 0)])
-    p = pl.pallas_call(
+    shapes = ((192, NG), (96, 192), (192, 128), (192, 128), (32, 96))
+    early = pl.pallas_call(
         contract_own,
-        out_shape=jax.ShapeDtypeStruct((2 * KQ * PAIR, NG), F32),
+        out_shape=tuple(jax.ShapeDtypeStruct(shape, F32) for shape in shapes),
         in_specs=[vm] * 3,
-        out_specs=vm,
+        out_specs=(vm,) * 5,
         compiler_params=kept,
         cost_estimate=cost,
     )(left, flipped, own)
     return pl.pallas_call(
         contract,
         out_shape=jax.ShapeDtypeStruct((16, KQ, 128), F32),
-        in_specs=[vm] * 5,
+        in_specs=[vm] * 9,
         out_specs=vm,
         compiler_params=kept,
         cost_estimate=cost,
-    )(left, flipped, val, p, oth)
+    )(left, flipped, val, *early, oth)
 
 
 def pick_rows(at_ref, got_ref, pay_ref, row_ref):
@@ -257,7 +263,6 @@
     other = xl ^ ((here + row_step) // 32 % 2)
     begin = (6 * yl - col_step + 12) % 12
     source = (here - row_step) % 32
-    source = source % 4 * 8 + source // 4
     col = (begin[:, None] + jnp.arange(KQ)) % 12
     base = jnp.array([0, 2, 8, 10])[:, None]
     slot = base + col // 6 * 4 + col % 6 // 3
@@ -279,7 +284,7 @@
         scratch_shapes=[pltpu.VMEM((Q * KQ, 128), F32)],
         compiler_params=kept,
     )(at, got)
-    came = lax.all_to_all(pay, ("yh", "z"), 0, 0)
+    came = lax.all_to_all(pay, ("z", "yh"), 0, 0)
     forward = pl.pallas_call(
         pick_forward, out_shape=out, in_specs=[sm, vm], out_specs=vm, compiler_params=kept
     )(at, got)

time: 115 us -> 115 us (level)
  the two profiles are of different devices: /device:TPU:8 before, /device:TPU:16 now
where the time goes in v12:
time: 115 us; the launch traced here: 114 us
  waiting for transfers between devices  46.5 us (40%)
  starting transfers between devices  42 us (37%)
  blocking collectives  10.6 us (9%)
  Pallas kernels  8.44 us (7%)
  other arithmetic  3.65 us (3%)
  local copies, waits for them, and re-layouts  1.91 us (2%)
    all_to_all x1, waiting for transfers between devices, local(): w = lax.all_to_all(w, ('yh', 'z', 'yl'), 0, 0)  25 us
    all_to_all x1, starting transfers between devices, local(): w = lax.all_to_all(w, ('yh', 'z', 'yl'), 0, 0)  16.6 us
    all_to_all x1, waiting for transfers between devices, local(): came = lax.all_to_all(pay, ('z', 'yh'), 0, 0)  11.5 us
    all_to_all x1, blocking collectives, local(): got = lax.all_to_all(slots, ('xl', 'yl', 'xh', 'c'), 0, 0)  10.6 us
    ppermute x3, starting transfers between devices, local(): piece = lax.ppermute(piece, ('xl', 'xh'), [(i, i ^ s) for i in range(4)])  9.81 us
    all_to_all x1, starting transfers between devices, local(): came = lax.all_to_all(pay, ('z', 'yh'), 0, 0)  7.32 us
    all_to_all x1, waiting for transfers between devices, local(): w = lax.all_to_all(screened.reshape(8, 8, 256), ('xl', 'xh', 'c'), 0, 0)  5.36 us
    ppermute x3, waiting for transfers between devices, local(): piece = lax.ppermute(piece, ('xl', 'xh'), [(i, i ^ s) for i in range(4)])  4.77 us
  transfers between devices with their start and end apart: 8, of which 5 were waited for; matrix products, arithmetic and copies ran while one was open for 5% of the time, Pallas kernels for 3%

profile of v12, /device:TPU:16, one launch (start us, length us, event | category | flops | bytes accessed | tf_op | source)
XLA Modules:
  0.0 114.0 jit_solution(13909212273792791999)
XLA Ops:
  0.6 4.3 %all-to-all-start = ((bf16[8,8,256]{2,1,0:T(8,128)(2,1)}), bf16[8,8,256]{2,1,0:T(8,128)(2,1)S(1)}, u32[]{:S(2)}, u32[]{:S(2)}) async-start(bf16[8,8,256]{2,1,0:T(8,128)(2,1)} %bitcast.58), calls=%async_computation | async-start | bytes 65536 | tf_op jit(solution)/shard_map/all_to_all | solution.py:238
  4.9 5.4 %all-to-all-done.w_ref = bf16[8,8,256]{2,1,0:T(8,128)(2,1)S(1)} async-done(((bf16[8,8,256]{2,1,0:T(8,128)(2,1)}), bf16[8,8,256]{2,1,0:T(8,128)(2,1)S(1)}, u32[]{:S(2)}, u32[]{:S(2)}) %all-to-all-start) | async-done | bytes 32800 | tf_op jit(solution)/shard_map/all_to_all | solution.py:238
  10.3 1.1 %shard_map.69 = bf16[64,8,1152]{2,1,0:T(8,128)(2,1)} custom-call(s32[1]{0:T(128)} %bitcast.28.at_ref, bf16[8,8,256]{2,1,0:T(8,128)(2,1)S(1)} %all-to-all-done.w_ref), custom_call_target="tpu_custom_call" | custom-call | tf_op jit(solution)/shard_map/pallas_call | solution.py:45
  11.4 16.6 %all-to-all-start.1 = ((bf16[64,8,1152]{2,1,0:T(8,128)(2,1)}), bf16[64,8,1152]{2,1,0:T(8,128)(2,1)S(1)}, u32[]{:S(2)}, u32[]{:S(2)}) async-start(bf16[64,8,1152]{2,1,0:T(8,128)(2,1)} %shard_map.69), calls=%async_computation.1 | async-start | bytes 2359296 | tf_op jit(solution)/shard_map/all_to_all | solution.py:240
  28.2 1.9 %collective-permute-start = (bf16[2,4,3,2,16,256]{5,4,3,2,1,0:T(8,128)(2,1)S(1)}, bf16[2,4,3,2,16,256]{5,4,3,2,1,0:T(8,128)(2,1)S(1)}, u32[]{:S(2)}, u32[]{:S(2)}) collective-permute-start(bf16[2,4,3,2,16,256]{5,4,3,2,1,0:T(8,128)(2,1)S(1)} %pad_maximum_fusion), channel_id=1, source_target_pairs={{0,1},{1,0},{2,3},{3,2},{4,5},{5,4},{6,7},{7,6},{8,9},{9,8},{10,11... | collective-permute-start | bytes 1179656 | tf_op jit(solution)/shard_map/ppermute | solution.py:249
  30.1 0.8 fusion.17
  30.9 1.4 %fusion.16 = (s32[4]{0:T(128)}, s32[4]{0:T(128)S(1)}, s32[4]{0:T(128)S(1)}) fusion(s32[4,768]{1,0:T(4,128)} %param.8, pred[4,1]{1,0:T(4,128)(4,1)S(1)} %get-tuple-element.22, s32[]{:T(128)S(6)} %add.210, s32[]{:T(128)} %axis_index.63, s32[]{:T(128)S(6)} %mul.19), kind=kLoop, calls=%fused_computation.63 | loop fusion | flops 184 | bytes 80 | tf_op jit(solution)/shard_map/jit(floor_divide)/div | solution.py:261
  33.5 25.0 %all-to-all-done.1 = bf16[64,8,1152]{2,1,0:T(8,128)(2,1)S(1)} async-done(((bf16[64,8,1152]{2,1,0:T(8,128)(2,1)}), bf16[64,8,1152]{2,1,0:T(8,128)(2,1)S(1)}, u32[]{:S(2)}, u32[]{:S(2)}) %all-to-all-start.1) | async-done | bytes 1179680 | tf_op jit(solution)/shard_map/all_to_all | solution.py:240
  58.4 2.1 %collective-permute-start.4 = (bf16[512,1152]{1,0:T(8,128)(2,1)S(1)}, bf16[512,1152]{1,0:T(8,128)(2,1)S(1)}, u32[]{:S(2)}, u32[]{:S(2)}) collective-permute-start(bf16[512,1152]{1,0:T(8,128)(2,1)S(1)} %bitcast.49), channel_id=1, source_target_pairs={{0,1},{1,0},{2,3},{3,2},{4,5},{5,4},{6,7},{7,6},{8,9},{9,8},{10,11... | collective-permute-start | bytes 3538952 | tf_op jit(solution)/shard_map/ppermute | solution.py:188
  60.7 3.2 %collective-permute-start.1 = (bf16[2,2,3,2,16,256]{5,4,3,2,1,0:T(8,128)(2,1)S(1)}, bf16[2,2,3,2,16,256]{5,4,3,2,1,0:T(8,128)(2,1)S(1)}, u32[]{:S(2)}, u32[]{:S(2)}) collective-permute-start(bf16[2,2,3,2,16,256]{5,4,3,2,1,0:T(8,128)(2,1)S(1)} %bitcast.56), channel_id=1, source_target_pairs={{0,2},{2,0},{256,258},{258,256},{1,3},{3,1},{257,259},{259,257},{4... | collective-permute-start | bytes 589832 | tf_op jit(solution)/shard_map/ppermute | solution.py:258
  63.9 2.7 %collective-permute-start.2 = (bf16[2,2,3,2,16,256]{5,4,3,2,1,0:T(8,128)(2,1)S(1)}, bf16[2,2,3,2,16,256]{5,4,3,2,1,0:T(8,128)(2,1)S(1)}, u32[]{:S(2)}, u32[]{:S(2)}) collective-permute-start(bf16[2,2,3,2,16,256]{5,4,3,2,1,0:T(8,128)(2,1)S(1)} %bitcast.57), channel_id=1, source_target_pairs={{0,256},{2,258},{256,0},{258,2},{1,257},{3,259},{257,1},{259,3},{4... | collective-permute-start | bytes 589832 | tf_op jit(solution)/shard_map/ppermute | solution.py:258
  66.6 0.7 pad_maximum_fusion.4
  67.3 4.0 %collective-permute-start.3 = (bf16[2,2,3,2,16,256]{5,4,3,2,1,0:T(8,128)(2,1)}, bf16[2,2,3,2,16,256]{5,4,3,2,1,0:T(8,128)(2,1)S(1)}, u32[]{:S(2)}, u32[]{:S(2)}) collective-permute-start(bf16[2,2,3,2,16,256]{5,4,3,2,1,0:T(8,128)(2,1)} %bitcast.27), channel_id=1, source_target_pairs={{0,258},{2,256},{256,2},{258,0},{1,259},{3,257},{257,3},{259,1},{4... | collective-permute-start | bytes 589832 | tf_op jit(solution)/shard_map/ppermute | solution.py:258
  72.6 1.5 %collective-permute-done.2.refs_2_ = bf16[2,2,3,2,16,256]{5,4,3,2,1,0:T(8,128)(2,1)S(1)} collective-permute-done((bf16[2,2,3,2,16,256]{5,4,3,2,1,0:T(8,128)(2,1)S(1)}, bf16[2,2,3,2,16,256]{5,4,3,2,1,0:T(8,128)(2,1)S(1)}, u32[]{:S(2)}, u32[]{:S(2)}) %collective-permute-start.2) | collective-permute-done | bytes 196640 | tf_op jit(solution)/shard_map/ppermute | solution.py:258
  74.1 3.3 %collective-permute-done.3.refs_3_ = bf16[2,2,3,2,16,256]{5,4,3,2,1,0:T(8,128)(2,1)S(1)} collective-permute-done((bf16[2,2,3,2,16,256]{5,4,3,2,1,0:T(8,128)(2,1)}, bf16[2,2,3,2,16,256]{5,4,3,2,1,0:T(8,128)(2,1)S(1)}, u32[]{:S(2)}, u32[]{:S(2)}) %collective-permute-start.3) | collective-permute-done | bytes 196640 | tf_op jit(solution)/shard_map/ppermute | solution.py:258
  77.3 0.8 shard_map.68
  78.1 0.9 shard_map.70
  79.0 1.9 %shard_map.71 = f32[16,6,128]{2,1,0:T(8,128)S(1)} custom-call(bf16[192,1024]{1,0:T(8,128)(2,1)S(1)} %get-tuple-element.10.left_ref, bf16[192,1024]{1,0:T(8,128)(2,1)S(1)} %get-tuple-element.11.flip_ref, bf16[192,1024]{1,0:T(8,128)(2,1)S(1)} %get-tuple-element.12.val_ref, f32[192,1024]{1,0:T(8,128)S(1)} %get-tuple-element.13.p_ref, ...), custom_call_target="tpu_custom_call" | custom-call | flops 800000000 | bytes 2000000 | tf_op jit(solution)/shard_map/pallas_call | solution.py:198
  80.9 10.6 %all_to_all.20.got_ref = f32[16,6,128]{2,1,0:T(8,128)S(1)} all-to-all(f32[16,6,128]{2,1,0:T(8,128)S(1)} %shard_map.71), channel_id=1, replica_groups=mesh['xl'=2,'z'=8,'yh'=4,'yl'=2,'xh'=2,'c'=2] {'xl','yl','xh','c'}, dimensions={0} | all-to-all | bytes 98304 | tf_op jit(solution)/shard_map/all_to_all | solution.py:274
  91.5 1.3 %shard_map.73 = bf16[32,24,128]{2,1,0:T(8,128)(2,1)} custom-call(s32[56]{0:T(128)S(1)} %concatenate.3.at_ref, f32[16,6,128]{2,1,0:T(8,128)S(1)} %all_to_all.20.got_ref), custom_call_target="tpu_custom_call" | custom-call | tf_op jit(solution)/shard_map/pallas_call | solution.py:279
  92.7 7.3 %all-to-all-start.3 = ((bf16[32,24,128]{2,1,0:T(8,128)(2,1)}), bf16[32,24,128]{2,1,0:T(8,128)(2,1)S(1)}, u32[]{:S(2)}, u32[]{:S(2)}) async-start(bf16[32,24,128]{2,1,0:T(8,128)(2,1)} %shard_map.73), calls=%async_computation.3 | async-start | bytes 393216 | tf_op jit(solution)/shard_map/all_to_all | solution.py:287
  100.1 1.2 %shard_map.72 = f32[4,6,2,64]{3,2,1,0:T(2,128)} custom-call(s32[56]{0:T(128)S(1)} %concatenate.3.at_ref, f32[16,6,128]{2,1,0:T(8,128)S(1)} %all_to_all.20.got_ref), custom_call_target="tpu_custom_call" | custom-call | tf_op jit(solution)/shard_map/pallas_call | solution.py:288
  101.3 11.5 %all-to-all-done.3.came_ref = bf16[32,24,128]{2,1,0:T(8,128)(2,1)S(1)} async-done(((bf16[32,24,128]{2,1,0:T(8,128)(2,1)}), bf16[32,24,128]{2,1,0:T(8,128)(2,1)S(1)}, u32[]{:S(2)}, u32[]{:S(2)}) %all-to-all-start.3) | async-done | bytes 196640 | tf_op jit(solution)/shard_map/all_to_all | solution.py:287
  112.8 1.2 %shard_map.74 = f32[4,6,2,64]{3,2,1,0:T(2,128)} custom-call(s32[56]{0:T(128)S(1)} %concatenate.3.at_ref, bf16[32,24,128]{2,1,0:T(8,128)(2,1)S(1)} %all-to-all-done.3.came_ref), custom_call_target="tpu_custom_call" | custom-call | tf_op jit(solution)/shard_map/pallas_call | solution.py:291
  (37 shorter events, 2.7 us)
Async XLA Ops:
  0.6 9.7 %all-to-all-start = ((bf16[8,8,256]{2,1,0:T(8,128)(2,1)}), bf16[8,8,256]{2,1,0:T(8,128)(2,1)S(1)}, u32[]{:S(2)}, u32[]{:S(2)}) async-start(bf16[8,8,256]{2,1,0:T(8,128)(2,1)} %bitcast.58), calls=%async_computation | async-start | bytes 65536 | tf_op jit(solution)/shard_map/all_to_all | solution.py:238
  11.4 16.6 %copy-start = (bf16[4,6,2,16,256]{4,3,2,1,0:T(8,128)(2,1)S(1)}, bf16[4,6,2,16,256]{4,3,2,1,0:T(8,128)(2,1)}, u32[]{:S(2)}) copy-start(bf16[4,6,2,16,256]{4,3,2,1,0:T(8,128)(2,1)} %param.6) | copy-start | bytes 1179652
  11.4 16.6 %copy-start.1 = (bf16[4,6,2,16,256]{4,3,2,1,0:T(8,128)(2,1)S(1)}, bf16[4,6,2,16,256]{4,3,2,1,0:T(8,128)(2,1)}, u32[]{:S(2)}) copy-start(bf16[4,6,2,16,256]{4,3,2,1,0:T(8,128)(2,1)} %param.5) | copy-start | bytes 1179652
  11.4 47.0 %all-to-all-start.1 = ((bf16[64,8,1152]{2,1,0:T(8,128)(2,1)}), bf16[64,8,1152]{2,1,0:T(8,128)(2,1)S(1)}, u32[]{:S(2)}, u32[]{:S(2)}) async-start(bf16[64,8,1152]{2,1,0:T(8,128)(2,1)} %shard_map.69), calls=%async_computation.1 | async-start | bytes 2359296 | tf_op jit(solution)/shard_map/all_to_all | solution.py:240
  28.1 4.6 %copy-start.7 = (s32[4]{0:T(128)S(1)}, s32[4]{0:T(128)}, u32[]{:S(2)}) copy-start(s32[4]{0:T(128)} %constant.403.clone) | copy-start | bytes 52
  28.2 32.3 %collective-permute-start = (bf16[2,4,3,2,16,256]{5,4,3,2,1,0:T(8,128)(2,1)S(1)}, bf16[2,4,3,2,16,256]{5,4,3,2,1,0:T(8,128)(2,1)S(1)}, u32[]{:S(2)}, u32[]{:S(2)}) collective-permute-start(bf16[2,4,3,2,16,256]{5,4,3,2,1,0:T(8,128)(2,1)S(1)} %pad_maximum_fusion), channel_id=1, source_target_pairs={{0,1},{1,0},{2,3},{3,2},{4,5},{5,4},{6,7},{7,6},{8,9},{9,8},{10,11... | collective-permute-start | bytes 1179656 | tf_op jit(solution)/shard_map/ppermute | solution.py:249
  58.4 5.4 %copy-start.4 = (bf16[1,3,2,16,256]{4,3,2,1,0:T(8,128)(2,1)S(1)}, bf16[1,3,2,16,256]{4,3,2,1,0:T(8,128)(2,1)}, u32[]{:S(2)}) copy-start(bf16[1,3,2,16,256]{4,3,2,1,0:T(8,128)(2,1)} %get-tuple-element.28) | copy-start | bytes 147460
  58.4 5.4 %copy-start.5 = (bf16[1,3,2,16,256]{4,3,2,1,0:T(8,128)(2,1)S(1)}, bf16[1,3,2,16,256]{4,3,2,1,0:T(8,128)(2,1)}, u32[]{:S(2)}) copy-start(bf16[1,3,2,16,256]{4,3,2,1,0:T(8,128)(2,1)} %get-tuple-element.47) | copy-start | bytes 147460
  58.4 8.1 %copy-start.2 = (bf16[1,3,2,16,256]{4,3,2,1,0:T(8,128)(2,1)S(1)}, bf16[1,3,2,16,256]{4,3,2,1,0:T(8,128)(2,1)}, u32[]{:S(2)}) copy-start(bf16[1,3,2,16,256]{4,3,2,1,0:T(8,128)(2,1)} %get-tuple-element.27) | copy-start | bytes 147460
  58.4 8.2 %copy-start.3 = (bf16[1,3,2,16,256]{4,3,2,1,0:T(8,128)(2,1)S(1)}, bf16[1,3,2,16,256]{4,3,2,1,0:T(8,128)(2,1)}, u32[]{:S(2)}) copy-start(bf16[1,3,2,16,256]{4,3,2,1,0:T(8,128)(2,1)} %get-tuple-element.48) | copy-start | bytes 147460
  58.4 20.6 %collective-permute-start.4 = (bf16[512,1152]{1,0:T(8,128)(2,1)S(1)}, bf16[512,1152]{1,0:T(8,128)(2,1)S(1)}, u32[]{:S(2)}, u32[]{:S(2)}) collective-permute-start(bf16[512,1152]{1,0:T(8,128)(2,1)S(1)} %bitcast.49), channel_id=1, source_target_pairs={{0,1},{1,0},{2,3},{3,2},{4,5},{5,4},{6,7},{7,6},{8,9},{9,8},{10,11... | collective-permute-start | bytes 3538952 | tf_op jit(solution)/shard_map/ppermute | solution.py:188
  60.5 10.7 %copy-start.6 = (s32[4]{0:T(128)S(1)}, s32[4]{0:T(128)}, u32[]{:S(2)}) copy-start(s32[4]{0:T(128)} %get-tuple-element.18) | copy-start | bytes 52
  60.7 11.9 %collective-permute-start.1 = (bf16[2,2,3,2,16,256]{5,4,3,2,1,0:T(8,128)(2,1)S(1)}, bf16[2,2,3,2,16,256]{5,4,3,2,1,0:T(8,128)(2,1)S(1)}, u32[]{:S(2)}, u32[]{:S(2)}) collective-permute-start(bf16[2,2,3,2,16,256]{5,4,3,2,1,0:T(8,128)(2,1)S(1)} %bitcast.56), channel_id=1, source_target_pairs={{0,2},{2,0},{256,258},{258,256},{1,3},{3,1},{257,259},{259,257},{4... | collective-permute-start | bytes 589832 | tf_op jit(solution)/shard_map/ppermute | solution.py:258
  63.9 10.2 %collective-permute-start.2 = (bf16[2,2,3,2,16,256]{5,4,3,2,1,0:T(8,128)(2,1)S(1)}, bf16[2,2,3,2,16,256]{5,4,3,2,1,0:T(8,128)(2,1)S(1)}, u32[]{:S(2)}, u32[]{:S(2)}) collective-permute-start(bf16[2,2,3,2,16,256]{5,4,3,2,1,0:T(8,128)(2,1)S(1)} %bitcast.57), channel_id=1, source_target_pairs={{0,256},{2,258},{256,0},{258,2},{1,257},{3,259},{257,1},{259,3},{4... | collective-permute-start | bytes 589832 | tf_op jit(solution)/shard_map/ppermute | solution.py:258
  67.3 10.0 %collective-permute-start.3 = (bf16[2,2,3,2,16,256]{5,4,3,2,1,0:T(8,128)(2,1)}, bf16[2,2,3,2,16,256]{5,4,3,2,1,0:T(8,128)(2,1)S(1)}, u32[]{:S(2)}, u32[]{:S(2)}) collective-permute-start(bf16[2,2,3,2,16,256]{5,4,3,2,1,0:T(8,128)(2,1)} %bitcast.27), channel_id=1, source_target_pairs={{0,258},{2,256},{256,2},{258,0},{1,259},{3,257},{257,3},{259,1},{4... | collective-permute-start | bytes 589832 | tf_op jit(solution)/shard_map/ppermute | solution.py:258
  92.7 20.0 %all-to-all-start.3 = ((bf16[32,24,128]{2,1,0:T(8,128)(2,1)}), bf16[32,24,128]{2,1,0:T(8,128)(2,1)S(1)}, u32[]{:S(2)}, u32[]{:S(2)}) async-start(bf16[32,24,128]{2,1,0:T(8,128)(2,1)} %shard_map.73), calls=%async_computation.3 | async-start | bytes 393216 | tf_op jit(solution)/shard_map/all_to_all | solution.py:287

commit v13 on v11

--- a/solution.py
+++ b/solution.py
@@ -27,17 +27,21 @@
     return jnp.dot(left, right, preferred_element_type=F32, precision=precision)
 
 
-def fan(at_ref, w_ref, out_ref):
+def fan(at_ref, w_ref, out_ref, piece_ref, sem):
     lane = 0
     for xl in range(2):
         for d in range(SENT - xl):
             block = lax.rem(at_ref[0] + (4 * xl + d), NB)
             lanes = pl.ds(pl.multiple_of((block % 2) * BLK, BLK), BLK)
-            out_ref[0, :, lane : lane + BLK] = w_ref[4 * xl + block // 2, :, lanes]
+            piece_ref[:, lane : lane + BLK] = w_ref[4 * xl + block // 2, :, lanes]
             lane += BLK
-    piece = out_ref[0]
-    for slot in range(1, 64):
-        out_ref[slot, :, :] = piece
+    copies = [
+        pltpu.make_async_copy(piece_ref, out_ref.at[slot], sem.at[slot]) for slot in range(64)
+    ]
+    for copy in copies:
+        copy.start()
+    for copy in copies:
+        copy.wait()
 
 
 def fanned(at, w):
@@ -46,7 +50,11 @@
         fan,
         out_shape=jax.ShapeDtypeStruct((64, 8, (2 * SENT - 1) * BLK), BF),
         in_specs=[pl.BlockSpec(memory_space=pltpu.SMEM), vm],
-        out_specs=vm,
+        out_specs=pl.BlockSpec(memory_space=pl.ANY),
+        scratch_shapes=[
+            pltpu.VMEM((8, (2 * SENT - 1) * BLK), BF),
+            pltpu.SemaphoreType.DMA((64,)),
+        ],
         compiler_params=pltpu.CompilerParams(vmem_limit_bytes=16 << 20),
     )(at, w)
 
@@ -257,7 +265,6 @@
     other = xl ^ ((here + row_step) // 32 % 2)
     begin = (6 * yl - col_step + 12) % 12
     source = (here - row_step) % 32
-    source = source % 4 * 8 + source // 4
     col = (begin[:, None] + jnp.arange(KQ)) % 12
     base = jnp.array([0, 2, 8, 10])[:, None]
     slot = base + col // 6 * 4 + col % 6 // 3
@@ -279,7 +286,7 @@
         scratch_shapes=[pltpu.VMEM((Q * KQ, 128), F32)],
         compiler_params=kept,
     )(at, got)
-    came = lax.all_to_all(pay, ("yh", "z"), 0, 0)
+    came = lax.all_to_all(pay, ("z", "yh"), 0, 0)
     forward = pl.pallas_call(
         pick_forward, out_shape=out, in_specs=[sm, vm], out_specs=vm, compiler_params=kept
     )(at, got)

time: 115 us -> 115 us (level)
  the two profiles are of different devices: /device:TPU:8 before, /device:TPU:16 now
where the time goes in v13:
time: 115 us
  waiting for transfers between devices  46.4 us (40%)
  starting transfers between devices  42 us (37%)
  blocking collectives  10.6 us (9%)
  Pallas kernels  8.91 us (8%)
  other arithmetic  3.75 us (3%)
  local copies, waits for them, and re-layouts  1.99 us (2%)
    all_to_all x1, waiting for transfers between devices, local(): w = lax.all_to_all(w, ('yh', 'z', 'yl'), 0, 0)  24.9 us
    all_to_all x1, starting transfers between devices, local(): w = lax.all_to_all(w, ('yh', 'z', 'yl'), 0, 0)  16.6 us
    all_to_all x1, waiting for transfers between devices, local(): came = lax.all_to_all(pay, ('z', 'yh'), 0, 0)  11.5 us
    all_to_all x1, blocking collectives, local(): got = lax.all_to_all(slots, ('xl', 'yl', 'xh', 'c'), 0, 0)  10.6 us
    ppermute x3, starting transfers between devices, local(): piece = lax.ppermute(piece, ('xl', 'xh'), [(i, i ^ s) for i in range(4)])  9.81 us
    all_to_all x1, starting transfers between devices, local(): came = lax.all_to_all(pay, ('z', 'yh'), 0, 0)  7.31 us
    all_to_all x1, waiting for transfers between devices, local(): w = lax.all_to_all(screened.reshape(8, 8, 256), ('xl', 'xh', 'c'), 0, 0)  5.36 us
    ppermute x3, waiting for transfers between devices, local(): piece = lax.ppermute(piece, ('xl', 'xh'), [(i, i ^ s) for i in range(4)])  4.66 us
  transfers between devices with their start and end apart: 8, of which 5 were waited for; matrix products, arithmetic and copies ran while one was open for 5% of the time, Pallas kernels for 3%

profile of v13, /device:TPU:16, one launch (start us, length us, event | category | flops | bytes accessed | tf_op | source)
XLA Modules:
  0.0 114.5 jit_solution(9056688906484396354)
XLA Ops:
  0.6 4.3 %all-to-all-start = ((bf16[8,8,256]{2,1,0:T(8,128)(2,1)}), bf16[8,8,256]{2,1,0:T(8,128)(2,1)S(1)}, u32[]{:S(2)}, u32[]{:S(2)}) async-start(bf16[8,8,256]{2,1,0:T(8,128)(2,1)} %bitcast.58), calls=%async_computation | async-start | bytes 65536 | tf_op jit(solution)/shard_map/all_to_all | solution.py:240
  4.9 5.4 %all-to-all-done.w_ref = bf16[8,8,256]{2,1,0:T(8,128)(2,1)S(1)} async-done(((bf16[8,8,256]{2,1,0:T(8,128)(2,1)}), bf16[8,8,256]{2,1,0:T(8,128)(2,1)S(1)}, u32[]{:S(2)}, u32[]{:S(2)}) %all-to-all-start) | async-done | bytes 32800 | tf_op jit(solution)/shard_map/all_to_all | solution.py:240
  10.3 1.6 %shard_map.69 = bf16[64,8,1152]{2,1,0:T(8,128)(2,1)} custom-call(s32[1]{0:T(128)} %bitcast.28.at_ref, bf16[8,8,256]{2,1,0:T(8,128)(2,1)S(1)} %all-to-all-done.w_ref), custom_call_target="tpu_custom_call" | custom-call | tf_op jit(solution)/shard_map/pallas_call | solution.py:49
  11.9 16.6 %all-to-all-start.1 = ((bf16[64,8,1152]{2,1,0:T(8,128)(2,1)}), bf16[64,8,1152]{2,1,0:T(8,128)(2,1)S(1)}, u32[]{:S(2)}, u32[]{:S(2)}) async-start(bf16[64,8,1152]{2,1,0:T(8,128)(2,1)} %shard_map.69), calls=%async_computation.1 | async-start | bytes 2359296 | tf_op jit(solution)/shard_map/all_to_all | solution.py:242
  28.7 1.9 %collective-permute-start = (bf16[2,4,3,2,16,256]{5,4,3,2,1,0:T(8,128)(2,1)S(1)}, bf16[2,4,3,2,16,256]{5,4,3,2,1,0:T(8,128)(2,1)S(1)}, u32[]{:S(2)}, u32[]{:S(2)}) collective-permute-start(bf16[2,4,3,2,16,256]{5,4,3,2,1,0:T(8,128)(2,1)S(1)} %pad_maximum_fusion), channel_id=1, source_target_pairs={{0,1},{1,0},{2,3},{3,2},{4,5},{5,4},{6,7},{7,6},{8,9},{9,8},{10,11... | collective-permute-start | bytes 1179656 | tf_op jit(solution)/shard_map/ppermute | solution.py:251
  30.6 0.8 fusion.17
  31.4 1.4 %fusion.16 = (s32[4]{0:T(128)}, s32[4]{0:T(128)S(1)}, s32[4]{0:T(128)S(1)}) fusion(s32[4,768]{1,0:T(4,128)} %param.8, pred[4,1]{1,0:T(4,128)(4,1)S(1)} %get-tuple-element.12, s32[]{:T(128)S(6)} %add.210, s32[]{:T(128)} %axis_index.63, s32[]{:T(128)S(6)} %mul.19), kind=kLoop, calls=%fused_computation.63 | loop fusion | flops 184 | bytes 80 | tf_op jit(solution)/shard_map/jit(floor_divide)/div | solution.py:263
  34.0 24.9 %all-to-all-done.1 = bf16[64,8,1152]{2,1,0:T(8,128)(2,1)S(1)} async-done(((bf16[64,8,1152]{2,1,0:T(8,128)(2,1)}), bf16[64,8,1152]{2,1,0:T(8,128)(2,1)S(1)}, u32[]{:S(2)}, u32[]{:S(2)}) %all-to-all-start.1) | async-done | bytes 1179680 | tf_op jit(solution)/shard_map/all_to_all | solution.py:242
  58.9 2.1 %collective-permute-start.4 = (bf16[512,1152]{1,0:T(8,128)(2,1)S(1)}, bf16[512,1152]{1,0:T(8,128)(2,1)S(1)}, u32[]{:S(2)}, u32[]{:S(2)}) collective-permute-start(bf16[512,1152]{1,0:T(8,128)(2,1)S(1)} %bitcast.49), channel_id=1, source_target_pairs={{0,1},{1,0},{2,3},{3,2},{4,5},{5,4},{6,7},{7,6},{8,9},{9,8},{10,11... | collective-permute-start | bytes 3538952 | tf_op jit(solution)/shard_map/ppermute | solution.py:191
  61.2 3.2 %collective-permute-start.1 = (bf16[2,2,3,2,16,256]{5,4,3,2,1,0:T(8,128)(2,1)S(1)}, bf16[2,2,3,2,16,256]{5,4,3,2,1,0:T(8,128)(2,1)S(1)}, u32[]{:S(2)}, u32[]{:S(2)}) collective-permute-start(bf16[2,2,3,2,16,256]{5,4,3,2,1,0:T(8,128)(2,1)S(1)} %bitcast.56), channel_id=1, source_target_pairs={{0,2},{2,0},{256,258},{258,256},{1,3},{3,1},{257,259},{259,257},{4... | collective-permute-start | bytes 589832 | tf_op jit(solution)/shard_map/ppermute | solution.py:260
  64.4 2.7 %collective-permute-start.2 = (bf16[2,2,3,2,16,256]{5,4,3,2,1,0:T(8,128)(2,1)S(1)}, bf16[2,2,3,2,16,256]{5,4,3,2,1,0:T(8,128)(2,1)S(1)}, u32[]{:S(2)}, u32[]{:S(2)}) collective-permute-start(bf16[2,2,3,2,16,256]{5,4,3,2,1,0:T(8,128)(2,1)S(1)} %bitcast.57), channel_id=1, source_target_pairs={{0,256},{2,258},{256,0},{258,2},{1,257},{3,259},{257,1},{259,3},{4... | collective-permute-start | bytes 589832 | tf_op jit(solution)/shard_map/ppermute | solution.py:260
  67.8 4.0 %collective-permute-start.3 = (bf16[2,2,3,2,16,256]{5,4,3,2,1,0:T(8,128)(2,1)}, bf16[2,2,3,2,16,256]{5,4,3,2,1,0:T(8,128)(2,1)S(1)}, u32[]{:S(2)}, u32[]{:S(2)}) collective-permute-start(bf16[2,2,3,2,16,256]{5,4,3,2,1,0:T(8,128)(2,1)} %bitcast.27), channel_id=1, source_target_pairs={{0,258},{2,256},{256,2},{258,0},{1,259},{3,257},{257,3},{259,1},{4... | collective-permute-start | bytes 589832 | tf_op jit(solution)/shard_map/ppermute | solution.py:260
  72.4 0.8 concatenate.3.at_ref
  73.2 1.4 %collective-permute-done.2.refs_2_ = bf16[2,2,3,2,16,256]{5,4,3,2,1,0:T(8,128)(2,1)S(1)} collective-permute-done((bf16[2,2,3,2,16,256]{5,4,3,2,1,0:T(8,128)(2,1)S(1)}, bf16[2,2,3,2,16,256]{5,4,3,2,1,0:T(8,128)(2,1)S(1)}, u32[]{:S(2)}, u32[]{:S(2)}) %collective-permute-start.2) | collective-permute-done | bytes 196640 | tf_op jit(solution)/shard_map/ppermute | solution.py:260
  74.6 3.3 %collective-permute-done.3.refs_3_ = bf16[2,2,3,2,16,256]{5,4,3,2,1,0:T(8,128)(2,1)S(1)} collective-permute-done((bf16[2,2,3,2,16,256]{5,4,3,2,1,0:T(8,128)(2,1)}, bf16[2,2,3,2,16,256]{5,4,3,2,1,0:T(8,128)(2,1)S(1)}, u32[]{:S(2)}, u32[]{:S(2)}) %collective-permute-start.3) | collective-permute-done | bytes 196640 | tf_op jit(solution)/shard_map/ppermute | solution.py:260
  77.9 0.8 shard_map.68
  78.6 0.9 shard_map.70.p_ref
  79.5 1.9 %shard_map.71 = f32[16,6,128]{2,1,0:T(8,128)S(1)} custom-call(bf16[192,1024]{1,0:T(8,128)(2,1)S(1)} %get-tuple-element.5.left_ref, bf16[192,1024]{1,0:T(8,128)(2,1)S(1)} %get-tuple-element.6.flip_ref, bf16[192,1024]{1,0:T(8,128)(2,1)S(1)} %get-tuple-element.7.val_ref, f32[192,1024]{1,0:T(8,128)S(1)} %shard_map.70.p_ref, ...), custom_call_target="tpu_custom_call" | custom-call | flops 800000000 | bytes 2000000 | tf_op jit(solution)/shard_map/pallas_call | solution.py:200
  81.4 10.6 %all_to_all.20.got_ref = f32[16,6,128]{2,1,0:T(8,128)S(1)} all-to-all(f32[16,6,128]{2,1,0:T(8,128)S(1)} %shard_map.71), channel_id=1, replica_groups=mesh['xl'=2,'z'=8,'yh'=4,'yl'=2,'xh'=2,'c'=2] {'xl','yl','xh','c'}, dimensions={0} | all-to-all | bytes 98304 | tf_op jit(solution)/shard_map/all_to_all | solution.py:276
  92.0 1.3 %shard_map.73 = bf16[32,24,128]{2,1,0:T(8,128)(2,1)} custom-call(s32[56]{0:T(128)S(1)} %concatenate.3.at_ref, f32[16,6,128]{2,1,0:T(8,128)S(1)} %all_to_all.20.got_ref), custom_call_target="tpu_custom_call" | custom-call | tf_op jit(solution)/shard_map/pallas_call | solution.py:281
  93.2 7.3 %all-to-all-start.3 = ((bf16[32,24,128]{2,1,0:T(8,128)(2,1)}), bf16[32,24,128]{2,1,0:T(8,128)(2,1)S(1)}, u32[]{:S(2)}, u32[]{:S(2)}) async-start(bf16[32,24,128]{2,1,0:T(8,128)(2,1)} %shard_map.73), calls=%async_computation.3 | async-start | bytes 393216 | tf_op jit(solution)/shard_map/all_to_all | solution.py:289
  100.6 1.2 %shard_map.72 = f32[4,6,2,64]{3,2,1,0:T(2,128)} custom-call(s32[56]{0:T(128)S(1)} %concatenate.3.at_ref, f32[16,6,128]{2,1,0:T(8,128)S(1)} %all_to_all.20.got_ref), custom_call_target="tpu_custom_call" | custom-call | tf_op jit(solution)/shard_map/pallas_call | solution.py:290
  101.8 11.5 %all-to-all-done.3.came_ref = bf16[32,24,128]{2,1,0:T(8,128)(2,1)S(1)} async-done(((bf16[32,24,128]{2,1,0:T(8,128)(2,1)}), bf16[32,24,128]{2,1,0:T(8,128)(2,1)S(1)}, u32[]{:S(2)}, u32[]{:S(2)}) %all-to-all-start.3) | async-done | bytes 196640 | tf_op jit(solution)/shard_map/all_to_all | solution.py:289
  113.3 1.2 %shard_map.74 = f32[4,6,2,64]{3,2,1,0:T(2,128)} custom-call(s32[56]{0:T(128)S(1)} %concatenate.3.at_ref, bf16[32,24,128]{2,1,0:T(8,128)(2,1)S(1)} %all-to-all-done.3.came_ref), custom_call_target="tpu_custom_call" | custom-call | tf_op jit(solution)/shard_map/pallas_call | solution.py:293
  (37 shorter events, 2.8 us)
Async XLA Ops:
  0.6 9.7 %all-to-all-start = ((bf16[8,8,256]{2,1,0:T(8,128)(2,1)}), bf16[8,8,256]{2,1,0:T(8,128)(2,1)S(1)}, u32[]{:S(2)}, u32[]{:S(2)}) async-start(bf16[8,8,256]{2,1,0:T(8,128)(2,1)} %bitcast.58), calls=%async_computation | async-start | bytes 65536 | tf_op jit(solution)/shard_map/all_to_all | solution.py:240
  11.9 16.7 %copy-start = (bf16[4,6,2,16,256]{4,3,2,1,0:T(8,128)(2,1)S(1)}, bf16[4,6,2,16,256]{4,3,2,1,0:T(8,128)(2,1)}, u32[]{:S(2)}) copy-start(bf16[4,6,2,16,256]{4,3,2,1,0:T(8,128)(2,1)} %param.6) | copy-start | bytes 1179652
  11.9 16.7 %copy-start.1 = (bf16[4,6,2,16,256]{4,3,2,1,0:T(8,128)(2,1)S(1)}, bf16[4,6,2,16,256]{4,3,2,1,0:T(8,128)(2,1)}, u32[]{:S(2)}) copy-start(bf16[4,6,2,16,256]{4,3,2,1,0:T(8,128)(2,1)} %param.5) | copy-start | bytes 1179652
  11.9 47.0 %all-to-all-start.1 = ((bf16[64,8,1152]{2,1,0:T(8,128)(2,1)}), bf16[64,8,1152]{2,1,0:T(8,128)(2,1)S(1)}, u32[]{:S(2)}, u32[]{:S(2)}) async-start(bf16[64,8,1152]{2,1,0:T(8,128)(2,1)} %shard_map.69), calls=%async_computation.1 | async-start | bytes 2359296 | tf_op jit(solution)/shard_map/all_to_all | solution.py:242
  28.6 4.6 %copy-start.7 = (s32[4]{0:T(128)S(1)}, s32[4]{0:T(128)}, u32[]{:S(2)}) copy-start(s32[4]{0:T(128)} %constant.403.clone) | copy-start | bytes 52
  28.7 32.3 %collective-permute-start = (bf16[2,4,3,2,16,256]{5,4,3,2,1,0:T(8,128)(2,1)S(1)}, bf16[2,4,3,2,16,256]{5,4,3,2,1,0:T(8,128)(2,1)S(1)}, u32[]{:S(2)}, u32[]{:S(2)}) collective-permute-start(bf16[2,4,3,2,16,256]{5,4,3,2,1,0:T(8,128)(2,1)S(1)} %pad_maximum_fusion), channel_id=1, source_target_pairs={{0,1},{1,0},{2,3},{3,2},{4,5},{5,4},{6,7},{7,6},{8,9},{9,8},{10,11... | collective-permute-start | bytes 1179656 | tf_op jit(solution)/shard_map/ppermute | solution.py:251
  58.9 5.4 %copy-start.4 = (bf16[1,3,2,16,256]{4,3,2,1,0:T(8,128)(2,1)S(1)}, bf16[1,3,2,16,256]{4,3,2,1,0:T(8,128)(2,1)}, u32[]{:S(2)}) copy-start(bf16[1,3,2,16,256]{4,3,2,1,0:T(8,128)(2,1)} %get-tuple-element.18) | copy-start | bytes 147460
  58.9 5.4 %copy-start.5 = (bf16[1,3,2,16,256]{4,3,2,1,0:T(8,128)(2,1)S(1)}, bf16[1,3,2,16,256]{4,3,2,1,0:T(8,128)(2,1)}, u32[]{:S(2)}) copy-start(bf16[1,3,2,16,256]{4,3,2,1,0:T(8,128)(2,1)} %get-tuple-element.37) | copy-start | bytes 147460
  58.9 8.1 %copy-start.2 = (bf16[1,3,2,16,256]{4,3,2,1,0:T(8,128)(2,1)S(1)}, bf16[1,3,2,16,256]{4,3,2,1,0:T(8,128)(2,1)}, u32[]{:S(2)}) copy-start(bf16[1,3,2,16,256]{4,3,2,1,0:T(8,128)(2,1)} %get-tuple-element.17) | copy-start | bytes 147460
  58.9 8.2 %copy-start.3 = (bf16[1,3,2,16,256]{4,3,2,1,0:T(8,128)(2,1)S(1)}, bf16[1,3,2,16,256]{4,3,2,1,0:T(8,128)(2,1)}, u32[]{:S(2)}) copy-start(bf16[1,3,2,16,256]{4,3,2,1,0:T(8,128)(2,1)} %get-tuple-element.38) | copy-start | bytes 147460
  58.9 20.6 %collective-permute-start.4 = (bf16[512,1152]{1,0:T(8,128)(2,1)S(1)}, bf16[512,1152]{1,0:T(8,128)(2,1)S(1)}, u32[]{:S(2)}, u32[]{:S(2)}) collective-permute-start(bf16[512,1152]{1,0:T(8,128)(2,1)S(1)} %bitcast.49), channel_id=1, source_target_pairs={{0,1},{1,0},{2,3},{3,2},{4,5},{5,4},{6,7},{7,6},{8,9},{9,8},{10,11... | collective-permute-start | bytes 3538952 | tf_op jit(solution)/shard_map/ppermute | solution.py:191
  61.1 10.7 %copy-start.6 = (s32[4]{0:T(128)S(1)}, s32[4]{0:T(128)}, u32[]{:S(2)}) copy-start(s32[4]{0:T(128)} %get-tuple-element.8) | copy-start | bytes 52
  61.2 12.0 %collective-permute-start.1 = (bf16[2,2,3,2,16,256]{5,4,3,2,1,0:T(8,128)(2,1)S(1)}, bf16[2,2,3,2,16,256]{5,4,3,2,1,0:T(8,128)(2,1)S(1)}, u32[]{:S(2)}, u32[]{:S(2)}) collective-permute-start(bf16[2,2,3,2,16,256]{5,4,3,2,1,0:T(8,128)(2,1)S(1)} %bitcast.56), channel_id=1, source_target_pairs={{0,2},{2,0},{256,258},{258,256},{1,3},{3,1},{257,259},{259,257},{4... | collective-permute-start | bytes 589832 | tf_op jit(solution)/shard_map/ppermute | solution.py:260
  64.4 10.2 %collective-permute-start.2 = (bf16[2,2,3,2,16,256]{5,4,3,2,1,0:T(8,128)(2,1)S(1)}, bf16[2,2,3,2,16,256]{5,4,3,2,1,0:T(8,128)(2,1)S(1)}, u32[]{:S(2)}, u32[]{:S(2)}) collective-permute-start(bf16[2,2,3,2,16,256]{5,4,3,2,1,0:T(8,128)(2,1)S(1)} %bitcast.57), channel_id=1, source_target_pairs={{0,256},{2,258},{256,0},{258,2},{1,257},{3,259},{257,1},{259,3},{4... | collective-permute-start | bytes 589832 | tf_op jit(solution)/shard_map/ppermute | solution.py:260
  67.8 10.0 %collective-permute-start.3 = (bf16[2,2,3,2,16,256]{5,4,3,2,1,0:T(8,128)(2,1)}, bf16[2,2,3,2,16,256]{5,4,3,2,1,0:T(8,128)(2,1)S(1)}, u32[]{:S(2)}, u32[]{:S(2)}) collective-permute-start(bf16[2,2,3,2,16,256]{5,4,3,2,1,0:T(8,128)(2,1)} %bitcast.27), channel_id=1, source_target_pairs={{0,258},{2,256},{256,2},{258,0},{1,259},{3,257},{257,3},{259,1},{4... | collective-permute-start | bytes 589832 | tf_op jit(solution)/shard_map/ppermute | solution.py:260
  93.2 20.0 %all-to-all-start.3 = ((bf16[32,24,128]{2,1,0:T(8,128)(2,1)}), bf16[32,24,128]{2,1,0:T(8,128)(2,1)S(1)}, u32[]{:S(2)}, u32[]{:S(2)}) async-start(bf16[32,24,128]{2,1,0:T(8,128)(2,1)} %shard_map.73), calls=%async_computation.3 | async-start | bytes 393216 | tf_op jit(solution)/shard_map/all_to_all | solution.py:289
